TPU v7x, 32 devices: a whole 2x2x4 slice. The times are simulated.
32 devices in a mesh: dp: 4 (over y, x), tensor: 8 (over z, core).
Axes of the slice: x: 2, y: 2, z: 4, core: 2. Of those that a mesh axis runs over, the one named last changes fastest.
Arguments:
- tokens: bfloat16 [8, 2048, 1024], P('dp', 'tensor'), may hold values from -6 to 6
- cotangent: bfloat16 [8, 2048, 1024], P('dp', 'tensor'), may hold values from -6 to 6
- lengths: int32 [8, 12], P('dp'), may hold values from 1 to 256, 1536 in all within a row
- parents: int32 [8, 13], P('dp'), may hold values from 0 to 4, as said below
- first_gain: float32 [1024], replicated, may hold values from 0.25 to 1.75
- first_shift: float32 [1024], replicated, may hold values from -1 to 1
- in_weight: bfloat16 [1024, 3, 1024], P(None, None, 'tensor'), may hold values from -0.1875 to 0.1875
- out_weight: bfloat16 [1024, 1024], P('tensor'), may hold values from -0.1875 to 0.1875
- second_gain: float32 [1024], replicated, may hold values from 0.25 to 1.75
- second_shift: float32 [1024], replicated, may hold values from -1 to 1
- third_gain: float32 [1024], replicated, may hold values from 0.25 to 1.75
- third_shift: float32 [1024], replicated, may hold values from -1 to 1
- up_weight: bfloat16 [1024, 4096], P(None, 'tensor'), may hold values from -0.1875 to 0.1875
- down_weight: bfloat16 [4096, 1024], P('tensor'), may hold values from -0.09375 to 0.09375
- fourth_gain: float32 [1024], replicated, may hold values from 0.25 to 1.75
- fourth_shift: float32 [1024], replicated, may hold values from -1 to 1
Outputs:
- output: bfloat16 [8, 2048, 1024], P('dp', 'tensor')
- tokens_gradient: bfloat16 [8, 2048, 1024], P('dp', 'tensor')
- first_gain_gradient: float32 [1024], replicated
- first_shift_gradient: float32 [1024], replicated
- in_weight_gradient: float32 [1024, 3, 1024], P(None, None, 'tensor')
- out_weight_gradient: float32 [1024, 1024], P('tensor')
- second_gain_gradient: float32 [1024], replicated
- second_shift_gradient: float32 [1024], replicated
- third_gain_gradient: float32 [1024], replicated
- third_shift_gradient: float32 [1024], replicated
- up_weight_gradient: float32 [1024, 4096], P(None, 'tensor')
- down_weight_gradient: float32 [4096, 1024], P('tensor')
- fourth_gain_gradient: float32 [1024], replicated
- fourth_shift_gradient: float32 [1024], replicated
Inputs may be any that keep to these rules, and one draw needn't show every extreme that they name: lengths of a tree's branches and leaves, summing to 1536. `parents`: segment 0 is the trunk (its own entry 0); segments 1 to 4 are branches with parent 0; segments 5 to 12 are leaves, two on each branch.
All inputs are finite; a program needn't handle non-finite values.
Results may differ from a plain program's by a relative error of at most 0.019.
Values may be sent and summed in bfloat16 or wider, within the bound.
A program may use at most 192 MiB of HBM per device.

v0:
```python
import jax
import jax.numpy as jnp
from jax import lax
from jax.sharding import PartitionSpec as P

D = 1024
HEAD_DIM = 64
TRUNK = 512
SEGMENTS = 13
TREE = 2048
QBLOCK = 512


rope_base = 10000.0
norm_eps = 1e-05
masked_score = -1e30


def layer_norm(values, gain, shift):
    average = jnp.mean(values, axis=-1, keepdims=True)
    centered = values - average
    spread = jnp.mean(centered * centered, axis=-1, keepdims=True)
    return centered * lax.rsqrt(spread + norm_eps) * gain + shift


def gelu_tanh(values):
    return (
        0.5
        * values
        * (1.0 + jnp.tanh(0.7978845608028654 * (values + 0.044715 * values * values * values)))
    )


def rotate(block, position):
    half = block.shape[-1] // 2
    inverse = rope_base ** (-jnp.arange(half, dtype=jnp.float32) * 2.0 / block.shape[-1])
    angle = position.astype(jnp.float32)[:, None] * inverse[None, :]
    cosine = jnp.cos(angle)[:, None, :]
    sine = jnp.sin(angle)[:, None, :]
    former = block[..., :half]
    latter = block[..., half:]
    return jnp.concatenate(
        [former * cosine - latter * sine, former * sine + latter * cosine], axis=-1
    )


def tree_layout(tree_lengths, tree_parents):
    seg_sizes = jnp.concatenate([jnp.full((1,), TRUNK, jnp.int32), tree_lengths])
    ends = jnp.cumsum(seg_sizes)
    starts = ends - seg_sizes
    places = jnp.arange(TREE, dtype=jnp.int32)
    labels = jnp.arange(SEGMENTS, dtype=jnp.int32)
    segment = jnp.sum((places[:, None] >= ends[None, :]).astype(jnp.int32), axis=1)
    own_hot = (segment[:, None] == labels[None, :]).astype(jnp.int32)
    parent = jnp.sum(own_hot * tree_parents[None, :], axis=1)
    parent_hot = (parent[:, None] == labels[None, :]).astype(jnp.int32)
    grandparent = jnp.sum(parent_hot * tree_parents[None, :], axis=1)
    parent_size = jnp.sum(parent_hot * seg_sizes[None, :], axis=1)
    depth_start = jnp.where(segment > 0, TRUNK, 0).astype(jnp.int32) + jnp.where(
        parent > 0, parent_size, 0
    )
    position = places - jnp.sum(own_hot * starts[None, :], axis=1) + depth_start
    return (segment, parent, grandparent, position)


def visible(first, segment, parent, grandparent):
    rows = first + jnp.arange(QBLOCK, dtype=jnp.int32)
    row_segment = lax.dynamic_slice_in_dim(segment, first, QBLOCK, 0)
    row_parent = lax.dynamic_slice_in_dim(parent, first, QBLOCK, 0)
    row_grand = lax.dynamic_slice_in_dim(grandparent, first, QBLOCK, 0)
    columns = jnp.arange(TREE, dtype=jnp.int32)
    same_path = (
        (segment[None, :] == row_segment[:, None])
        | (segment[None, :] == row_parent[:, None])
        | (segment[None, :] == row_grand[:, None])
    )
    return same_path & (columns[None, :] <= rows[:, None])


def attend(query, keys, values, layout):
    segment, parent, grandparent = layout
    scale = HEAD_DIM ** (-0.5)

    def one_block(index):
        first = index * QBLOCK
        rows = lax.dynamic_slice_in_dim(query, first, QBLOCK, 0)
        allowed = visible(first, segment, parent, grandparent)
        raw = jnp.einsum("qhd,khd->hqk", rows, keys, preferred_element_type=jnp.float32)
        scores = jnp.where(allowed[None], raw * scale, masked_score)
        top = jnp.max(scores, axis=-1, keepdims=True)
        exponent = jnp.exp(scores - top)
        total = jnp.sum(exponent, axis=-1, keepdims=True)
        weights = (exponent / total).astype(jnp.bfloat16)
        result = jnp.einsum("hqk,khd->qhd", weights, values, preferred_element_type=jnp.float32)
        return (result, (top + jnp.log(total))[..., 0])

    results, log_totals = lax.map(one_block, jnp.arange(TREE // QBLOCK, dtype=jnp.int32))
    return (results.reshape(TREE, query.shape[1], query.shape[2]), log_totals)


def attend_back(query, keys, values, log_totals, back_attended, layout):
    segment, parent, grandparent = layout
    scale = HEAD_DIM ** (-0.5)

    def one_block(carry, index):
        back_keys, back_values = carry
        first = index * QBLOCK
        rows = lax.dynamic_slice_in_dim(query, first, QBLOCK, 0)
        back_rows = lax.dynamic_slice_in_dim(back_attended, first, QBLOCK, 0)
        allowed = visible(first, segment, parent, grandparent)
        raw = jnp.einsum("qhd,khd->hqk", rows, keys, preferred_element_type=jnp.float32)
        scores = jnp.where(allowed[None], raw * scale, masked_score)
        weights = jnp.exp(scores - log_totals[index][..., None])
        weights_low = weights.astype(jnp.bfloat16)
        back_weights = jnp.einsum(
            "qhd,khd->hqk", back_rows, values, preferred_element_type=jnp.float32
        )
        inner = jnp.sum(weights * back_weights, axis=-1, keepdims=True)
        back_scores = (weights * (back_weights - inner) * scale).astype(jnp.bfloat16)
        back_query = jnp.einsum(
            "hqk,khd->qhd", back_scores, keys, preferred_element_type=jnp.float32
        )
        back_keys = back_keys + jnp.einsum(
            "hqk,qhd->khd", back_scores, rows, preferred_element_type=jnp.float32
        )
        back_values = back_values + jnp.einsum(
            "hqk,qhd->khd", weights_low, back_rows, preferred_element_type=jnp.float32
        )
        return ((back_keys, back_values), back_query)

    empty = jnp.zeros(keys.shape, jnp.float32)
    (back_keys, back_values), back_query = lax.scan(
        one_block, (empty, empty), jnp.arange(TREE // QBLOCK, dtype=jnp.int32)
    )
    return (back_query.reshape(query.shape), back_keys, back_values)


def shards(
    tokens,
    cotangent,
    lengths,
    parents,
    first_gain,
    first_shift,
    in_weight,
    out_weight,
    second_gain,
    second_shift,
    third_gain,
    third_shift,
    up_weight,
    down_weight,
    fourth_gain,
    fourth_shift,
):
    head_count = out_weight.shape[0] // HEAD_DIM
    mixed_weight = in_weight.reshape(D, -1)
    feed_up, feed_down = (up_weight, down_weight)

    def one_tree(sums, inputs):
        rows_in, back_rows, tree_lengths, tree_parents = inputs
        segment, parent, grandparent, position = tree_layout(tree_lengths, tree_parents)
        layout = (segment, parent, grandparent)
        rows = rows_in.astype(jnp.float32)
        normed, first_back = jax.vjp(layer_norm, rows, first_gain, first_shift)
        gathered = lax.all_gather(normed.astype(jnp.bfloat16), "tensor", axis=0, tiled=True)
        mixed = jnp.dot(gathered, mixed_weight, preferred_element_type=jnp.float32)
        mixed = mixed.reshape(TREE, 3, head_count, HEAD_DIM)
        (query_full, keys_full), rotate_back = jax.vjp(
            lambda former, latter: (rotate(former, position), rotate(latter, position)),
            mixed[:, 0],
            mixed[:, 1],
        )
        query = query_full.astype(jnp.bfloat16)
        keys = keys_full.astype(jnp.bfloat16)
        values = mixed[:, 2].astype(jnp.bfloat16)
        attended, log_totals = attend(query, keys, values, layout)
        attended_low = attended.astype(jnp.bfloat16).reshape(TREE, -1)
        branch = lax.psum_scatter(
            jnp.dot(attended_low, out_weight, preferred_element_type=jnp.float32),
            "tensor",
            scatter_dimension=0,
            tiled=True,
        )
        branch_normed, second_back = jax.vjp(layer_norm, branch, second_gain, second_shift)
        hidden = rows + branch_normed
        feed_normed, third_back = jax.vjp(layer_norm, hidden, third_gain, third_shift)
        feed_low = feed_normed.astype(jnp.bfloat16)
        feed_in = lax.all_gather(feed_low, "tensor", axis=0, tiled=True)
        upper = jnp.dot(feed_in, feed_up, preferred_element_type=jnp.float32)
        active, gelu_back = jax.vjp(gelu_tanh, upper)
        active_low = active.astype(jnp.bfloat16)
        feed_out = lax.psum_scatter(
            jnp.dot(active_low, feed_down, preferred_element_type=jnp.float32),
            "tensor",
            scatter_dimension=0,
            tiled=True,
        )
        result_normed, fourth_back = jax.vjp(layer_norm, feed_out, fourth_gain, fourth_shift)
        output = (hidden + result_normed).astype(jnp.bfloat16)
        back_out = back_rows.astype(jnp.float32)
        back_feed, fourth_gain_back, fourth_shift_back = fourth_back(back_out)
        back_feed_low = back_feed.astype(jnp.bfloat16)
        back_feed_all = lax.all_gather(back_feed_low, "tensor", axis=0, tiled=True)
        back_active = jnp.einsum(
            "td,fd->tf", back_feed_all, feed_down, preferred_element_type=jnp.float32
        )
        down_part = jnp.einsum(
            "tf,td->fd", active_low, back_feed_all, preferred_element_type=jnp.float32
        )
        (back_upper,) = gelu_back(back_active)
        back_upper_low = back_upper.astype(jnp.bfloat16)
        up_part = jnp.einsum(
            "td,tf->df", feed_in, back_upper_low, preferred_element_type=jnp.float32
        )
        back_feed_in = lax.psum_scatter(
            jnp.einsum("tf,df->td", back_upper_low, feed_up, preferred_element_type=jnp.float32),
            "tensor",
            scatter_dimension=0,
            tiled=True,
        )
        back_hidden_part, third_gain_back, third_shift_back = third_back(back_feed_in)
        back_hidden = back_out + back_hidden_part
        back_branch, second_gain_back, second_shift_back = second_back(back_hidden)
        back_branch_all = lax.all_gather(
            back_branch.astype(jnp.bfloat16), "tensor", axis=0, tiled=True
        )
        back_attended = jnp.einsum(
            "td,ed->te", back_branch_all, out_weight, preferred_element_type=jnp.float32
        )
        back_attended = back_attended.astype(jnp.bfloat16).reshape(TREE, head_count, HEAD_DIM)
        out_part = jnp.einsum(
            "te,td->ed", attended_low, back_branch_all, preferred_element_type=jnp.float32
        )
        back_query, back_keys, back_values = attend_back(
            query, keys, values, log_totals, back_attended, layout
        )
        back_former, back_latter = rotate_back((back_query, back_keys))
        back_mixed = (
            jnp.stack([back_former, back_latter, back_values], axis=1)
            .reshape(TREE, -1)
            .astype(jnp.bfloat16)
        )
        in_part = jnp.einsum("td,tc->dc", gathered, back_mixed, preferred_element_type=jnp.float32)
        back_normed = lax.psum_scatter(
            jnp.einsum(
                "tc,dc->td", back_mixed, mixed_weight, preferred_element_type=jnp.float32
            ).astype(jnp.bfloat16),
            "tensor",
            scatter_dimension=0,
            tiled=True,
        ).astype(jnp.float32)
        back_rows_in, first_gain_back, first_shift_back = first_back(back_normed)
        back_tokens = (back_hidden + back_rows_in).astype(jnp.bfloat16)
        parts = (
            first_gain_back,
            first_shift_back,
            in_part,
            out_part,
            second_gain_back,
            second_shift_back,
            third_gain_back,
            third_shift_back,
            up_part,
            down_part,
            fourth_gain_back,
            fourth_shift_back,
        )
        sums = jax.tree.map(lambda total, part: total + part, sums, parts)
        return (sums, (output, back_tokens))

    vector_zero = jnp.zeros((D,), jnp.float32)
    initial = (
        vector_zero,
        vector_zero,
        jnp.zeros(mixed_weight.shape, jnp.float32),
        jnp.zeros(out_weight.shape, jnp.float32),
        vector_zero,
        vector_zero,
        vector_zero,
        vector_zero,
        jnp.zeros(feed_up.shape, jnp.float32),
        jnp.zeros(feed_down.shape, jnp.float32),
        vector_zero,
        vector_zero,
    )
    sums, (outputs, back_tokens) = lax.scan(
        one_tree, initial, (tokens, cotangent, lengths, parents)
    )
    (
        first_gain_sum,
        first_shift_sum,
        in_sum,
        out_sum,
        second_gain_sum,
        second_shift_sum,
        third_gain_sum,
        third_shift_sum,
        up_sum,
        down_sum,
        fourth_gain_sum,
        fourth_shift_sum,
    ) = sums
    in_sum, out_sum, up_sum, down_sum = (
        lax.psum(in_sum.astype(jnp.bfloat16), "dp").astype(jnp.float32),
        lax.psum(out_sum.astype(jnp.bfloat16), "dp").astype(jnp.float32),
        lax.psum(up_sum.astype(jnp.bfloat16), "dp").astype(jnp.float32),
        lax.psum(down_sum.astype(jnp.bfloat16), "dp").astype(jnp.float32),
    )
    norm_totals = lax.psum(
        (
            first_gain_sum,
            first_shift_sum,
            second_gain_sum,
            second_shift_sum,
            third_gain_sum,
            third_shift_sum,
            fourth_gain_sum,
            fourth_shift_sum,
        ),
        ("dp", "tensor"),
    )
    return (
        outputs,
        back_tokens,
        norm_totals[0],
        norm_totals[1],
        in_sum.reshape(in_weight.shape),
        out_sum,
        norm_totals[2],
        norm_totals[3],
        norm_totals[4],
        norm_totals[5],
        up_sum,
        down_sum,
        norm_totals[6],
        norm_totals[7],
    )


def solution(mesh):
    in_specs = (
        P("dp", "tensor", None),
        P("dp", "tensor", None),
        P("dp", None),
        P("dp", None),
        P(),
        P(),
        P(None, None, "tensor"),
        P("tensor", None),
        P(),
        P(),
        P(),
        P(),
        P(None, "tensor"),
        P("tensor", None),
        P(),
        P(),
    )
    out_specs = (
        P("dp", "tensor", None),
        P("dp", "tensor", None),
        P(),
        P(),
        P(None, None, "tensor"),
        P("tensor", None),
        P(),
        P(),
        P(),
        P(),
        P(None, "tensor"),
        P("tensor", None),
        P(),
        P(),
    )
    return jax.shard_map(shards, mesh=mesh, in_specs=in_specs, out_specs=out_specs, check_vma=False)
```

profile of v0, /device:TPU:0, one launch (start us, length us, event | category | flops | bytes accessed | tf_op | source)
XLA Modules:
  0.0 1786.9 jit_solution(14136928889603180438)
XLA Ops:
  10.7 1665.2 %while.97 = (s32[]{:T(128)}, f32[1024]{0:T(1024)}, f32[1024]{0:T(1024)}, f32[1024,384]{1,0:T(8,128)}, f32[128,1024]{1,0:T(8,128)}, /*index=5*/f32[1024]{0:T(1024...) while((s32[]{:T(128)}, f32[1024]{0:T(1024)}, ...), condition=%wide.region_42.43_spmd.clone, body=%wide.region_0.42_spmd.clone.sunk | while | flops 21393750016 | bytes 692590336 | solution.py:287
  19.7 46.6 %all-gather.5.cloned.1.call-done = bf16[2048,1024]{1,0:T(8,128)(2,1)} async-done(((bf16[256,1024]{1,0:T(8,128)(2,1)}), bf16[2048,1024]{1,0:T(8,128)(2,1)}) %all-gather.5.cloned.1.call-update) | async-done | bytes 4194320 | tf_op jit(solution)/shard_map/while/body/eval_jaxpr/all_gather | solution.py:166
  71.1 41.0 %while.98 = (s32[]{:T(128)}, bf16[4,512,2,64]{1,3,2,0:T(8,128)(2,1)S(1)}, f32[4,2,512]{2,1,0:T(2,128)S(1)}, s32[2048]{0:T(1024)S(1)}, s32[4]{0:T(128)S(1)}, /*in...) while((s32[]{:T(128)}, ...), condition=%wide.region_12.12_spmd, body=%wide.region_9.11_spmd.sunk | while | flops 569376256 | bytes 30865636 | solution.py:97
  118.8 87.8 %reduce-scatter.5.cloned.1.call-done = f32[256,1024]{1,0:T(8,128)} async-done(((f32[2048,1024]{1,0:T(8,128)}), f32[256,1024]{1,0:T(8,128)}) %reduce-scatter.5.cloned.1.call-update) | async-done | bytes 1048592 | tf_op jit(solution)/shard_map/while/body/eval_jaxpr/reduce_scatter | solution.py:179
  212.5 45.4 %all-gather.7.cloned.1.call-done = bf16[2048,1024]{1,0:T(8,128)(2,1)} async-done(((bf16[256,1024]{1,0:T(8,128)(2,1)}), bf16[2048,1024]{1,0:T(8,128)(2,1)}) %all-gather.7.cloned.1.call-update) | async-done | bytes 4194320 | tf_op jit(solution)/shard_map/while/body/eval_jaxpr/all_gather | solution.py:189
  270.6 88.4 %reduce-scatter.7.cloned.1.call-done = f32[256,1024]{1,0:T(8,128)} async-done(((f32[2048,1024]{1,0:T(8,128)}), f32[256,1024]{1,0:T(8,128)}) %reduce-scatter.7.cloned.1.call-update) | async-done | bytes 1048592 | tf_op jit(solution)/shard_map/while/body/eval_jaxpr/reduce_scatter | solution.py:193
  365.1 45.4 %all-gather.9.cloned.1.call-done = bf16[2048,1024]{1,0:T(8,128)(2,1)} async-done(((bf16[256,1024]{1,0:T(8,128)(2,1)}), bf16[2048,1024]{1,0:T(8,128)(2,1)}) %all-gather.9.cloned.1.call-update) | async-done | bytes 4194320 | tf_op jit(solution)/shard_map/while/body/eval_jaxpr/all_gather | solution.py:204
  425.5 88.4 %reduce-scatter.9.cloned.1.call-done = f32[256,1024]{1,0:T(8,128)} async-done(((f32[2048,1024]{1,0:T(8,128)}), f32[256,1024]{1,0:T(8,128)}) %reduce-scatter.9.cloned.1.call-update) | async-done | bytes 1048592 | tf_op jit(solution)/shard_map/while/body/eval_jaxpr/reduce_scatter | solution.py:216
  520.0 45.4 %all-gather.11.cloned.1.call-done = bf16[2048,1024]{1,0:T(8,128)(2,1)} async-done(((bf16[256,1024]{1,0:T(8,128)(2,1)}), bf16[2048,1024]{1,0:T(8,128)(2,1)}) %all-gather.11.cloned.1.call-update) | async-done | bytes 4194320 | tf_op jit(solution)/shard_map/while/body/eval_jaxpr/all_gather | solution.py:225
  569.9 208.0 %while.99 = (s32[]{:T(128)}, f32[2048,2,64]{0,2,1:T(8,128)}, f32[2048,2,64]{0,2,1:T(8,128)}, f32[4,512,2,64]{1,0,3,2:T(4,128)}, s32[4]{0:T(128)S(1)}, /*index=5*...) while((s32[]{:T(128)}, f32[2048,2,64]{0,2,1:T(8,128)}, ...), condition=%wide.region_30.30_spmd.clone, body=%wide.region_28.29_spmd.clone.sunk | while | flops 1405098496 | bytes 134535632 | solution.py:132
  600.2 15.1 fusion.295
  651.8 15.4 fusion.295
  690.0 13.7 fusion.297
  703.7 15.4 fusion.295
  755.7 15.4 fusion.295
  809.5 29.1 %reduce-scatter.11.cloned.1.call-done = bf16[256,1024]{1,0:T(8,128)(2,1)} async-done(((bf16[2048,1024]{1,0:T(8,128)(2,1)}), bf16[256,1024]{1,0:T(8,128)(2,1)}) %reduce-scatter.11.cloned.1.call-update) | async-done | bytes 524304 | tf_op jit(solution)/shard_map/while/body/eval_jaxpr/reduce_scatter | solution.py:245
  853.3 42.3 %all-gather.5.cloned.1.call-done = bf16[2048,1024]{1,0:T(8,128)(2,1)} async-done(((bf16[256,1024]{1,0:T(8,128)(2,1)}), bf16[2048,1024]{1,0:T(8,128)(2,1)}) %all-gather.5.cloned.1.call-update) | async-done | bytes 4194320 | tf_op jit(solution)/shard_map/while/body/eval_jaxpr/all_gather | solution.py:166
  900.5 41.0 %while.98 = (s32[]{:T(128)}, bf16[4,512,2,64]{1,3,2,0:T(8,128)(2,1)S(1)}, f32[4,2,512]{2,1,0:T(2,128)S(1)}, s32[2048]{0:T(1024)S(1)}, s32[4]{0:T(128)S(1)}, /*in...) while((s32[]{:T(128)}, ...), condition=%wide.region_12.12_spmd, body=%wide.region_9.11_spmd.sunk | while | flops 569376256 | bytes 30865636 | solution.py:97
  947.9 88.0 %reduce-scatter.5.cloned.1.call-done = f32[256,1024]{1,0:T(8,128)} async-done(((f32[2048,1024]{1,0:T(8,128)}), f32[256,1024]{1,0:T(8,128)}) %reduce-scatter.5.cloned.1.call-update) | async-done | bytes 1048592 | tf_op jit(solution)/shard_map/while/body/eval_jaxpr/reduce_scatter | solution.py:179
  1041.8 45.4 %all-gather.7.cloned.1.call-done = bf16[2048,1024]{1,0:T(8,128)(2,1)} async-done(((bf16[256,1024]{1,0:T(8,128)(2,1)}), bf16[2048,1024]{1,0:T(8,128)(2,1)}) %all-gather.7.cloned.1.call-update) | async-done | bytes 4194320 | tf_op jit(solution)/shard_map/while/body/eval_jaxpr/all_gather | solution.py:189
  1099.9 88.4 %reduce-scatter.7.cloned.1.call-done = f32[256,1024]{1,0:T(8,128)} async-done(((f32[2048,1024]{1,0:T(8,128)}), f32[256,1024]{1,0:T(8,128)}) %reduce-scatter.7.cloned.1.call-update) | async-done | bytes 1048592 | tf_op jit(solution)/shard_map/while/body/eval_jaxpr/reduce_scatter | solution.py:193
  1194.5 45.4 %all-gather.9.cloned.1.call-done = bf16[2048,1024]{1,0:T(8,128)(2,1)} async-done(((bf16[256,1024]{1,0:T(8,128)(2,1)}), bf16[2048,1024]{1,0:T(8,128)(2,1)}) %all-gather.9.cloned.1.call-update) | async-done | bytes 4194320 | tf_op jit(solution)/shard_map/while/body/eval_jaxpr/all_gather | solution.py:204
  1254.8 88.4 %reduce-scatter.9.cloned.1.call-done = f32[256,1024]{1,0:T(8,128)} async-done(((f32[2048,1024]{1,0:T(8,128)}), f32[256,1024]{1,0:T(8,128)}) %reduce-scatter.9.cloned.1.call-update) | async-done | bytes 1048592 | tf_op jit(solution)/shard_map/while/body/eval_jaxpr/reduce_scatter | solution.py:216
  1349.3 45.4 %all-gather.11.cloned.1.call-done = bf16[2048,1024]{1,0:T(8,128)(2,1)} async-done(((bf16[256,1024]{1,0:T(8,128)(2,1)}), bf16[2048,1024]{1,0:T(8,128)(2,1)}) %all-gather.11.cloned.1.call-update) | async-done | bytes 4194320 | tf_op jit(solution)/shard_map/while/body/eval_jaxpr/all_gather | solution.py:225
  1399.2 208.0 %while.99 = (s32[]{:T(128)}, f32[2048,2,64]{0,2,1:T(8,128)}, f32[2048,2,64]{0,2,1:T(8,128)}, f32[4,512,2,64]{1,0,3,2:T(4,128)}, s32[4]{0:T(128)S(1)}, /*index=5*...) while((s32[]{:T(128)}, f32[2048,2,64]{0,2,1:T(8,128)}, ...), condition=%wide.region_30.30_spmd.clone, body=%wide.region_28.29_spmd.clone.sunk | while | flops 1405098496 | bytes 134535632 | solution.py:132
  1429.5 15.1 fusion.295
  1481.1 15.4 fusion.295
  1533.1 15.4 fusion.295
  1585.0 15.4 fusion.295
  1641.0 27.0 %reduce-scatter.11.cloned.1.call-done = bf16[256,1024]{1,0:T(8,128)(2,1)} async-done(((bf16[2048,1024]{1,0:T(8,128)(2,1)}), bf16[256,1024]{1,0:T(8,128)(2,1)}) %reduce-scatter.11.cloned.1.call-update) | async-done | bytes 524304 | tf_op jit(solution)/shard_map/while/body/eval_jaxpr/reduce_scatter | solution.py:245
  1684.5 39.7 %all-reduce.4 = (f32[1024]{0:T(1024)}, f32[1024]{0:T(1024)}, f32[1024]{0:T(1024)}, f32[1024]{0:T(1024)}, f32[1024]{0:T(1024)}, /*index=5*/f32[1024]{0:T(1024)}, f32[1024]{0:T(1024)}, f32[1024]{0:T(1024)}) all-reduce(f32[1024]{0:T(1024)S(1)} %copy-done.65, ...), channel_id=1, replica_groups=mesh['dp'=4,'tensor'=8] {'dp','tensor'}, use_global_device_ids=true, to_apply=%region_43.44 | all-reduce | flops 8192 | bytes 65536 | tf_op jit(solution)/shard_map/psum | solution.py:310
  1724.3 46.4 %all-reduce.8.cloned.1.call-done = (bf16[1024,3,128]{0,2,1:T(8,128)(2,1)}, bf16[128,1024]{1,0:T(8,128)(2,1)}, bf16[1024,512]{1,0:T(8,128)(2,1)}, bf16[512,1024]{1,0:T(8,128)(2,1)}) async-done(((bf16[1024,3,128]{0,2,1:T(8,128)(2,1)}, bf16[128,1024]{1,0:T(8,128)(2,1)}, bf16[1024,512]{1,0:T(8,128)(2,1)}, bf16[512,1024]{1,0:T(8,128)(2,1)}), (bf16[1024,3,128]{0,2,1:T(8,128)(2,1)}, bf16[128,1024]{1,0:T(8,128)(2,1)}, ...) | async-done | bytes 3145744 | tf_op jit(solution)/shard_map/psum | solution.py:305
  (763 shorter events, 570.0 us)
Async XLA Ops:
  10.7 55.5 %all-gather.5.cloned.1.call-start = ((), (), s32[]{:S(2)}) async-start(), calls=%async_computation.5 | async-start | bytes 4718592 | tf_op jit(solution)/shard_map/while/body/eval_jaxpr/all_gather | solution.py:166
  16.5 190.1 %reduce-scatter.5.cloned.1.call-start = ((), (), s32[]{:S(2)}) async-start(), calls=%async_computation.6 | async-start | bytes 9437184 | tf_op jit(solution)/shard_map/while/body/eval_jaxpr/reduce_scatter | solution.py:179
  118.0 91.4 %copy-start.35 = (f32[1024]{0:T(1024)S(1)}, f32[1024]{0:T(1024)}, u32[]{:S(2)}) copy-start(f32[1024]{0:T(1024)} %get-tuple-element.1640) | copy-start | bytes 12292 | tf_op jit(solution)/shard_map/while
  118.1 91.4 %copy-start.66 = (f32[1024]{0:T(1024)S(1)}, f32[1024]{0:T(1024)}, u32[]{:S(2)}) copy-start(f32[1024]{0:T(1024)} %get-tuple-element.1641) | copy-start | bytes 12292 | tf_op jit(solution)/shard_map/while
  118.1 93.3 %copy-start.33 = (f32[1024]{0:T(1024)S(1)}, f32[1024]{0:T(1024)}, u32[]{:S(2)}) copy-start(f32[1024]{0:T(1024)} %get-tuple-element.1642) | copy-start | bytes 12292 | tf_op jit(solution)/shard_map/while
  118.1 93.3 %copy-start.67 = (f32[1024]{0:T(1024)S(1)}, f32[1024]{0:T(1024)}, u32[]{:S(2)}) copy-start(f32[1024]{0:T(1024)} %get-tuple-element.1643) | copy-start | bytes 12292 | tf_op jit(solution)/shard_map/while
  118.1 139.8 %copy-start.71 = (bf16[1024,512]{1,0:T(8,128)(2,1)S(1)}, bf16[1024,512]{1,0:T(8,128)(2,1)}, u32[]{:S(2)}) copy-start(bf16[1024,512]{1,0:T(8,128)(2,1)} %get-tuple-element.1644) | copy-start | bytes 3145732 | tf_op jit(solution)/shard_map/while
  118.1 139.8 %all-gather.7.cloned.1.call-start = ((), (), s32[]{:S(2)}) async-start(), calls=%async_computation.7 | async-start | bytes 4718592 | tf_op jit(solution)/shard_map/while/body/eval_jaxpr/all_gather | solution.py:189
  212.5 146.5 %reduce-scatter.7.cloned.1.call-start = ((), (), s32[]{:S(2)}) async-start(), calls=%async_computation.8 | async-start | bytes 9437184 | tf_op jit(solution)/shard_map/while/body/eval_jaxpr/reduce_scatter | solution.py:193
  270.5 91.5 %copy-start.13 = (bf16[2,256,1024]{2,1,0:T(8,128)(2,1)S(1)}, bf16[2,256,1024]{2,1,0:T(8,128)(2,1)}, u32[]{:S(2)}) copy-start(bf16[2,256,1024]{2,1,0:T(8,128)(2,1)} %get-tuple-element.1638) | copy-start | bytes 3145732 | tf_op jit(solution)/shard_map/while
  270.5 91.5 %copy-start.34 = (f32[1024]{0:T(1024)S(1)}, f32[1024]{0:T(1024)}, u32[]{:S(2)}) copy-start(f32[1024]{0:T(1024)} %get-tuple-element.1645) | copy-start | bytes 12292 | tf_op jit(solution)/shard_map/while
  270.5 140.0 %all-gather.9.cloned.1.call-start = ((), (), s32[]{:S(2)}) async-start(), calls=%async_computation.9 | async-start | bytes 4718592 | tf_op jit(solution)/shard_map/while/body/eval_jaxpr/all_gather | solution.py:204
  365.1 148.8 %reduce-scatter.9.cloned.1.call-start = ((), (), s32[]{:S(2)}) async-start(), calls=%async_computation.10 | async-start | bytes 9437184 | tf_op jit(solution)/shard_map/while/body/eval_jaxpr/reduce_scatter | solution.py:216
  425.4 91.8 %copy-start.2 = (f32[256,1024]{1,0:T(8,128)S(1)}, f32[256,1024]{1,0:T(8,128)}, u32[]{:S(2)}) copy-start(f32[256,1024]{1,0:T(8,128)} %reduce-scatter.5.cloned.1.call-done) | copy-start | bytes 3145732 | tf_op jit(solution)/shard_map/while
  425.5 139.9 %all-gather.11.cloned.1.call-start = ((), (), s32[]{:S(2)}) async-start(), calls=%async_computation.11 | async-start | bytes 4718592 | tf_op jit(solution)/shard_map/while/body/eval_jaxpr/all_gather | solution.py:225
  519.9 318.8 %reduce-scatter.11.cloned.1.call-start = ((), (), s32[]{:S(2)}) async-start(), calls=%async_computation.12 | async-start | bytes 4718592 | tf_op jit(solution)/shard_map/while/body/eval_jaxpr/reduce_scatter | solution.py:245
  844.2 51.4 %all-gather.5.cloned.1.call-start = ((), (), s32[]{:S(2)}) async-start(), calls=%async_computation.5 | async-start | bytes 4718592 | tf_op jit(solution)/shard_map/while/body/eval_jaxpr/all_gather | solution.py:166
  850.1 185.8 %reduce-scatter.5.cloned.1.call-start = ((), (), s32[]{:S(2)}) async-start(), calls=%async_computation.6 | async-start | bytes 9437184 | tf_op jit(solution)/shard_map/while/body/eval_jaxpr/reduce_scatter | solution.py:179
  947.4 91.4 %copy-start.35 = (f32[1024]{0:T(1024)S(1)}, f32[1024]{0:T(1024)}, u32[]{:S(2)}) copy-start(f32[1024]{0:T(1024)} %get-tuple-element.1640) | copy-start | bytes 12292 | tf_op jit(solution)/shard_map/while
  947.4 93.3 %copy-start.33 = (f32[1024]{0:T(1024)S(1)}, f32[1024]{0:T(1024)}, u32[]{:S(2)}) copy-start(f32[1024]{0:T(1024)} %get-tuple-element.1642) | copy-start | bytes 12292 | tf_op jit(solution)/shard_map/while
  947.4 93.3 %copy-start.67 = (f32[1024]{0:T(1024)S(1)}, f32[1024]{0:T(1024)}, u32[]{:S(2)}) copy-start(f32[1024]{0:T(1024)} %get-tuple-element.1643) | copy-start | bytes 12292 | tf_op jit(solution)/shard_map/while
  947.4 139.8 %copy-start.71 = (bf16[1024,512]{1,0:T(8,128)(2,1)S(1)}, bf16[1024,512]{1,0:T(8,128)(2,1)}, u32[]{:S(2)}) copy-start(bf16[1024,512]{1,0:T(8,128)(2,1)} %get-tuple-element.1644) | copy-start | bytes 3145732 | tf_op jit(solution)/shard_map/while
  947.4 139.8 %all-gather.7.cloned.1.call-start = ((), (), s32[]{:S(2)}) async-start(), calls=%async_computation.7 | async-start | bytes 4718592 | tf_op jit(solution)/shard_map/while/body/eval_jaxpr/all_gather | solution.py:189
  1041.8 146.6 %reduce-scatter.7.cloned.1.call-start = ((), (), s32[]{:S(2)}) async-start(), calls=%async_computation.8 | async-start | bytes 9437184 | tf_op jit(solution)/shard_map/while/body/eval_jaxpr/reduce_scatter | solution.py:193
  1099.8 91.5 %copy-start.13 = (bf16[2,256,1024]{2,1,0:T(8,128)(2,1)S(1)}, bf16[2,256,1024]{2,1,0:T(8,128)(2,1)}, u32[]{:S(2)}) copy-start(bf16[2,256,1024]{2,1,0:T(8,128)(2,1)} %get-tuple-element.1638) | copy-start | bytes 3145732 | tf_op jit(solution)/shard_map/while
  1099.8 91.5 %copy-start.34 = (f32[1024]{0:T(1024)S(1)}, f32[1024]{0:T(1024)}, u32[]{:S(2)}) copy-start(f32[1024]{0:T(1024)} %get-tuple-element.1645) | copy-start | bytes 12292 | tf_op jit(solution)/shard_map/while
  1099.9 140.0 %all-gather.9.cloned.1.call-start = ((), (), s32[]{:S(2)}) async-start(), calls=%async_computation.9 | async-start | bytes 4718592 | tf_op jit(solution)/shard_map/while/body/eval_jaxpr/all_gather | solution.py:204
  1194.4 148.8 %reduce-scatter.9.cloned.1.call-start = ((), (), s32[]{:S(2)}) async-start(), calls=%async_computation.10 | async-start | bytes 9437184 | tf_op jit(solution)/shard_map/while/body/eval_jaxpr/reduce_scatter | solution.py:216
  1254.8 91.8 %copy-start.2 = (f32[256,1024]{1,0:T(8,128)S(1)}, f32[256,1024]{1,0:T(8,128)}, u32[]{:S(2)}) copy-start(f32[256,1024]{1,0:T(8,128)} %reduce-scatter.5.cloned.1.call-done) | copy-start | bytes 3145732 | tf_op jit(solution)/shard_map/while
  1254.8 139.9 %all-gather.11.cloned.1.call-start = ((), (), s32[]{:S(2)}) async-start(), calls=%async_computation.11 | async-start | bytes 4718592 | tf_op jit(solution)/shard_map/while/body/eval_jaxpr/all_gather | solution.py:225
  1349.2 318.8 %reduce-scatter.11.cloned.1.call-start = ((), (), s32[]{:S(2)}) async-start(), calls=%async_computation.12 | async-start | bytes 4718592 | tf_op jit(solution)/shard_map/while/body/eval_jaxpr/reduce_scatter | solution.py:245
  1675.9 94.8 %all-reduce.8.cloned.1.call-start = ((), (), s32[]{:S(2)}) async-start(), calls=%async_computation.4 | async-start | bytes 6291456 | tf_op jit(solution)/shard_map/psum | solution.py:305
  (159 other events, 1772.2 us)
Sparse Core Ops, SparseCore 0:
  16.6 49.5 all-gather.4
  118.2 88.3 reduce-scatter.4
  212.6 45.3 all-gather.6
  270.7 88.3 reduce-scatter.6
  365.2 45.3 all-gather.8
  425.6 88.3 reduce-scatter.8
  520.0 45.3 all-gather.10
  789.9 48.6 reduce-scatter.10
  850.2 45.3 all-gather.4
  947.5 88.3 reduce-scatter.4
  1041.9 45.3 all-gather.6
  1100.0 88.3 reduce-scatter.6
  1194.5 45.3 all-gather.8
  1254.9 88.3 reduce-scatter.8
  1349.3 45.3 all-gather.10
  1619.3 48.7 reduce-scatter.10
Sparse Core Ops, SparseCore 1:
  1684.5 86.1 all-reduce.7
where the time goes:
time: 1790 us
  waiting for transfers between devices  994 us (56%)
  matrix products  464 us (26%)
  other arithmetic  127 us (7%)
  local copies, waits for them, and re-layouts  114 us (6%)
  blocking collectives  39.7 us (2%)
  loops' own time  31.6 us (2%)
    reduce_scatter x2, waiting for transfers between devices, one_tree(): lax.psum_scatter(jnp.dot(active_low, feed_down, preferred_element_type=jn...  177 us
    reduce_scatter x2, waiting for transfers between devices, one_tree(): lax.psum_scatter(jnp.einsum('tf,df->td', back_upper_low, feed_up, preferr...  177 us
    reduce_scatter x2, waiting for transfers between devices, one_tree(): lax.psum_scatter(jnp.dot(attended_low, out_weight, preferred_element_type...  176 us
    dot_general x8, matrix products, one_block(): jnp.einsum('hqk,qhd->khd', back_scores, rows, preferred_element_type=jnp....  123 us
    dot_general x8, matrix products, one_block(): jnp.einsum('hqk,khd->qhd', back_scores, keys, preferred_element_type=jnp....  110 us
    all_gather x2, waiting for transfers between devices, one_tree(): feed_in = lax.all_gather(feed_low, 'tensor', axis=0, tiled=True)  90.9 us
    all_gather x2, waiting for transfers between devices, one_tree(): back_feed_all = lax.all_gather(back_feed_low, 'tensor', axis=0, tiled=True)  90.9 us
    all_gather x2, waiting for transfers between devices, one_tree(): lax.all_gather(back_branch.astype(jnp.bfloat16), 'tensor', axis=0, tiled=...  90.8 us
  transfers between devices with their start and end apart: 17, of which 17 were waited for; matrix products, arithmetic and copies ran while one was open for 2% of the time, Pallas kernels for 0%

commit v1 on v0

v1 whole, which is shorter than its diff:
```python
import functools
import jax
import jax.numpy as jnp
from jax import lax
from jax.experimental import pallas as pl
from jax.experimental.pallas import tpu as pltpu
from jax.sharding import PartitionSpec as P

HEAD_DIM = 64
LANES = 128
VROWS = 80
BLOCK = 256
TRUNK = 512
SEGMENTS = 13

rope_base = 10000.0
norm_eps = 1e-05
masked_score = -1e30
f32, bf16 = jnp.float32, jnp.bfloat16
NN = (((1,), (0,)), ((), ()))
NT = (((1,), (1,)), ((), ()))
TN = (((0,), (0,)), ((), ()))
MESH = pl.DeviceIdType.MESH
VMEM = pl.BlockSpec(memory_space=pltpu.VMEM)


def dot(a, b, dims=NN):
    return lax.dot_general(a, b, dims, preferred_element_type=f32)


def lane_of(shape):
    return lax.broadcasted_iota(jnp.int32, shape, len(shape) - 1)


def row_of(shape):
    return lax.broadcasted_iota(jnp.int32, shape, len(shape) - 2)


def span(i, n):
    return pl.ds(pl.multiple_of(i * n, n), n)


def split3(v):
    hi = v.astype(bf16).astype(f32)
    mid = (v - hi).astype(bf16).astype(f32)
    return hi, mid, v - hi - mid


def layer_norm(values, gain, shift):
    average = jnp.mean(values, axis=-1, keepdims=True)
    centered = values - average
    spread = jnp.mean(centered * centered, axis=-1, keepdims=True)
    return centered * lax.rsqrt(spread + norm_eps) * gain + shift


def tree_layout(tree_lengths, tree_parents, rows):
    seg_sizes = jnp.concatenate([jnp.full((1,), TRUNK, jnp.int32), tree_lengths])
    ends = jnp.cumsum(seg_sizes)
    starts = ends - seg_sizes
    places = jnp.arange(rows, dtype=jnp.int32)
    labels = jnp.arange(SEGMENTS, dtype=jnp.int32)
    segment = jnp.sum((places[:, None] >= ends[None, :]).astype(jnp.int32), axis=1)
    own_hot = (segment[:, None] == labels[None, :]).astype(jnp.int32)
    parent = jnp.sum(own_hot * tree_parents[None, :], axis=1)
    parent_hot = (parent[:, None] == labels[None, :]).astype(jnp.int32)
    grandparent = jnp.sum(parent_hot * tree_parents[None, :], axis=1)
    parent_size = jnp.sum(parent_hot * seg_sizes[None, :], axis=1)
    depth_start = jnp.where(segment > 0, TRUNK, 0).astype(jnp.int32) + jnp.where(
        parent > 0, parent_size, 0
    )
    position = places - jnp.sum(own_hot * starts[None, :], axis=1) + depth_start
    return (segment, parent, grandparent, position)


def tables(tree_lengths, tree_parents, rows):
    segment, parent, grand, position = tree_layout(tree_lengths, tree_parents, rows)
    lane = jnp.arange(LANES, dtype=jnp.int32)
    half = HEAD_DIM // 2
    inverse = rope_base ** (-(lane % half).astype(f32) * 2.0 / HEAD_DIM)
    angle = position.astype(f32)[:, None] * inverse[None, :]
    cosine = jnp.cos(angle)
    sine = jnp.where((lane % HEAD_DIM) < half, -1.0, 1.0)[None, :] * jnp.sin(angle)
    label = (lane - HEAD_DIM)[None, :]
    own = segment[:, None] == label
    path = own | (parent[:, None] == label) | (grand[:, None] == label)
    hidden = (label >= 0) & (label < SEGMENTS) & ~path
    queries = jnp.where(hidden, masked_score, 0.0).astype(f32)
    ones = (label >= 16) & (label < 19)
    keys = jnp.where(own | ones, 1.0, 0.0).astype(f32)
    return cosine, sine, queries, keys
def barrier(partners):
    semaphore = pltpu.get_barrier_semaphore()
    for partner in partners:
        pl.semaphore_signal(semaphore, inc=1, device_id=partner, device_id_type=MESH)
    pl.semaphore_wait(semaphore, len(partners))


def send(source, target, send_sem, recv_sem, device):
    copy = pltpu.make_async_remote_copy(
        src_ref=source,
        dst_ref=target,
        send_sem=send_sem,
        recv_sem=recv_sem,
        device_id=device,
        device_id_type=MESH,
    )
    copy.start()
    return copy


def gather_kernel(n_d, n_t, x_ref, w_ref, o_ref, u_ref, rs, ss, rb, sb, rw, sw, rp, sp):
    d, t = lax.axis_index("dp"), lax.axis_index("tensor")
    trees, rows, _ = x_ref.shape
    chips = n_t // 2
    group = n_t // trees
    chip, core = t // 2, lax.rem(t, 2)
    other = 2 * chip + 1 - core
    near = group // 2
    tree = t // group
    line = [lax.rem(chip + k, chips) for k in range(1, chips)]
    planes = [lax.rem(d + k, n_d) for k in range(1, n_d)]
    owners = [(j * group + t // trees) for j in range(trees)]
    givers = [lax.rem(t, group) * trees + i for i in range(trees)]
    barrier([(d, lax.rem(t + k, n_t)) for k in range(1, n_t)] + [(p, t) for p in planes])
    part = w_ref.shape[1] // n_d

    copies = []
    mine = w_ref.at[:, span(d, part), :]
    for j in range(trees):
        slot = u_ref.at[lax.rem(t, trees), :, span(d, part), :]

        @pl.when(owners[j] != t)
        def _():
            send(mine, slot, sw.at[j], rw.at[lax.rem(t, trees)], (d, owners[j]))

        @pl.when(owners[j] == t)
        def _():
            u_ref[lax.rem(t, trees), :, span(d, part), :] = w_ref[:, span(d, part), :]

    def block(c, k):
        return o_ref.at[span(2 * c + k, rows)]

    for k, c in enumerate(line):
        copies.append(send(x_ref.at[c // near], block(chip, core), ss.at[k], rs.at[k], (d, 2 * c + core)))
    o_ref[span(t, rows), :] = x_ref[tree]
    copies.append(send(x_ref.at[tree], block(chip, core), sb.at[chips - 1], rb.at[chips - 1], (d, other)))
    for i in range(trees):
        slot = u_ref.at[i, :, span(d, part), :]

        @pl.when(givers[i] != t)
        def _():
            pltpu.make_async_remote_copy(
                src_ref=mine, dst_ref=slot, send_sem=sw.at[0], recv_sem=rw.at[i],
                device_id=(d, givers[i]), device_id_type=MESH,
            ).wait_recv()

    mine_all = u_ref.at[:, :, span(d, part), :]
    for k, p in enumerate(planes):
        copies.append(send(mine_all, mine_all, sp.at[k], rp.at[k], (p, t)))
    for k in range(chips - 1):
        source = lax.rem(chip + chips - 1 - k, chips)
        copies[k].wait_recv()
        copies.append(send(block(source, core), block(source, core), sb.at[k], rb.at[k], (d, other)))
    for j in range(trees):

        @pl.when(owners[j] != t)
        def _():
            pltpu.make_async_remote_copy(
                src_ref=mine, dst_ref=mine, send_sem=sw.at[j], recv_sem=rw.at[0],
                device_id=(d, owners[j]), device_id_type=MESH,
            ).wait_send()

    for i, copy in enumerate(copies):
        if i < chips - 1:
            copy.wait_send()
        else:
            copy.wait()


def gather_tree(n_d, n_t, normed, weight):
    trees, rows, wide = normed.shape
    chips = n_t // 2
    dma = pltpu.SemaphoreType.DMA
    return pl.pallas_call(
        functools.partial(gather_kernel, n_d, n_t),
        in_specs=[VMEM] * 2,
        out_specs=[VMEM] * 2,
        out_shape=[
            jax.ShapeDtypeStruct((n_t * rows, wide), bf16),
            jax.ShapeDtypeStruct((trees,) + weight.shape, bf16),
        ],
        scratch_shapes=[
            dma((chips - 1,)), dma((chips - 1,)), dma((chips,)), dma((chips,)),
            dma((trees,)), dma((trees,)), dma((n_d - 1,)), dma((n_d - 1,)),
        ],
        compiler_params=pltpu.CompilerParams(collective_id=0, has_side_effects=True),
        name="gather_tree",
    )(normed, weight)


def heads_kernel(n_t, trees, back, x_ref, o_ref, ss, rs):
    d, t = lax.axis_index("dp"), lax.axis_index("tensor")
    group = n_t // trees
    others = [lax.rem(t + k, n_t) for k in range(1, n_t)]
    barrier([(d, o) for o in others])
    if back:
        rows, width = x_ref.shape[1], x_ref.shape[2] // group
        cut = lambda o: x_ref.at[o // group, :, span(lax.rem(o, group), width)]
        place = o_ref.at[span(t, rows), :]
    else:
        rows, width = o_ref.shape[1], x_ref.shape[1]
        cut = lambda o: x_ref.at[span(o, rows), :]
        place = o_ref.at[t // group, :, span(lax.rem(t, group), width)]
    copies = [
        send(cut(o), place, ss.at[k], rs.at[k], (d, o)) for k, o in enumerate(others)
    ]
    place[...] = cut(t)[...]
    for copy in copies:
        copy.wait()


def exchange_heads(n_t, trees, x, back):
    if back:
        _, rows, wide = x.shape
        shape = (n_t * rows, wide * trees // n_t)
    else:
        shape = (trees, x.shape[0] // n_t, x.shape[1] * (n_t // trees))
    dma = pltpu.SemaphoreType.DMA
    return pl.pallas_call(
        functools.partial(heads_kernel, n_t, trees, back),
        in_specs=[VMEM],
        out_specs=VMEM,
        out_shape=jax.ShapeDtypeStruct(shape, bf16),
        scratch_shapes=[dma((n_t - 1,)), dma((n_t - 1,))],
        compiler_params=pltpu.CompilerParams(collective_id=2 if back else 1, has_side_effects=True),
        name="heads_back" if back else "heads_out",
    )(x)


def reduce_kernel(n_t, x_ref, o_ref, side, out, land, ss, rs, sb, rb):
    d, t = lax.axis_index("dp"), lax.axis_index("tensor")
    trees, rows, _ = o_ref.shape
    chips = n_t // 2
    near = chips // trees
    chip, core = t // 2, lax.rem(t, 2)
    other = 2 * chip + 1 - core
    line = [lax.rem(chip + k, chips) for k in range(1, chips)]
    barrier([(d, other)] + [(d, 2 * c + core) for c in line])
    pairs = []
    for k, c in enumerate(line + [chip]):
        theirs = x_ref.at[span(2 * c + 1 - core, rows), :]
        pairs.append(send(theirs, side.at[k], sb.at[k], rb.at[k], (d, other)))
    copies = []
    for k, c in enumerate(line):
        pairs[k].wait_recv()
        out[k] = (x_ref[span(2 * c + core, rows), :].astype(f32) + side[k].astype(f32)).astype(bf16)
        copies.append(send(out.at[k], land.at[k], ss.at[k], rs.at[k], (d, 2 * c + core)))
    pairs[chips - 1].wait_recv()
    o_ref[...] = jnp.zeros_like(o_ref)
    o_ref[chip // near] = x_ref[span(t, rows), :].astype(f32) + side[chips - 1].astype(f32)
    for k in range(chips - 1):
        copies[k].wait_recv()
        source = lax.rem(chip + chips - 1 - k, chips)
        o_ref[source // near] += land[k].astype(f32)
    for copy in pairs + copies:
        copy.wait_send()


def reduce_tree(n_t, trees, x):
    rows, wide = x.shape[0] // n_t, x.shape[1]
    chips = n_t // 2
    dma = pltpu.SemaphoreType.DMA
    return pl.pallas_call(
        functools.partial(reduce_kernel, n_t),
        in_specs=[VMEM],
        out_specs=VMEM,
        out_shape=jax.ShapeDtypeStruct((trees, rows, wide), f32),
        scratch_shapes=[
            pltpu.VMEM((chips, rows, wide), bf16),
            pltpu.VMEM((chips - 1, rows, wide), bf16),
            pltpu.VMEM((chips - 1, rows, wide), bf16),
            dma((chips - 1,)), dma((chips - 1,)), dma((chips,)), dma((chips,)),
        ],
        compiler_params=pltpu.CompilerParams(collective_id=3, has_side_effects=True),
        name="reduce_tree",
    )(x)
def qkv_kernel(x_ref, w_ref, cos_ref, sin_ref, mq_ref, mk_ref, q_ref, k_ref, v_ref, kt_ref, vt_ref):
    x = x_ref[...]
    heads = q_ref.shape[0]
    cosine, sine = cos_ref[...], sin_ref[...]
    mq, mk = mq_ref[...], mk_ref[...]
    lane = lane_of(cosine.shape)
    low = lax.rem(lane, HEAD_DIM) < HEAD_DIM // 2
    first = lane < HEAD_DIM
    mv = jnp.where((lane >= HEAD_DIM) & (lane < HEAD_DIM + 3), 1.0, 0.0)
    tail = jnp.where(row_of((VROWS - HEAD_DIM, x.shape[0])) == 0, 1.0, 0.0).astype(bf16)

    def both(slab):
        return slab, pltpu.roll(slab, HEAD_DIM, 1)

    def rotate(slab):
        partner = jnp.where(
            low, pltpu.roll(slab, LANES - HEAD_DIM // 2, 1), pltpu.roll(slab, HEAD_DIM // 2, 1)
        )
        return slab * cosine + partner * sine

    q_all, k_all, v_all = (dot(x, w_ref[i]) for i in range(3))
    for h in range(0, heads, 2):
        cols = slice(h * HEAD_DIM, (h + 2) * HEAD_DIM)
        for g, slab in enumerate(both(rotate(q_all[:, cols]) * HEAD_DIM**-0.5)):
            q_ref[h + g] = jnp.where(first, slab, mq).astype(bf16)
        keys = rotate(k_all[:, cols])
        for g, slab in enumerate(both(keys)):
            k_ref[h + g] = jnp.where(first, slab, mk).astype(bf16)
        flat = keys.T.astype(bf16)
        for g, slab in enumerate(both(v_all[:, cols])):
            v_ref[h + g] = jnp.where(first, slab, mv).astype(bf16)
        flat_v = v_all[:, cols].T.astype(bf16)
        for g in range(2):
            part = slice(g * HEAD_DIM, (g + 1) * HEAD_DIM)
            kt_ref[h + g] = flat[part]
            vt_ref[h + g, :HEAD_DIM] = flat_v[part]
            vt_ref[h + g, HEAD_DIM:] = tail


def project(x, w, cosine, sine, mq, mk):
    rows, wide = x.shape
    heads = w.shape[2] // HEAD_DIM
    table = pl.BlockSpec((BLOCK, LANES), lambda i: (i, 0))
    slab = pl.BlockSpec((heads, BLOCK, LANES), lambda i: (0, i, 0))
    shape = jax.ShapeDtypeStruct((heads, rows, LANES), bf16)
    return pl.pallas_call(
        qkv_kernel,
        grid=(rows // BLOCK,),
        in_specs=[
            pl.BlockSpec((BLOCK, wide), lambda i: (i, 0)),
            pl.BlockSpec(w.shape, lambda i: (0, 0, 0)),
            table, table, table, table,
        ],
        out_specs=[
            slab, slab, slab,
            pl.BlockSpec((heads, HEAD_DIM, BLOCK), lambda i: (0, 0, i)),
            pl.BlockSpec((heads, VROWS, BLOCK), lambda i: (0, 0, i)),
        ],
        out_shape=[
            shape, shape, shape,
            jax.ShapeDtypeStruct((heads, HEAD_DIM, rows), bf16),
            jax.ShapeDtypeStruct((heads, VROWS, rows), bf16),
        ],
        name="project",
    )(x, w, cosine, sine, mq, mk)


def fwd_kernel(q_ref, k_ref, vt_ref, o_ref, qb_ref):
    qi = pl.program_id(1)
    heads = q_ref.shape[0]
    row, col = row_of((BLOCK, BLOCK)), lane_of((BLOCK, BLOCK))
    qs = [q_ref[h] for h in range(heads)]

    def scores(h, j):
        return dot(k_ref[h, span(j, BLOCK), :], qs[h], NT)

    state = []
    for h in range(heads):
        s = jnp.where(row <= col, scores(h, qi), masked_score)
        m = jnp.max(s, axis=0, keepdims=True)
        p = jnp.exp(s - m)
        state.append((m, dot(vt_ref[h, :, span(qi, BLOCK)], p.astype(bf16))))

    def step(j, carry):
        out = []
        for h in range(heads):
            m, acc = carry[h]
            s = scores(h, j)
            top = jnp.maximum(m, jnp.max(s, axis=0, keepdims=True))
            p = jnp.exp(s - top)
            acc = acc * jnp.exp(m - top) + dot(vt_ref[h, :, span(j, BLOCK)], p.astype(bf16))
            out.append((top, acc))
        return tuple(out)

    state = lax.fori_loop(0, qi, step, tuple(state))
    r = row_of((LANES, BLOCK))
    for h in range(0, heads, 2):
        outs = []
        for g in (h, h + 1):
            m, acc = state[g]
            total = acc[HEAD_DIM : HEAD_DIM + 1]
            outs.append(acc[:HEAD_DIM] / total)
            a, b, c = split3(-(m + jnp.log(total)))
            extra = jnp.where(r == 80, a, jnp.where(r == 81, b, jnp.where(r == 82, c, 0.0))).T
            qb_ref[g] = qs[g] + extra.astype(bf16)
        o_ref[:, h * HEAD_DIM : (h + 2) * HEAD_DIM] = jnp.concatenate(outs, axis=0).T.astype(bf16)


def attend(q, k, vt):
    heads, rows, _ = q.shape
    together = min(4, heads)
    slab = pl.BlockSpec((together, rows, LANES), lambda h, i: (h, 0, 0))
    block = pl.BlockSpec((together, BLOCK, LANES), lambda h, i: (h, i, 0))
    return pl.pallas_call(
        fwd_kernel,
        grid=(heads // together, rows // BLOCK),
        in_specs=[block, slab, pl.BlockSpec((together, VROWS, rows), lambda h, i: (h, 0, 0))],
        out_specs=[pl.BlockSpec((BLOCK, together * HEAD_DIM), lambda h, i: (i, h)), block],
        out_shape=[
            jax.ShapeDtypeStruct((rows, heads * HEAD_DIM), bf16),
            jax.ShapeDtypeStruct(q.shape, bf16),
        ],
        name="attend",
    )(q, k, vt)


def bwd_kernel(q_ref, k_ref, v_ref, kt_ref, d_ref, o_ref, cos_ref, sin_ref, m_ref, sums, wide):
    j = pl.program_id(0)
    heads, rows, _ = q_ref.shape
    nq = rows // BLOCK
    row, col = row_of((BLOCK, BLOCK)), lane_of((BLOCK, BLOCK))
    lane = lane_of((BLOCK, LANES))
    first = lane < HEAD_DIM

    @pl.when(j == 0)
    def _():
        sums[...] = jnp.zeros_like(sums)

        def widen(i, _):
            at = span(i, BLOCK)
            for h in range(0, heads, 2):
                cols = slice(h * HEAD_DIM, (h + 2) * HEAD_DIM)
                slab = d_ref[at, cols].astype(f32)
                prod = slab * o_ref[at, cols].astype(f32)
                for g, (s, mine) in enumerate(((slab, first), (pltpu.roll(slab, HEAD_DIM, 1), ~first))):
                    inner = -jnp.sum(jnp.where(mine, prod, 0.0), axis=1, keepdims=True)
                    a, b, c = split3(inner)
                    n = HEAD_DIM
                    tail = jnp.where(lane == n, a, jnp.where(lane == n + 1, b, jnp.where(lane == n + 2, c, 0.0)))
                    wide[h + g, at, :] = jnp.where(first, s, tail).astype(bf16)
            return 0

        lax.fori_loop(0, nq, widen, 0)

    ks = [k_ref[h] for h in range(heads)]
    vs = [v_ref[h] for h in range(heads)]
    kts = [kt_ref[h] for h in range(heads)]

    def pair(h, i, mask):
        at = span(i, BLOCK)
        q = q_ref[h, at, :]
        d = wide[h, at, :]
        s = dot(ks[h], q, NT)
        if mask:
            s = jnp.where(row <= col, s, masked_score)
        p = jnp.exp(s)
        back = (p * dot(vs[h], d, NT)).astype(bf16)
        sums[h, :, at] += dot(kts[h], back)
        return dot(back, q), dot(p.astype(bf16), d)

    def step(i, carry):
        out = []
        for h in range(heads):
            dk, dv = pair(h, i, False)
            out.append((carry[h][0] + dk, carry[h][1] + dv))
        return tuple(out)

    state = tuple(pair(h, j, True) for h in range(heads))
    state = lax.fori_loop(j + 1, nq, step, state)

    def join(a, b):
        return jnp.where(first, a, pltpu.roll(b, HEAD_DIM, 1))

    cosine, sine = cos_ref[...], sin_ref[...]
    low = lax.rem(lane, HEAD_DIM) < HEAD_DIM // 2

    def unrotate(slab):
        partner = jnp.where(
            low, pltpu.roll(slab, LANES - HEAD_DIM // 2, 1), pltpu.roll(slab, HEAD_DIM // 2, 1)
        )
        return slab * cosine - partner * sine

    at = span(j, BLOCK)
    total = heads * HEAD_DIM
    for h in range(0, heads, 2):
        dq = jnp.concatenate([sums[h, :, at], sums[h + 1, :, at]], axis=0).T * HEAD_DIM**-0.5
        dk = join(state[h][0], state[h + 1][0])
        dv = join(state[h][1], state[h + 1][1])
        for n, part in enumerate((unrotate(dq), unrotate(dk), dv)):
            begin = n * total + h * HEAD_DIM
            m_ref[:, begin : begin + 2 * HEAD_DIM] = part.astype(bf16)


def attend_back(q, k, v, kt, d, o, cosine, sine):
    heads, rows, _ = q.shape
    whole = lambda a: pl.BlockSpec(a.shape, lambda j: (0,) * a.ndim)
    block = pl.BlockSpec((heads, BLOCK, LANES), lambda j: (0, j, 0))
    table = pl.BlockSpec((BLOCK, LANES), lambda j: (j, 0))
    return pl.pallas_call(
        bwd_kernel,
        grid=(rows // BLOCK,),
        in_specs=[
            whole(q), block, block,
            pl.BlockSpec((heads, HEAD_DIM, BLOCK), lambda j: (0, 0, j)),
            whole(d), whole(o), table, table,
        ],
        out_specs=pl.BlockSpec((BLOCK, 3 * heads * HEAD_DIM), lambda j: (j, 0)),
        out_shape=jax.ShapeDtypeStruct((rows, 3 * heads * HEAD_DIM), bf16),
        scratch_shapes=[
            pltpu.VMEM((heads, HEAD_DIM, rows), f32),
            pltpu.VMEM((heads, rows, LANES), bf16),
        ],
        name="attend_back",
    )(q, k, v, kt, d, o, cosine, sine)


def ln_parts(v):
    centered = v - jnp.mean(v, axis=-1, keepdims=True)
    r = lax.rsqrt(jnp.mean(centered * centered, axis=-1, keepdims=True) + norm_eps)
    return centered * r, r


def ln_back(e, n, r, gain):
    f = e * gain
    return r * (f - jnp.mean(f, axis=-1, keepdims=True) - n * jnp.mean(f * n, axis=-1, keepdims=True))


def feed_kernel(
    att_ref, x_ref, cot_ref, ow_ref, par_ref, up_ref, down_ref,
    out_ref, hid_ref, ba_ref, upg_ref, downg_ref, outg_ref, vec_ref,
    hidden, branch, acc, feed_in, back_feed, active, slope,
):
    phase, n = pl.program_id(0), pl.program_id(1)
    last = pl.num_programs(1) - 1
    par = lambda i: par_ref[i : i + 1]
    total = lambda v: jnp.sum(v, axis=0, keepdims=True)

    @pl.when((phase == 0) & (n == 0))
    def _():
        b = dot(att_ref[...], ow_ref[...])
        branch[...] = b
        h = x_ref[...].astype(f32) + ln_parts(b)[0] * par(0) + par(1)
        hidden[...] = h
        feed_in[...] = (ln_parts(h)[0] * par(2) + par(3)).astype(bf16)
        acc[...] = jnp.zeros_like(acc)

    up = up_ref[...].reshape(feed_in.shape[1], -1)
    down = down_ref[...].reshape(-1, feed_in.shape[1])

    @pl.when(phase == 0)
    def _():
        u = dot(feed_in[...], up)
        t = jnp.tanh(0.7978845608028654 * (u + 0.044715 * u * u * u))
        half = 0.5 * (1.0 + t)
        a = (u * half).astype(bf16)
        active[n] = a
        slope[n] = half + 0.5 * u * (1.0 - t * t) * (
            0.7978845608028654 * (1.0 + 3 * 0.044715 * u * u)
        )
        acc[...] += dot(a, down)

    @pl.when((phase == 1) & (n == 0))
    def _():
        e = cot_ref[...].astype(f32)
        norm, r = ln_parts(acc[...])
        out_ref[...] = (hidden[...] + norm * par(4) + par(5)).astype(bf16)
        vec_ref[4:5] = total(e * norm)
        vec_ref[5:6] = total(e)
        back_feed[...] = ln_back(e, norm, r, par(4)).astype(bf16)
        acc[...] = jnp.zeros_like(acc)

    @pl.when(phase == 1)
    def _():
        b = back_feed[...]
        upper = (dot(b, down, NT) * slope[n]).astype(bf16)
        acc[...] += dot(upper, up, NT)
        downg_ref[0] = dot(active[n], b, TN).astype(bf16)
        upg_ref[0] = dot(feed_in[...], upper, TN).astype(bf16)

    @pl.when((phase == 1) & (n == last))
    def _():
        e = acc[...]
        norm, r = ln_parts(hidden[...])
        vec_ref[2:3] = total(e * norm)
        vec_ref[3:4] = total(e)
        h = cot_ref[...].astype(f32) + ln_back(e, norm, r, par(2))
        hid_ref[...] = h
        norm, r = ln_parts(branch[...])
        vec_ref[0:1] = total(h * norm)
        vec_ref[1:2] = total(h)
        b = ln_back(h, norm, r, par(0)).astype(bf16)
        ba_ref[...] = dot(b, ow_ref[...], NT).astype(bf16)
        outg_ref[...] = dot(att_ref[...], b, TN).astype(bf16)


def feed(att, x, cot, ow, par, up, down):
    rows, wide = att.shape
    n_d, n_t, _, width = up.shape
    one = lambda a: pl.BlockSpec(a.shape, lambda p, n: (0,) * len(a.shape), pipeline_mode=pl.Buffered(1))
    sds = jax.ShapeDtypeStruct
    outs = [
        sds((rows, wide), bf16), sds((rows, wide), f32), sds((rows, wide), bf16),
        sds((n_t, wide, width), bf16), sds((n_t, width, wide), bf16), sds((wide, wide), bf16),
        sds((8, wide), f32),
    ]
    chunk = lambda a: pl.BlockSpec((1,) + a.shape[1:], lambda p, n: (p * n, 0, 0))
    weight = lambda a: pl.BlockSpec((a.shape[0], 1) + a.shape[2:], lambda p, n: (0, n, 0, 0))
    return pl.pallas_call(
        feed_kernel,
        grid=(2, n_t),
        in_specs=[one(a) for a in (att, x, cot, ow, par)] + [weight(up), weight(down)],
        out_specs=[one(o) for o in outs[:3]] + [chunk(outs[3]), chunk(outs[4])] + [one(o) for o in outs[5:]],
        out_shape=outs,
        scratch_shapes=[
            pltpu.VMEM((rows, wide), f32), pltpu.VMEM((rows, wide), f32), pltpu.VMEM((rows, wide), f32),
            pltpu.VMEM((rows, wide), bf16), pltpu.VMEM((rows, wide), bf16),
            pltpu.VMEM((n_t, rows, width), bf16), pltpu.VMEM((n_t, rows, width), f32),
        ],
        compiler_params=pltpu.CompilerParams(vmem_limit_bytes=64 << 20),
        name="feed",
    )(att, x, cot, ow, par, up, down)
def shards(
    n_d, n_t,
    tokens, cotangent, lengths, parents, first_gain, first_shift, in_weight, out_weight,
    second_gain, second_shift, third_gain, third_shift, up_weight, down_weight, fourth_gain, fourth_shift,
):
    trees, rows, wide = tokens.shape
    group = n_t // trees
    d, t = lax.axis_index("dp"), lax.axis_index("tensor")
    tree = t // group
    width = out_weight.shape[0]

    def part(w):
        return lax.dynamic_slice_in_dim(w, d * (w.shape[0] // n_d), w.shape[0] // n_d, 0)

    def everyone(w):
        full = lax.all_gather(part(w), ("dp", "tensor"), axis=0, tiled=False)
        return full.reshape((n_d, n_t) + full.shape[1:])

    out_all, up_all, down_all = everyone(out_weight), everyone(up_weight), everyone(down_weight)
    out_all = out_all.transpose(1, 0, 2, 3).reshape(-1, wide)

    mine = lambda a: lax.dynamic_index_in_dim(a, tree, 0, keepdims=False)
    cosine, sine, mq, mk = tables(mine(lengths), mine(parents), n_t * rows)

    x = tokens.astype(f32)
    normed, first_back = jax.vjp(layer_norm, x, first_gain, first_shift)
    gathered, w = gather_tree(n_d, n_t, normed.astype(bf16), in_weight.transpose(1, 0, 2))
    w = w.transpose(1, 2, 0, 3).reshape(3, wide, -1)
    q, k, v, kt, vt = project(gathered, w, cosine, sine, mq, mk)
    attended, qb = attend(q, k, vt)
    att = exchange_heads(n_t, trees, attended, False)
    par = jnp.stack(
        [second_gain, second_shift, third_gain, third_shift, fourth_gain, fourth_shift, first_gain, first_shift]
    )
    flat = lambda a: a.reshape(trees * rows, a.shape[-1])
    output, back_hidden, back_att, up_g, down_g, out_g, vec = feed(
        flat(att), flat(tokens), flat(cotangent), out_all, par, up_all, down_all
    )
    d_heads = exchange_heads(n_t, trees, back_att.reshape(trees, rows, wide), True)
    back_mixed = attend_back(qb, k, v, kt, d_heads, attended, cosine, sine)
    w_flat = w.transpose(1, 0, 2).reshape(wide, -1)
    partial = lax.dot_general(back_mixed, w_flat, NT, preferred_element_type=f32).astype(bf16)
    in_part = lax.dot_general(gathered, back_mixed, TN, preferred_element_type=f32)
    back_normed = reduce_tree(n_t, trees, partial)
    back_x, first_gain_back, first_shift_back = first_back(back_normed)
    back_tokens = (back_hidden.reshape(x.shape) + back_x).astype(bf16)

    in_part = in_part.astype(bf16).reshape(wide, 3, trees, width).transpose(2, 0, 1, 3)
    own = lax.rem(t, group) * trees
    spread = jnp.zeros((n_t, wide, 3, width), bf16)
    spread = lax.dynamic_update_slice(spread, in_part, (own, 0, 0, 0))

    def collect(g):
        mine = lax.psum_scatter(g, "tensor", scatter_dimension=0, tiled=False)
        return lax.psum(mine, "dp").astype(f32)

    vec = jnp.concatenate([vec[:6], first_gain_back[None], first_shift_back[None]])
    vec = lax.psum(vec, ("dp", "tensor"))
    return (
        output.reshape(tokens.shape),
        back_tokens,
        vec[6], vec[7],
        collect(spread),
        collect(out_g.reshape(n_t, width, wide)),
        vec[0], vec[1], vec[2], vec[3],
        collect(up_g),
        collect(down_g),
        vec[4], vec[5],
    )


def solution(mesh):
    in_specs = (
        P("dp", "tensor", None), P("dp", "tensor", None), P("dp", None), P("dp", None),
        P(), P(), P(None, None, "tensor"), P("tensor", None), P(), P(), P(), P(),
        P(None, "tensor"), P("tensor", None), P(), P(),
    )
    out_specs = (
        P("dp", "tensor", None), P("dp", "tensor", None), P(), P(), P(None, None, "tensor"),
        P("tensor", None), P(), P(), P(), P(), P(None, "tensor"), P("tensor", None), P(), P(),
    )
    run = functools.partial(shards, mesh.shape["dp"], mesh.shape["tensor"])
    return jax.shard_map(run, mesh=mesh, in_specs=in_specs, out_specs=out_specs, check_vma=False)
```

time: 1790 us -> 803 us (0.45)
  waiting for transfers between devices: 994 us -> 332 us
  matrix products: 464 us -> 13.6 us
  Pallas kernels: 0 us -> 346 us
  other arithmetic: 127 us -> 24.3 us
  local copies, waits for them, and re-layouts: 114 us -> 21.4 us
  loops' own time: 31.6 us -> 0 us
    dot_general x80 -> x2, matrix products: 464 us -> 13.6 us  [the longest x1 6.96 us: shards(): lax.dot_general(back_mixed, w_flat, NT, preferred_element_type=f32)]
    pallas_call x0 -> x8, Pallas kernels: none -> 346 us  [the longest x2 65.9 us: exchange_heads(): pl.pallas_call(functools.partial(heads_kernel, n_t, trees, back), in_spec...]
    reduce_scatter x8 -> x4, waiting for transfers between devices: 586 us -> 257 us  [collect(): mine = lax.psum_scatter(g, 'tensor', scatter_dimension=0, tiled=False)]
    all_gather x8 -> x3, waiting for transfers between devices: 361 us -> 73.2 us  [everyone(): full = lax.all_gather(part(w), ('dp', 'tensor'), axis=0, tiled=False)]
    dynamic_update_slice x16 -> x1, local copies, waits for them, and re-layouts: 51.2 us -> 1.25 us  [shards(): spread = lax.dynamic_update_slice(spread, in_part, (own, 0, 0, 0))]
    psum x1, waiting for transfers between devices: 46.4 us -> 0.01 us  [collect(): return lax.psum(mine, 'dp').astype(f32)]
    while x331 -> x0, local copies, waits for them, and re-layouts: 36.8 us -> none
    another operation x5 -> x0, loops' own time: 31.6 us -> none  [the longest x2 21.9 us: attend_back(): lax.scan(one_block, (empty, empty), jnp.arange(TREE // QBLOCK, dtype=jnp....]
  transfers between devices with their start and end apart: 17 -> 8, of which waited for: 17 -> 4; matrix products, arithmetic and copies ran while one was open for 2% -> 6% of each run, Pallas kernels for 0% -> 37%
where the time goes in v1:
time: 803 us
  Pallas kernels  346 us (43%)
  waiting for transfers between devices  332 us (41%)
  blocking collectives  50.6 us (6%)
  other arithmetic  24.3 us (3%)
  local copies, waits for them, and re-layouts  21.4 us (3%)
  between operations  14.6 us (2%)
  matrix products  13.6 us (2%)
    reduce_scatter x4, waiting for transfers between devices, collect(): mine = lax.psum_scatter(g, 'tensor', scatter_dimension=0, tiled=False)  257 us
    all_gather x3, waiting for transfers between devices, everyone(): full = lax.all_gather(part(w), ('dp', 'tensor'), axis=0, tiled=False)  73.2 us
    pallas_call x2, Pallas kernels, exchange_heads(): pl.pallas_call(functools.partial(heads_kernel, n_t, trees, back), in_spec...  65.9 us
    pallas_call x1, Pallas kernels, attend_back(): pl.pallas_call(bwd_kernel, grid=(rows // BLOCK,), in_specs=[whole(q), blo...  60.8 us
    pallas_call x1, Pallas kernels, gather_tree(): pl.pallas_call(functools.partial(gather_kernel, n_d, n_t), in_specs=[VMEM...  60.5 us
    pallas_call x1, Pallas kernels, feed(): pl.pallas_call(feed_kernel, grid=(2, n_t), in_specs=[one(a) for a in (att...  52.3 us
    psum x1, blocking collectives, shards(): vec = lax.psum(vec, ('dp', 'tensor'))  50.6 us
    pallas_call x1, Pallas kernels, attend(): pl.pallas_call(fwd_kernel, grid=(heads // together, rows // BLOCK), in_sp...  50.2 us
  transfers between devices with their start and end apart: 8, of which 4 were waited for; matrix products, arithmetic and copies ran while one was open for 6% of the time, Pallas kernels for 37%

profile of v1, /device:TPU:0, one launch (start us, length us, event | category | flops | bytes accessed | tf_op | source)
XLA Modules:
  0.0 802.5 jit_solution(8948505869522345469)
XLA Ops:
  7.3 1.5 constant_dynamic-slice_fusion.2
  8.9 1.7 constant_dynamic-slice_fusion.1
  10.6 1.7 constant_dynamic-slice_fusion
  14.6 1.4 fusion.7.x_ref
  16.0 60.5 %gather_tree.1 = (bf16[2048,1024]{1,0:T(8,128)(2,1)}, bf16[2,3,1024,128]{3,2,1,0:T(8,128)(2,1)}) custom-call(bf16[2,256,1024]{2,1,0:T(8,128)(2,1)} %fusion.7.x_ref, bf16[3,1024,128]{2,1,0:T(8,128)(2,1)} %bitcast.77), custom_call_target="tpu_custom_call" | custom-call | tf_op jit(solution)/shard_map/gather_tree/pallas_call | solution.py:184
  77.0 3.3 fusion.26
  80.4 5.5 fusion.11
  85.9 2.6 fusion.16
  88.5 12.7 %project.1 = (bf16[4,2048,128]{2,1,0:T(8,128)(2,1)}, bf16[4,2048,128]{2,1,0:T(8,128)(2,1)}, bf16[4,2048,128]{2,1,0:T(8,128)(2,1)}, bf16[4,64,2048]{2,1,0:T(8,128)(2,1)}, bf16[4,80,2048]{2,1,0:T(8,128)(2,1)}) custom-call(bf16[2048,1024]{1,0:T(8,128)(2,1)} %get-tuple-element.30.x_ref, bf16[3,1024,256]{2,1,0:T(8,128)(2,1)} %get-tuple-element.58.w_ref, ...), custom_call_target="tpu_custom_call" | custom-call | tf_op jit(solution)/shard_map/project/pallas_call | solution.py:332
  101.2 50.2 %attend.1 = (bf16[2048,256]{1,0:T(8,128)(2,1)}, bf16[4,2048,128]{2,1,0:T(8,128)(2,1)}) custom-call(bf16[4,2048,128]{2,1,0:T(8,128)(2,1)} %get-tuple-element.32.q_ref, bf16[4,2048,128]{2,1,0:T(8,128)(2,1)} %get-tuple-element.33.k_ref, bf16[4,80,2048]{2,1,0:T(8,128)(2,1)} %get-tuple-element.34.vt_ref), custom_call_target="tpu_custom_call" | custom-call | tf_op jit(solution)/shard_map/attend/pallas_call | solution.py:400
  151.5 35.1 %heads_out.1 = bf16[2,256,1024]{2,1,0:T(8,128)(2,1)} custom-call(bf16[2048,256]{1,0:T(8,128)(2,1)} %get-tuple-element.35.x_ref.o_ref), custom_call_target="tpu_custom_call" | custom-call | tf_op jit(solution)/shard_map/heads_out/pallas_call | solution.py:229
  187.4 3.2 copy.38
  190.5 73.2 %all-gather.11.cloned.1.call-done = bf16[4096,1024]{1,0:T(8,128)(2,1)} async-done(((bf16[128,1024]{1,0:T(8,128)(2,1)}), bf16[4096,1024]{1,0:T(8,128)(2,1)}) %all-gather.11.cloned.1.call-update) | async-done | bytes 8388624 | tf_op jit(solution)/shard_map/all_gather | solution.py:633
  263.7 52.3 %feed.1 = (bf16[512,1024]{1,0:T(8,128)(2,1)}, f32[512,1024]{1,0:T(8,128)}, bf16[512,1024]{1,0:T(8,128)(2,1)}, bf16[8,1024,512]{2,1,0:T(8,128)(2,1)}, bf16[8,512,...) custom-call(bf16[512,1024]{1,0:T(8,128)(2,1)} %bitcast.67, bf16[512,1024]{1,0:T(8,128)(2,1)} %bitcast.63, ...), custom_call_target="tpu_custom_call" | custom-call | tf_op jit(solution)/shard_map/feed/pallas_call | solution.py:604
  316.1 30.8 %heads_back.1.d_ref = bf16[2048,256]{1,0:T(8,128)(2,1)} custom-call(bf16[2,256,1024]{2,1,0:T(8,128)(2,1)} %bitcast.75), custom_call_target="tpu_custom_call" | custom-call | tf_op jit(solution)/shard_map/heads_back/pallas_call | solution.py:229
  346.9 60.8 %attend_back.1 = bf16[2048,768]{1,0:T(8,128)(2,1)} custom-call(bf16[4,2048,128]{2,1,0:T(8,128)(2,1)} %get-tuple-element.38.q_ref, bf16[4,2048,128]{2,1,0:T(8,128)(2,1)} %get-tuple-element.33.k_ref, bf16[4,2048,128]{2,1,0:T(8,128)(2,1)} %get-tuple-element.39.v_ref, bf16[4,64,2048]{2,1,0:T(8,128)(2,1)} %get-tuple-element.40.kt_ref, ...), custom_call_target="tpu_custom_call" | custom-call | tf_op jit(solution)/shard_map/attend_back/pallas_call | solution.py:495
  407.7 6.6 convolution_convert_fusion.1
  415.3 4.0 broadcast_in_dim.74
  419.3 1.3 bitcast_dynamic-update-slice_fusion
  422.0 76.7 %reduce-scatter.5.cloned.1.call-done = bf16[1,1024,3,128]{3,1,2,0:T(8,128)(2,1)} async-done(((bf16[8,1024,3,128]{3,1,2,0:T(8,128)(2,1)}), bf16[1,1024,3,128]{3,1,2,0:T(8,128)(2,1)}) %reduce-scatter.5.cloned.1.call-update) | async-done | bytes 786448 | tf_op jit(solution)/shard_map/reduce_scatter | solution.py:671
  498.7 90.2 %reduce-scatter.9.cloned.1.call-done = bf16[1,1024,512]{2,1,0:T(8,128)(2,1)} async-done(((bf16[8,1024,512]{2,1,0:T(8,128)(2,1)}), bf16[1,1024,512]{2,1,0:T(8,128)(2,1)}) %reduce-scatter.9.cloned.1.call-update) | async-done | bytes 1048592 | tf_op jit(solution)/shard_map/reduce_scatter | solution.py:671
  588.9 90.3 %reduce-scatter.11.cloned.1.call-done = bf16[1,512,1024]{2,1,0:T(8,128)(2,1)} async-done(((bf16[8,512,1024]{2,1,0:T(8,128)(2,1)}), bf16[1,512,1024]{2,1,0:T(8,128)(2,1)}) %reduce-scatter.11.cloned.1.call-update) | async-done | bytes 1048592 | tf_op jit(solution)/shard_map/reduce_scatter | solution.py:671
  679.2 1.1 copy.39
  680.3 7.0 convolution_convert_fusion.x_ref
  687.3 43.5 %reduce_tree.1 = f32[2,256,1024]{2,1,0:T(8,128)} custom-call(bf16[2048,1024]{1,0:T(8,128)(2,1)} %convolution_convert_fusion.x_ref), custom_call_target="tpu_custom_call" | custom-call | tf_op jit(solution)/shard_map/reduce_tree/pallas_call | solution.py:273
  730.9 2.4 fusion.10
  733.4 1.1 fusion.8
  734.5 50.6 %psum.35 = f32[8,1024]{1,0:T(8,128)S(1)} all-reduce(f32[8,1024]{1,0:T(8,128)S(1)} %pad_maximum_fusion), channel_id=1, replica_groups=mesh['dp'=4,'tensor'=8] {'dp','tensor'}, use_global_device_ids=true, to_apply=%region_12.13 | all-reduce | flops 8192 | bytes 65536 | tf_op jit(solution)/shard_map/psum | solution.py:675
  785.8 3.3 add_convert_fusion
  789.1 2.9 convert_element_type.56
  792.0 1.6 convert_element_type.57
  793.6 1.2 convert_element_type.54
  (91 shorter events, 7.6 us)
Async XLA Ops:
  7.2 6.2 copy-start
  7.2 7.4 copy-start.7
  7.2 7.4 copy-start.16
  7.2 180.1 %all-gather.7.cloned.1.call-start = ((), (), s32[]{:S(2)}) async-start(), calls=%async_computation.8 | async-start | bytes 2162688 | tf_op jit(solution)/shard_map/all_gather | solution.py:633
  8.8 181.7 %all-gather.9.cloned.1.call-start = ((), (), s32[]{:S(2)}) async-start(), calls=%async_computation.9 | async-start | bytes 8650752 | tf_op jit(solution)/shard_map/all_gather | solution.py:633
  10.6 253.1 %all-gather.11.cloned.1.call-start = ((), (), s32[]{:S(2)}) async-start(), calls=%async_computation.10 | async-start | bytes 8650752 | tf_op jit(solution)/shard_map/all_gather | solution.py:633
  12.3 409.6 %reduce-scatter.7.cloned.1.call-start = ((), (), s32[]{:S(2)}) async-start(), calls=%async_computation.5 | async-start | bytes 2359296 | tf_op jit(solution)/shard_map/reduce_scatter | solution.py:671
  13.6 2.5 copy-start.9
  14.0 0.6 copy-start.14
  14.6 62.0 %copy-start.23 = (s32[2,13]{1,0:T(2,128)S(1)}, s32[2,13]{1,0:T(2,128)}, u32[]{:S(2)}) copy-start(s32[2,13]{1,0:T(2,128)} %param.19) | copy-start | bytes 316
  14.6 1.4 copy-start.12
  151.4 35.2 %copy-start.17 = (f32[1024]{0:T(1024)S(1)}, f32[1024]{0:T(1024)}, u32[]{:S(2)}) copy-start(f32[1024]{0:T(1024)} %param.24) | copy-start | bytes 12292
  151.4 35.2 %copy-start.18 = (f32[1024]{0:T(1024)S(1)}, f32[1024]{0:T(1024)}, u32[]{:S(2)}) copy-start(f32[1024]{0:T(1024)} %param.25) | copy-start | bytes 12292
  151.4 35.2 %copy-start.19 = (f32[1024]{0:T(1024)S(1)}, f32[1024]{0:T(1024)}, u32[]{:S(2)}) copy-start(f32[1024]{0:T(1024)} %param.26) | copy-start | bytes 12292
  151.4 35.2 %copy-start.20 = (f32[1024]{0:T(1024)S(1)}, f32[1024]{0:T(1024)}, u32[]{:S(2)}) copy-start(f32[1024]{0:T(1024)} %param.27) | copy-start | bytes 12292
  151.5 35.2 %copy-start.21 = (f32[1024]{0:T(1024)S(1)}, f32[1024]{0:T(1024)}, u32[]{:S(2)}) copy-start(f32[1024]{0:T(1024)} %param.30) | copy-start | bytes 12292
  151.5 35.2 %copy-start.22 = (f32[1024]{0:T(1024)S(1)}, f32[1024]{0:T(1024)}, u32[]{:S(2)}) copy-start(f32[1024]{0:T(1024)} %param.31) | copy-start | bytes 12292
  316.0 182.6 %reduce-scatter.5.cloned.1.call-start = ((), (), s32[]{:S(2)}) async-start(), calls=%async_computation.4 | async-start | bytes 7077888 | tf_op jit(solution)/shard_map/reduce_scatter | solution.py:671
  420.6 168.3 %reduce-scatter.9.cloned.1.call-start = ((), (), s32[]{:S(2)}) async-start(), calls=%async_computation.6 | async-start | bytes 9437184 | tf_op jit(solution)/shard_map/reduce_scatter | solution.py:671
  421.1 258.0 %reduce-scatter.11.cloned.1.call-start = ((), (), s32[]{:S(2)}) async-start(), calls=%async_computation.7 | async-start | bytes 9437184 | tf_op jit(solution)/shard_map/reduce_scatter | solution.py:671
  421.9 257.3 %copy-start.3 = (bf16[1024,3,256]{2,0,1:T(8,128)(2,1)S(1)}, bf16[1024,3,256]{2,0,1:T(8,128)(2,1)}, u32[]{:S(2)}) copy-start(bf16[1024,3,256]{2,0,1:T(8,128)(2,1)} %get-tuple-element.57) | copy-start | bytes 4718596
  421.9 367.2 %all-reduce.3.cloned.1.call-start = ((), (), s32[]{:S(2)}) async-start(), calls=%async_computation.11 | async-start | bytes 6291456 | tf_op jit(solution)/shard_map/psum | solution.py:672
  687.3 43.5 %copy-start.1 = (bf16[2,256,1024]{2,1,0:T(8,128)(2,1)S(1)}, bf16[2,256,1024]{2,1,0:T(8,128)(2,1)}, u32[]{:S(2)}) copy-start(bf16[2,256,1024]{2,1,0:T(8,128)(2,1)} %param.16) | copy-start | bytes 3145732
  687.3 43.5 %copy-start.8 = (f32[1024]{0:T(1024)S(1)}, f32[1024]{0:T(1024)}, u32[]{:S(2)}) copy-start(f32[1024]{0:T(1024)} %param.20) | copy-start | bytes 12292
  687.3 43.5 %copy-start.10 = (f32[2,256]{1,0:T(2,128)S(1)}, f32[2,256]{1,0:T(2,128)}, u32[]{:S(2)}) copy-start(f32[2,256]{1,0:T(2,128)} %copy-done.9) | copy-start | bytes 6148
  730.8 2.5 copy-start.15
  730.9 2.6 copy-start.2
  730.9 2.6 copy-start.13
  733.3 1.2 copy-start.11
  789.1 2.9 copy-start.4
  792.0 1.6 copy-start.5
  792.0 2.8 copy-start.6
Sparse Core Ops, SparseCore 0:
  11.0 82.2 all-gather.6
  96.9 89.4 all-gather.8
  189.4 74.2 all-gather.10
  316.2 49.4 reduce-scatter.6
  420.7 77.9 reduce-scatter.4
  500.8 87.9 reduce-scatter.8
  591.2 87.9 reduce-scatter.10
  682.5 86.0 all-reduce.2

commit v2 on v1

--- a/solution.py
+++ b/solution.py
@@ -237,53 +237,6 @@
     )(x)
 
 
-def reduce_kernel(n_t, x_ref, o_ref, side, out, land, ss, rs, sb, rb):
-    d, t = lax.axis_index("dp"), lax.axis_index("tensor")
-    trees, rows, _ = o_ref.shape
-    chips = n_t // 2
-    near = chips // trees
-    chip, core = t // 2, lax.rem(t, 2)
-    other = 2 * chip + 1 - core
-    line = [lax.rem(chip + k, chips) for k in range(1, chips)]
-    barrier([(d, other)] + [(d, 2 * c + core) for c in line])
-    pairs = []
-    for k, c in enumerate(line + [chip]):
-        theirs = x_ref.at[span(2 * c + 1 - core, rows), :]
-        pairs.append(send(theirs, side.at[k], sb.at[k], rb.at[k], (d, other)))
-    copies = []
-    for k, c in enumerate(line):
-        pairs[k].wait_recv()
-        out[k] = (x_ref[span(2 * c + core, rows), :].astype(f32) + side[k].astype(f32)).astype(bf16)
-        copies.append(send(out.at[k], land.at[k], ss.at[k], rs.at[k], (d, 2 * c + core)))
-    pairs[chips - 1].wait_recv()
-    o_ref[...] = jnp.zeros_like(o_ref)
-    o_ref[chip // near] = x_ref[span(t, rows), :].astype(f32) + side[chips - 1].astype(f32)
-    for k in range(chips - 1):
-        copies[k].wait_recv()
-        source = lax.rem(chip + chips - 1 - k, chips)
-        o_ref[source // near] += land[k].astype(f32)
-    for copy in pairs + copies:
-        copy.wait_send()
-
-
-def reduce_tree(n_t, trees, x):
-    rows, wide = x.shape[0] // n_t, x.shape[1]
-    chips = n_t // 2
-    dma = pltpu.SemaphoreType.DMA
-    return pl.pallas_call(
-        functools.partial(reduce_kernel, n_t),
-        in_specs=[VMEM],
-        out_specs=VMEM,
-        out_shape=jax.ShapeDtypeStruct((trees, rows, wide), f32),
-        scratch_shapes=[
-            pltpu.VMEM((chips, rows, wide), bf16),
-            pltpu.VMEM((chips - 1, rows, wide), bf16),
-            pltpu.VMEM((chips - 1, rows, wide), bf16),
-            dma((chips - 1,)), dma((chips - 1,)), dma((chips,)), dma((chips,)),
-        ],
-        compiler_params=pltpu.CompilerParams(collective_id=3, has_side_effects=True),
-        name="reduce_tree",
-    )(x)
 def qkv_kernel(x_ref, w_ref, cos_ref, sin_ref, mq_ref, mk_ref, q_ref, k_ref, v_ref, kt_ref, vt_ref):
     x = x_ref[...]
     heads = q_ref.shape[0]
@@ -615,6 +568,315 @@
         compiler_params=pltpu.CompilerParams(vmem_limit_bytes=64 << 20),
         name="feed",
     )(att, x, cot, ow, par, up, down)
+def add_rows(target, source, step=64):
+    rows = target.shape[0]
+    step = min(step, rows)
+    while rows % step:
+        step //= 2
+
+    def body(i, _):
+        at = span(i, step)
+        target[at, :] = target[at, :] + source[at, :]
+        return 0
+
+    lax.fori_loop(0, rows // step, body, 0)
+
+
+def orders(n_d):
+    bits = n_d.bit_length() - 1
+    return [list(range(bits)), list(range(bits - 1, -1, -1))]
+
+
+def combos(bits):
+    masks = [0]
+    for b in bits:
+        masks = masks + [m ^ (1 << b) for m in masks]
+    return masks
+
+
+def finish_kernel(
+    n_d, n_t, sum_ref, x_ref, hid_ref, par_ref, vec_in, up_ref, down_ref, og_ref, ig_ref,
+    bt_ref, vec_ref, up_out, down_out, og_out, ig_out,
+    mine_up, mine_down, mine_og, mine_ig, side_up, side_down, side_og,
+    hop_up, hop_down, hop_og, hop_ig, far_up, far_down, far_og, far_ig,
+    full_up, full_down, full_og, full_ig,
+    r_side, r_out, r_land, vec_now, vec_got, vec_far,
+    s_load, s_side, r_sides, s_hop, r_hop, s_far, r_far, s_all, r_all, s_own, r_own,
+    s_red, r_red, s_redside, r_redside, s_vec, r_vec,
+):
+    d, t = lax.axis_index("dp"), lax.axis_index("tensor")
+    trees, rows, wide = x_ref.shape
+    chips = n_t // 2
+    near = chips // trees
+    group = n_t // trees
+    chip, core = t // 2, lax.rem(t, 2)
+    other = 2 * chip + 1 - core
+    line = [lax.rem(chip + k, chips) for k in range(1, chips)]
+    dest = line + [chip]
+    peers = [lax.rem(d + k, n_d) for k in range(1, n_d)]
+    bits = n_d.bit_length() - 1
+    barrier([(d, lax.rem(t + k, n_t)) for k in range(1, n_t)] + [(p, t) for p in peers])
+
+    red_pairs = []
+    for k, c in enumerate(dest):
+        theirs = sum_ref.at[span(2 * c + 1 - core, rows), :]
+        red_pairs.append(send(theirs, r_side.at[k], s_redside.at[k], r_redside.at[k], (d, other)))
+
+    items = [
+        (up_ref, mine_up, side_up, hop_up, far_up, full_up, up_out),
+        (down_ref, mine_down, side_down, hop_down, far_down, full_down, down_out),
+        (og_ref, mine_og, side_og, hop_og, far_og, full_og, og_out),
+        (ig_ref, mine_ig, None, hop_ig, far_ig, full_ig, ig_out),
+    ]
+    units = [(n, k) for k in range(chips) for n in range(3)]
+    units = units[:3] + [(3, i) for i in range(trees)] + units[3:]
+    number = {u: i for i, u in enumerate(units)}
+    loads, sides = {}, {}
+    for u in units:
+        n, k = u
+        source, mine, side = items[n][:3]
+        i = number[u]
+        if n < 3:
+            sides[u] = send(source.at[2 * dest[k] + 1 - core], side.at[k], s_side.at[i], r_sides.at[i], (d, other))
+            loads[u] = pltpu.make_async_copy(source.at[2 * dest[k] + core], mine.at[k], s_load.at[i])
+        else:
+            loads[u] = pltpu.make_async_copy(source.at[k], mine.at[k], s_load.at[i])
+        loads[u].start()
+
+    red_copies = []
+    for k, c in enumerate(line):
+        red_pairs[k].wait_recv()
+        r_out[k] = sum_ref[span(2 * c + core, rows), :] + r_side[k]
+        red_copies.append(send(r_out.at[k], r_land.at[k], s_red.at[k], r_red.at[k], (d, 2 * c + core)))
+
+    hops = {}
+
+    def cut(n, k, part, stream):
+        mine = items[n][1]
+        height, width = mine.shape[1] // n_d, mine.shape[2] // (2 if n < 3 else 1)
+        return mine.at[k, span(part, height), pl.ds(stream * width, width)]
+
+    def streams(n, k):
+        return orders(n_d) if n < 3 else [orders(n_d)[k % 2]]
+
+    def begin(u):
+        n, k = u
+        loads[u].wait()
+        if n < 3:
+            sides[u].wait_recv()
+            add_rows(items[n][1].at[k], items[n][2].at[k])
+        hop(u, 0)
+
+    def hop(u, step):
+        n, k = u
+        slot = 0 if step == 0 else n_d - (n_d >> step)
+        for stream, order in enumerate(streams(n, k)):
+            partner = lax.bitwise_xor(d, 1 << order[step])
+            for j, m in enumerate(combos(order[step + 1 :])):
+                i = (slot + j) * 2 + stream
+                hops[u, step, stream, j] = send(
+                    cut(n, k, lax.bitwise_xor(partner, m), stream),
+                    items[n][3].at[k, i],
+                    s_hop.at[number[u], i],
+                    r_hop.at[number[u], i],
+                    (partner, t),
+                )
+
+    def land(u, step):
+        n, k = u
+        slot = 0 if step == 0 else n_d - (n_d >> step)
+        for stream, order in enumerate(streams(n, k)):
+            for j, m in enumerate(combos(order[step + 1 :])):
+                i = (slot + j) * 2 + stream
+                hops[u, step, stream, j].wait_recv()
+                add_rows(cut(n, k, lax.bitwise_xor(d, m), stream), items[n][3].at[k, i])
+        if step + 1 < bits:
+            hop(u, step + 1)
+        else:
+            away(u)
+
+    fars = {}
+
+    def piece(n, k):
+        mine = items[n][1]
+        return mine.at[k, span(d, mine.shape[1] // n_d), :]
+
+    def owner(i):
+        return lax.rem(t, group) * trees + i
+
+    def away(u):
+        n, k = u
+        far = items[n][4]
+        if n < 3:
+            if k < chips - 1:
+                fars[u] = send(piece(n, k), far.at[k], s_far.at[n, k], r_far.at[n, k], (d, 2 * dest[k] + core))
+        else:
+            here = t // group
+
+            @pl.when(owner(k) != t)
+            def _():
+                send(piece(n, k), far.at[here], s_own.at[k], r_own.at[here], (d, owner(k)))
+
+            @pl.when(owner(k) == t)
+            def _():
+                far[here] = piece(n, k)[...]
+
+    def reduced():
+        red_pairs[chips - 1].wait_recv()
+        back = [None] * trees
+        own = sum_ref[span(t, rows), :].astype(f32) + r_side[chips - 1].astype(f32)
+        hit = chip // near
+        x = x_ref[...].astype(f32)
+        for k in range(chips - 1):
+            red_copies[k].wait_recv()
+        for tree in range(trees):
+            e = jnp.where(hit == tree, own, 0.0)
+            for k in range(chips - 1):
+                source = lax.rem(chip + chips - 1 - k, chips)
+                e = e + jnp.where(source // near == tree, r_land[k].astype(f32), 0.0)
+            norm, r = ln_parts(x[tree])
+            g, b = jnp.sum(e * norm, axis=0, keepdims=True), jnp.sum(e, axis=0, keepdims=True)
+            bt_ref[tree] = (hid_ref[tree] + ln_back(e, norm, r, par_ref[6:7])).astype(bf16)
+            back[tree] = (g, b)
+        vec_now[0:6] = vec_in[0:6]
+        vec_now[6:7] = sum(g for g, _ in back)
+        vec_now[7:8] = sum(b for _, b in back)
+
+    vec_partners = [(d, other)] + [(lax.bitwise_xor(d, 1 << b), t) for b in range(bits)]
+    vec_copies = []
+
+    def vec_step(i):
+        if i > 0:
+            vec_copies[i - 1].wait()
+            vec_now[...] = vec_now[...] + vec_got[i - 1]
+        if i < len(vec_partners):
+            vec_got[len(vec_partners) + i] = vec_now[...]
+            vec_copies.append(
+                send(vec_got.at[len(vec_partners) + i], vec_got.at[i], s_vec.at[i], r_vec.at[i], vec_partners[i])
+            )
+        else:
+            vec_far[chip] = vec_now[...]
+            for k, c in enumerate(line):
+                n = len(vec_partners) + k
+                vec_copies.append(
+                    send(vec_far.at[chip], vec_far.at[chip], s_vec.at[n], r_vec.at[n], (d, 2 * c + core))
+                )
+
+    count = len(units)
+    vec_at = count - 1 - len(vec_partners)
+    for i in range(count + bits):
+        if i < count:
+            begin(units[i])
+        for step in range(bits):
+            if 0 <= i - 1 - step < count:
+                land(units[i - 1 - step], step)
+        if i == vec_at - 1:
+            reduced()
+        if vec_at <= i <= vec_at + len(vec_partners):
+            vec_step(i - vec_at)
+
+    spreads = []
+    for n in range(4):
+        source, mine, side, hops_ref, far, full, out = items[n]
+        height = full.shape[0] // n_d
+        if n < 3:
+            for k in range(chips - 1):
+                fars[n, k].wait_recv()
+            total = mine[chips - 1, span(d, height), :].astype(f32)
+            for k in range(chips - 1):
+                total = total + far[k].astype(f32)
+        else:
+            for j in range(trees):
+                giver = j * group + t // trees
+
+                @pl.when(giver != t)
+                def _():
+                    pltpu.make_async_remote_copy(
+                        src_ref=far.at[j], dst_ref=far.at[j], send_sem=s_own.at[0], recv_sem=r_own.at[j],
+                        device_id=(d, giver), device_id_type=MESH,
+                    ).wait_recv()
+
+            total = far[0].astype(f32)
+            for j in range(1, trees):
+                total = total + far[j].astype(f32)
+        at = span(d, height)
+        full[at, :] = total.astype(bf16)
+        for j, p in enumerate(peers):
+            spreads.append(send(full.at[at, :], full.at[at, :], s_all.at[n, j], r_all.at[n, j], (p, t)))
+    for k in range(chips - 1):
+        vec_copies[len(vec_partners) + k].wait()
+    total = vec_far[0]
+    for c in range(1, chips):
+        total = total + vec_far[c]
+    vec_ref[...] = total
+    for n in range(4):
+        full, out = items[n][5:7]
+        for j in range(n_d - 1):
+            spreads[n * (n_d - 1) + j].wait_recv()
+
+        height = 64
+        while full.shape[0] % height:
+            height //= 2
+
+        def widen(i, _):
+            out[span(i, height), :] = full[span(i, height), :].astype(f32)
+            return 0
+
+        lax.fori_loop(0, full.shape[0] // height, widen, 0)
+
+    for k in range(trees):
+
+        @pl.when(owner(k) != t)
+        def _():
+            pltpu.make_async_remote_copy(
+                src_ref=piece(3, k), dst_ref=piece(3, k), send_sem=s_own.at[k], recv_sem=r_own.at[0],
+                device_id=(d, owner(k)), device_id_type=MESH,
+            ).wait_send()
+
+    for copy in red_pairs + red_copies + list(sides.values()) + list(hops.values()) + list(fars.values()) + spreads:
+        copy.wait_send()
+
+
+def finish(n_d, n_t, partial, x, hidden, par, vec, up_g, down_g, out_g, in_g):
+    trees, rows, wide = x.shape
+    chips = n_t // 2
+    bits = n_d.bit_length() - 1
+    dma = pltpu.SemaphoreType.DMA
+    sds = jax.ShapeDtypeStruct
+    any_ = pl.BlockSpec(memory_space=pl.ANY)
+    shapes = [a.shape[1:] for a in (up_g, down_g, out_g, in_g)]
+    counts = [chips] * 3 + [trees]
+    vm = lambda lead, shape, kind=bf16: pltpu.VMEM(tuple(lead) + tuple(shape), kind)
+    mine = [vm((c,), s) for c, s in zip(counts, shapes)]
+    side = [vm((c,), s) for c, s in zip(counts[:3], shapes[:3])]
+    slots = 2 * (n_d - 1)
+    hop = [vm((c, slots), (s[0] // n_d, s[1] // 2)) for c, s in zip(counts[:3], shapes[:3])]
+    hop.append(vm((trees, slots), (shapes[3][0] // n_d, shapes[3][1])))
+    far = [vm((c,), (s[0] // n_d, s[1])) for c, s in zip([chips - 1] * 3 + [trees], shapes)]
+    full = [vm((), s) for s in shapes]
+    n_units = 3 * chips + trees
+    partners = 1 + bits
+    return pl.pallas_call(
+        functools.partial(finish_kernel, n_d, n_t),
+        in_specs=[VMEM] * 5 + [any_] * 4,
+        out_specs=[VMEM] * 6,
+        out_shape=[sds(x.shape, bf16), sds((8, wide), f32)] + [sds(s, f32) for s in shapes],
+        scratch_shapes=mine + side + hop + far + full + [
+            vm((chips, rows), (wide,)), vm((chips - 1, rows), (wide,)), vm((chips - 1, rows), (wide,)),
+            vm((8,), (wide,), f32), vm((2 * partners, 8), (wide,), f32), vm((chips, 8), (wide,), f32),
+            dma((n_units,)), dma((n_units,)), dma((n_units,)),
+            dma((n_units, slots)), dma((n_units, slots)),
+            dma((3, chips - 1)), dma((3, chips - 1)),
+            dma((4, n_d - 1)), dma((4, n_d - 1)),
+            dma((trees,)), dma((trees,)),
+            dma((chips - 1,)), dma((chips - 1,)), dma((chips,)), dma((chips,)),
+            dma((partners + chips - 1,)), dma((partners + chips - 1,)),
+        ],
+        compiler_params=pltpu.CompilerParams(
+            collective_id=3, has_side_effects=True, vmem_limit_bytes=67043328
+        ),
+        name="finish",
+    )(partial, x, hidden, par, vec, up_g, down_g, out_g, in_g)
 def shards(
     n_d, n_t,
     tokens, cotangent, lengths, parents, first_gain, first_shift, in_weight, out_weight,
@@ -640,7 +902,7 @@
     cosine, sine, mq, mk = tables(mine(lengths), mine(parents), n_t * rows)
 
     x = tokens.astype(f32)
-    normed, first_back = jax.vjp(layer_norm, x, first_gain, first_shift)
+    normed = layer_norm(x, first_gain, first_shift)
     gathered, w = gather_tree(n_d, n_t, normed.astype(bf16), in_weight.transpose(1, 0, 2))
     w = w.transpose(1, 2, 0, 3).reshape(3, wide, -1)
     q, k, v, kt, vt = project(gathered, w, cosine, sine, mq, mk)
@@ -658,30 +920,20 @@
     w_flat = w.transpose(1, 0, 2).reshape(wide, -1)
     partial = lax.dot_general(back_mixed, w_flat, NT, preferred_element_type=f32).astype(bf16)
     in_part = lax.dot_general(gathered, back_mixed, TN, preferred_element_type=f32)
-    back_normed = reduce_tree(n_t, trees, partial)
-    back_x, first_gain_back, first_shift_back = first_back(back_normed)
-    back_tokens = (back_hidden.reshape(x.shape) + back_x).astype(bf16)
-
-    in_part = in_part.astype(bf16).reshape(wide, 3, trees, width).transpose(2, 0, 1, 3)
-    own = lax.rem(t, group) * trees
-    spread = jnp.zeros((n_t, wide, 3, width), bf16)
-    spread = lax.dynamic_update_slice(spread, in_part, (own, 0, 0, 0))
-
-    def collect(g):
-        mine = lax.psum_scatter(g, "tensor", scatter_dimension=0, tiled=False)
-        return lax.psum(mine, "dp").astype(f32)
-
-    vec = jnp.concatenate([vec[:6], first_gain_back[None], first_shift_back[None]])
-    vec = lax.psum(vec, ("dp", "tensor"))
+    in_part = in_part.astype(bf16).reshape(wide, 3, trees, width).transpose(2, 1, 0, 3)
+    back_tokens, vec, up_sum, down_sum, out_sum, in_sum = finish(
+        n_d, n_t, partial, tokens, back_hidden.reshape(x.shape), par, vec,
+        up_g, down_g, out_g.reshape(n_t, width, wide), in_part.reshape(trees, 3 * wide, width),
+    )
     return (
         output.reshape(tokens.shape),
         back_tokens,
         vec[6], vec[7],
-        collect(spread),
-        collect(out_g.reshape(n_t, width, wide)),
+        in_sum.reshape(3, wide, width).transpose(1, 0, 2),
+        out_sum,
         vec[0], vec[1], vec[2], vec[3],
-        collect(up_g),
-        collect(down_g),
+        up_sum,
+        down_sum,
         vec[4], vec[5],
     )
 

time: 803 us -> 574 us (0.71)
  waiting for transfers between devices: 332 us -> 64.7 us
  Pallas kernels: 346 us -> 445 us
  blocking collectives: 50.6 us -> 0 us
  other arithmetic: 24.3 us -> 11 us
    reduce_scatter x4 -> x0, waiting for transfers between devices: 257 us -> none  [collect(): mine = lax.psum_scatter(g, 'tensor', scatter_dimension=0, tiled=False)]
    pallas_call x1, Pallas kernels: 43.5 us -> 153 us  [finish(): pl.pallas_call(functools.partial(finish_kernel, n_d, n_t), in_specs=[VMEM...]
    psum x1 -> x0, blocking collectives: 50.6 us -> none  [shards(): vec = lax.psum(vec, ('dp', 'tensor'))]
    pallas_call x2, Pallas kernels: 65.9 us -> 56 us  [exchange_heads(): pl.pallas_call(functools.partial(heads_kernel, n_t, trees, back), in_spec...]
    convert_element_type x5 -> x0, other arithmetic: 9.85 us -> none  [the longest x4 6.58 us: collect(): return lax.psum(mine, 'dp').astype(f32)]
    all_gather x3, waiting for transfers between devices: 73.2 us -> 64.6 us  [everyone(): full = lax.all_gather(part(w), ('dp', 'tensor'), axis=0, tiled=False)]
  transfers between devices with their start and end apart: 8 -> 3, of which waited for: 4 -> 1; matrix products, arithmetic and copies ran while one was open for 6% -> 4% of each run, Pallas kernels for 37% -> 28%
where the time goes in v2:
time: 574 us; the launch traced here: 572 us
  Pallas kernels  445 us (78%)
  waiting for transfers between devices  64.7 us (11%)
  local copies, waits for them, and re-layouts  25.5 us (4%)
  between operations  14 us (2%)
  matrix products  11.7 us (2%)
  other arithmetic  11 us (2%)
    pallas_call x1, Pallas kernels, finish(): pl.pallas_call(functools.partial(finish_kernel, n_d, n_t), in_specs=[VMEM...  153 us
    all_gather x3, waiting for transfers between devices, everyone(): full = lax.all_gather(part(w), ('dp', 'tensor'), axis=0, tiled=False)  64.6 us
    pallas_call x1, Pallas kernels, attend_back(): pl.pallas_call(bwd_kernel, grid=(rows // BLOCK,), in_specs=[whole(q), blo...  60.8 us
    pallas_call x1, Pallas kernels, gather_tree(): pl.pallas_call(functools.partial(gather_kernel, n_d, n_t), in_specs=[VMEM...  60.4 us
    pallas_call x2, Pallas kernels, exchange_heads(): pl.pallas_call(functools.partial(heads_kernel, n_t, trees, back), in_spec...  56 us
    pallas_call x1, Pallas kernels, feed(): pl.pallas_call(feed_kernel, grid=(2, n_t), in_specs=[one(a) for a in (att...  52.3 us
    pallas_call x1, Pallas kernels, attend(): pl.pallas_call(fwd_kernel, grid=(heads // together, rows // BLOCK), in_sp...  50.3 us
    pallas_call x1, Pallas kernels, project(): pl.pallas_call(qkv_kernel, grid=(rows // BLOCK,), in_specs=[pl.BlockSpec(...  12.7 us
  transfers between devices with their start and end apart: 3, of which 1 were waited for; matrix products, arithmetic and copies ran while one was open for 4% of the time, Pallas kernels for 28%

profile of v2, /device:TPU:0, one launch (start us, length us, event | category | flops | bytes accessed | tf_op | source)
XLA Modules:
  0.0 572.4 jit_solution(8737843675906274023)
XLA Ops:
  7.3 1.5 constant_dynamic-slice_fusion.2
  8.9 1.7 constant_dynamic-slice_fusion.1
  10.6 1.7 constant_dynamic-slice_fusion
  12.3 0.7 fusion.12
  13.5 0.4 fusion.2
  14.0 1.4 fusion.5.x_ref
  15.4 60.4 %gather_tree.1 = (bf16[2048,1024]{1,0:T(8,128)(2,1)}, bf16[2,3,1024,128]{3,2,1,0:T(8,128)(2,1)}) custom-call(bf16[2,256,1024]{2,1,0:T(8,128)(2,1)} %fusion.5.x_ref, bf16[3,1024,128]{2,1,0:T(8,128)(2,1)} %bitcast.74), custom_call_target="tpu_custom_call" | custom-call | tf_op jit(solution)/shard_map/gather_tree/pallas_call | solution.py:184
  75.8 2.8 fusion.19
  78.6 1.7 copy.39
  80.8 5.6 fusion.6
  86.4 2.6 fusion.11
  89.0 12.7 %project.1 = (bf16[4,2048,128]{2,1,0:T(8,128)(2,1)}, bf16[4,2048,128]{2,1,0:T(8,128)(2,1)}, bf16[4,2048,128]{2,1,0:T(8,128)(2,1)}, bf16[4,64,2048]{2,1,0:T(8,128)(2,1)}, bf16[4,80,2048]{2,1,0:T(8,128)(2,1)}) custom-call(bf16[2048,1024]{1,0:T(8,128)(2,1)} %get-tuple-element.36.x_ref, bf16[3,1024,256]{2,1,0:T(8,128)(2,1)} %get-tuple-element.63.w_ref, ...), custom_call_target="tpu_custom_call" | custom-call | tf_op jit(solution)/shard_map/project/pallas_call | solution.py:285
  101.7 50.3 %attend.1 = (bf16[2048,256]{1,0:T(8,128)(2,1)}, bf16[4,2048,128]{2,1,0:T(8,128)(2,1)}) custom-call(bf16[4,2048,128]{2,1,0:T(8,128)(2,1)} %get-tuple-element.38.q_ref, bf16[4,2048,128]{2,1,0:T(8,128)(2,1)} %get-tuple-element.39.k_ref, bf16[4,80,2048]{2,1,0:T(8,128)(2,1)} %get-tuple-element.40.vt_ref), custom_call_target="tpu_custom_call" | custom-call | tf_op jit(solution)/shard_map/attend/pallas_call | solution.py:353
  152.0 34.3 %heads_out.1 = bf16[2,256,1024]{2,1,0:T(8,128)(2,1)} custom-call(bf16[2048,256]{1,0:T(8,128)(2,1)} %get-tuple-element.41.x_ref.o_ref), custom_call_target="tpu_custom_call" | custom-call | tf_op jit(solution)/shard_map/heads_out/pallas_call | solution.py:229
  186.4 0.7 stack.35.par_ref
  187.1 3.2 copy.38
  190.3 64.6 %all-gather.11.cloned.1.call-done = bf16[4096,1024]{1,0:T(8,128)(2,1)} async-done(((bf16[128,1024]{1,0:T(8,128)(2,1)}), bf16[4096,1024]{1,0:T(8,128)(2,1)}) %all-gather.11.cloned.1.call-update) | async-done | bytes 8388624 | tf_op jit(solution)/shard_map/all_gather | solution.py:895
  254.9 52.3 %feed.1 = (bf16[512,1024]{1,0:T(8,128)(2,1)}, f32[512,1024]{1,0:T(8,128)}, bf16[512,1024]{1,0:T(8,128)(2,1)}, bf16[8,1024,512]{2,1,0:T(8,128)(2,1)}, bf16[8,512,...) custom-call(bf16[512,1024]{1,0:T(8,128)(2,1)} %bitcast.65, bf16[512,1024]{1,0:T(8,128)(2,1)} %bitcast.60, ...), custom_call_target="tpu_custom_call" | custom-call | tf_op jit(solution)/shard_map/feed/pallas_call | solution.py:557
  307.2 21.7 %heads_back.1.d_ref = bf16[2048,256]{1,0:T(8,128)(2,1)} custom-call(bf16[2,256,1024]{2,1,0:T(8,128)(2,1)} %bitcast.72), custom_call_target="tpu_custom_call" | custom-call | tf_op jit(solution)/shard_map/heads_back/pallas_call | solution.py:229
  328.9 60.8 %attend_back.1 = bf16[2048,768]{1,0:T(8,128)(2,1)} custom-call(bf16[4,2048,128]{2,1,0:T(8,128)(2,1)} %get-tuple-element.43.q_ref, bf16[4,2048,128]{2,1,0:T(8,128)(2,1)} %get-tuple-element.39.k_ref, bf16[4,2048,128]{2,1,0:T(8,128)(2,1)} %get-tuple-element.44.v_ref, bf16[4,64,2048]{2,1,0:T(8,128)(2,1)} %get-tuple-element.45.kt_ref, ...), custom_call_target="tpu_custom_call" | custom-call | tf_op jit(solution)/shard_map/attend_back/pallas_call | solution.py:448
  389.6 6.8 %convolution_convert_fusion.1 = bf16[1024,768]{0,1:T(8,128)(2,1)S(1)} fusion(bf16[2048,1024]{1,0:T(8,128)(2,1)} %get-tuple-element.36.x_ref, bf16[2048,768]{1,0:T(8,128)(2,1)} %attend_back.1), kind=kOutput, calls=%fused_computation.9 | convolution fusion | flops 3222011904 | bytes 8912896 | tf_op jit(solution)/shard_map/dot_general | solution.py:922
  396.4 4.9 convolution_convert_fusion.sum_ref
  401.4 1.6 copy.40
  402.9 152.9 %finish.1 = (bf16[2,256,1024]{2,1,0:T(8,128)(2,1)}, f32[8,1024]{1,0:T(8,128)}, f32[1024,512]{1,0:T(8,128)}, f32[512,1024]{1,0:T(8,128)}, f32[128,1024]{1,0:T(8,128)}, /*index=5*/f32[3072,128]{1,0:T(8,128)}) custom-call(bf16[2048,1024]{1,0:T(8,128)(2,1)} %convolution_convert_fusion.sum_ref, bf16[2,256,1024]{2,1,0:T(8,128)(2,1)} %x_ref.1, ...), custom_call_target="tpu_custom_call" | custom-call | tf_op jit(solution)/shard_map/finish/pallas_call | solution.py:859
  555.9 1.8 fusion.20
  557.6 2.3 copy.50
  559.9 1.1 copy.51
  561.0 0.2 copy-done.6
  561.3 0.8 copy.52
  562.2 1.3 copy.53
  563.6 1.0 copy-done.2
  564.6 1.3 copy.54
  (52 shorter events, 1.4 us)
Async XLA Ops:
  7.2 6.1 %copy-start = (bf16[2,256,1024]{2,1,0:T(8,128)(2,1)S(1)}, bf16[2,256,1024]{2,1,0:T(8,128)(2,1)}, u32[]{:S(2)}) copy-start(bf16[2,256,1024]{2,1,0:T(8,128)(2,1)} %x_ref.1) | copy-start | bytes 3145732
  7.2 6.8 %copy-start.7 = (f32[1024]{0:T(1024)S(1)}, f32[1024]{0:T(1024)}, u32[]{:S(2)}) copy-start(f32[1024]{0:T(1024)} %param.21) | copy-start | bytes 12292
  7.2 6.8 %copy-start.8 = (f32[1024]{0:T(1024)S(1)}, f32[1024]{0:T(1024)}, u32[]{:S(2)}) copy-start(f32[1024]{0:T(1024)} %param.20) | copy-start | bytes 12292
  7.2 179.9 %all-gather.7.cloned.1.call-start = ((), (), s32[]{:S(2)}) async-start(), calls=%async_computation | async-start | bytes 2162688 | tf_op jit(solution)/shard_map/all_gather | solution.py:895
  8.8 181.4 %all-gather.9.cloned.1.call-start = ((), (), s32[]{:S(2)}) async-start(), calls=%async_computation.1 | async-start | bytes 8650752 | tf_op jit(solution)/shard_map/all_gather | solution.py:895
  10.6 244.3 %all-gather.11.cloned.1.call-start = ((), (), s32[]{:S(2)}) async-start(), calls=%async_computation.2 | async-start | bytes 8650752 | tf_op jit(solution)/shard_map/all_gather | solution.py:895
  78.6 1.7 copy-start.15
  152.0 34.4 %copy-start.9 = (f32[1024]{0:T(1024)S(1)}, f32[1024]{0:T(1024)}, u32[]{:S(2)}) copy-start(f32[1024]{0:T(1024)} %param.24) | copy-start | bytes 12292
  152.0 34.4 %copy-start.10 = (f32[1024]{0:T(1024)S(1)}, f32[1024]{0:T(1024)}, u32[]{:S(2)}) copy-start(f32[1024]{0:T(1024)} %param.25) | copy-start | bytes 12292
  152.0 34.4 %copy-start.11 = (f32[1024]{0:T(1024)S(1)}, f32[1024]{0:T(1024)}, u32[]{:S(2)}) copy-start(f32[1024]{0:T(1024)} %param.26) | copy-start | bytes 12292
  152.0 34.4 %copy-start.12 = (f32[1024]{0:T(1024)S(1)}, f32[1024]{0:T(1024)}, u32[]{:S(2)}) copy-start(f32[1024]{0:T(1024)} %param.27) | copy-start | bytes 12292
  152.0 34.4 %copy-start.13 = (f32[1024]{0:T(1024)S(1)}, f32[1024]{0:T(1024)}, u32[]{:S(2)}) copy-start(f32[1024]{0:T(1024)} %param.30) | copy-start | bytes 12292
  152.0 34.4 %copy-start.14 = (f32[1024]{0:T(1024)S(1)}, f32[1024]{0:T(1024)}, u32[]{:S(2)}) copy-start(f32[1024]{0:T(1024)} %param.31) | copy-start | bytes 12292
  389.6 6.8 %copy-start.1 = (bf16[2048,768]{1,0:T(8,128)(2,1)S(1)}, bf16[2048,768]{1,0:T(8,128)(2,1)}, u32[]{:S(2)}) copy-start(bf16[2048,768]{1,0:T(8,128)(2,1)} %attend_back.1) | copy-start | bytes 9437188
  389.6 6.8 %copy-start.4 = (bf16[1024,3,256]{0,2,1:T(8,128)(2,1)S(1)}, bf16[1024,3,256]{0,2,1:T(8,128)(2,1)}, u32[]{:S(2)}) copy-start(bf16[1024,3,256]{0,2,1:T(8,128)(2,1)} %copy.39) | copy-start | bytes 4718596
  555.9 4.0 copy-start.5
  559.9 1.4 copy-start.6
  559.9 2.3 copy-start.3
  562.2 2.3 copy-start.2
Sparse Core Ops, SparseCore 0:
  11.0 81.6 all-gather.6
  96.2 79.6 all-gather.8
  179.0 75.8 all-gather.10

commit v3 on v2

--- a/solution.py
+++ b/solution.py
@@ -22,6 +22,7 @@
 TN = (((0,), (0,)), ((), ()))
 MESH = pl.DeviceIdType.MESH
 VMEM = pl.BlockSpec(memory_space=pltpu.VMEM)
+HBM = pl.BlockSpec(memory_space=pltpu.HBM)
 
 
 def dot(a, b, dims=NN):
@@ -108,7 +109,154 @@
     return copy
 
 
-def gather_kernel(n_d, n_t, x_ref, w_ref, o_ref, u_ref, rs, ss, rb, sb, rw, sw, rp, sp):
+def orders(n_d):
+    bits = n_d.bit_length() - 1
+    return [list(range(bits)), list(range(bits - 1, -1, -1))]
+
+
+def combos(bits):
+    masks = [0]
+    for b in bits:
+        masks = masks + [m ^ (1 << b) for m in masks]
+    return masks
+
+
+class Spread:
+    def __init__(self, n_d, n_t, shards, alls, sems):
+        self.n_d, self.n_t, self.shards, self.alls = n_d, n_t, shards, alls
+        self.zs, self.zr, self.ps, self.pr, self.ys, self.yr, self.own = sems
+        self.d, self.t = lax.axis_index("dp"), lax.axis_index("tensor")
+        self.chips = n_t // 2
+        self.chip, self.core = self.t // 2, lax.rem(self.t, 2)
+        self.other = 2 * self.chip + 1 - self.core
+        self.bits = n_d.bit_length() - 1
+        self.arrays = range(len(shards))
+
+    @staticmethod
+    def sems(count, n_d, n_t):
+        dma = pltpu.SemaphoreType.DMA
+        hops, slots = n_t // 2 - 1, 2 * (n_d - 1)
+        z, p, y = (count, 2 * hops), (count, 2 * hops, slots), (count, 2 * hops + 1)
+        return [dma(z), dma(z), dma(p), dma(p), dma(y), dma(y), dma((count,))]
+
+    def exists(self, c):
+        return (c >= 0) & (c < self.chips)
+
+    def rows(self, a):
+        return self.shards[a].shape[0] // self.n_d
+
+    def slot(self, way, h):
+        return h - 1 + (self.chips - 1 if way < 0 else 0)
+
+    def remote(self, src, dst, ssem, rsem, device):
+        return pltpu.make_async_remote_copy(
+            src_ref=src, dst_ref=dst, send_sem=ssem, recv_sem=rsem, device_id=device, device_id_type=MESH
+        )
+
+    def along(self, a, way, h, arriving):
+        source = self.chip - way * (h if arriving else h - 1)
+        at = span(self.d, self.rows(a))
+        dst = self.alls[a].at[2 * source + self.core, at]
+        src = self.shards[a].at[at] if h == 1 and not arriving else dst
+        peer = self.chip - way if arriving else self.chip + way
+        i = self.slot(way, h)
+        return self.remote(src, dst, self.zs.at[a, i], self.zr.at[a, i], (self.d, 2 * peer + self.core))
+
+    def across(self, a, way, h, step, arriving):
+        source = self.chip - way * h
+        q, half = self.rows(a), self.shards[a].shape[1] // 2
+        out = []
+        for stream, order in enumerate(orders(self.n_d)):
+            partner = lax.bitwise_xor(self.d, 1 << order[step])
+            for j, m in enumerate(combos(order[:step])):
+                block = lax.bitwise_xor(partner if arriving else self.d, m)
+                ref = self.alls[a].at[2 * source + self.core, span(block, q), pl.ds(stream * half, half)]
+                i = stream * (self.n_d - 1) + (1 << step) - 1 + j
+                k = self.slot(way, h)
+                out.append(self.remote(ref, ref, self.ps.at[a, k, i], self.pr.at[a, k, i], (partner, self.t)))
+        return out
+
+    def beside(self, a, way, h, arriving=False):
+        source = self.chip - way * h
+        ref = self.alls[a].at[2 * source + (1 - self.core if arriving else self.core)]
+        k = self.slot(way, h)
+        return self.remote(ref, ref, self.ys.at[a, k], self.yr.at[a, k], (self.d, self.other))
+
+    def mine(self, a, arriving=False):
+        k = 2 * (self.chips - 1)
+        dst = self.alls[a].at[self.other if arriving else self.t]
+        return self.remote(self.shards[a], dst, self.ys.at[a, k], self.yr.at[a, k], (self.d, self.other))
+
+    def keep(self, a):
+        return pltpu.make_async_copy(self.shards[a], self.alls[a].at[self.t], self.own.at[a])
+
+    def begin(self):
+        for way in (1, -1):
+
+            @pl.when(self.exists(self.chip + way))
+            def _():
+                for a in self.arrays:
+                    self.along(a, way, 1, False).start()
+
+        for a in self.arrays:
+            self.keep(a).start()
+            self.mine(a).start()
+
+    def phase(self, p, h):
+        for way in (1, -1):
+
+            @pl.when(self.exists(self.chip - way * h))
+            def _():
+                for a in self.arrays:
+                    if p == 0:
+                        self.along(a, way, h, True).wait_recv()
+                        if h < self.chips - 1:
+
+                            @pl.when(self.exists(self.chip + way))
+                            def _():
+                                self.along(a, way, h + 1, False).start()
+                    else:
+                        for copy in self.across(a, way, h, p - 1, True):
+                            copy.wait_recv()
+                    if p < self.bits:
+                        for copy in self.across(a, way, h, p, False):
+                            copy.start()
+                    else:
+                        self.beside(a, way, h).start()
+
+    def groups(self):
+        return self.chips - 1 + self.bits
+
+    def group(self, g):
+        for h in range(1, self.chips):
+            if 0 <= g - (h - 1) <= self.bits:
+                self.phase(g - (h - 1), h)
+
+    def end(self):
+        for h in range(1, self.chips):
+            for way in (1, -1):
+
+                @pl.when(self.exists(self.chip + way) & self.exists(self.chip - way * (h - 1)))
+                def _():
+                    for a in self.arrays:
+                        self.along(a, way, h, False).wait_send()
+
+                @pl.when(self.exists(self.chip - way * h))
+                def _():
+                    for a in self.arrays:
+                        for step in range(self.bits):
+                            for copy in self.across(a, way, h, step, False):
+                                copy.wait_send()
+                        self.beside(a, way, h).wait_send()
+                        self.beside(a, way, h, True).wait_recv()
+
+        for a in self.arrays:
+            self.keep(a).wait()
+            self.mine(a).wait_send()
+            self.mine(a, True).wait_recv()
+
+
+def gather_kernel(n_d, n_t, x_ref, w_ref, f_ref, o_ref, u_ref, all_ref, rs, ss, rb, sb, rw, sw, rp, sp, *sems):
     d, t = lax.axis_index("dp"), lax.axis_index("tensor")
     trees, rows, _ = x_ref.shape
     chips = n_t // 2
@@ -142,6 +290,8 @@
 
     for k, c in enumerate(line):
         copies.append(send(x_ref.at[c // near], block(chip, core), ss.at[k], rs.at[k], (d, 2 * c + core)))
+    weights = Spread(n_d, n_t, [f_ref], [all_ref], sems)
+    weights.begin()
     o_ref[span(t, rows), :] = x_ref[tree]
     copies.append(send(x_ref.at[tree], block(chip, core), sb.at[chips - 1], rb.at[chips - 1], (d, other)))
     for i in range(trees):
@@ -161,6 +311,9 @@
         source = lax.rem(chip + chips - 1 - k, chips)
         copies[k].wait_recv()
         copies.append(send(block(source, core), block(source, core), sb.at[k], rb.at[k], (d, other)))
+    for g in range(weights.groups()):
+        weights.group(g)
+    weights.end()
     for j in range(trees):
 
         @pl.when(owners[j] != t)
@@ -177,40 +330,36 @@
             copy.wait()
 
 
-def gather_tree(n_d, n_t, normed, weight):
+def gather_tree(n_d, n_t, normed, weight, down):
     trees, rows, wide = normed.shape
     chips = n_t // 2
     dma = pltpu.SemaphoreType.DMA
     return pl.pallas_call(
         functools.partial(gather_kernel, n_d, n_t),
-        in_specs=[VMEM] * 2,
-        out_specs=[VMEM] * 2,
+        in_specs=[VMEM] * 3,
+        out_specs=[VMEM] * 2 + [HBM],
         out_shape=[
             jax.ShapeDtypeStruct((n_t * rows, wide), bf16),
             jax.ShapeDtypeStruct((trees,) + weight.shape, bf16),
+            jax.ShapeDtypeStruct((n_t,) + down.shape, bf16),
         ],
         scratch_shapes=[
             dma((chips - 1,)), dma((chips - 1,)), dma((chips,)), dma((chips,)),
             dma((trees,)), dma((trees,)), dma((n_d - 1,)), dma((n_d - 1,)),
-        ],
+        ] + Spread.sems(1, n_d, n_t),
         compiler_params=pltpu.CompilerParams(collective_id=0, has_side_effects=True),
         name="gather_tree",
-    )(normed, weight)
-
-
-def heads_kernel(n_t, trees, back, x_ref, o_ref, ss, rs):
+    )(normed, weight, down)
+
+
+def heads_kernel(n_t, trees, x_ref, o_ref, ss, rs):
     d, t = lax.axis_index("dp"), lax.axis_index("tensor")
     group = n_t // trees
     others = [lax.rem(t + k, n_t) for k in range(1, n_t)]
     barrier([(d, o) for o in others])
-    if back:
-        rows, width = x_ref.shape[1], x_ref.shape[2] // group
-        cut = lambda o: x_ref.at[o // group, :, span(lax.rem(o, group), width)]
-        place = o_ref.at[span(t, rows), :]
-    else:
-        rows, width = o_ref.shape[1], x_ref.shape[1]
-        cut = lambda o: x_ref.at[span(o, rows), :]
-        place = o_ref.at[t // group, :, span(lax.rem(t, group), width)]
+    rows, width = x_ref.shape[1], x_ref.shape[2] // group
+    cut = lambda o: x_ref.at[o // group, :, span(lax.rem(o, group), width)]
+    place = o_ref.at[span(t, rows), :]
     copies = [
         send(cut(o), place, ss.at[k], rs.at[k], (d, o)) for k, o in enumerate(others)
     ]
@@ -219,21 +368,17 @@
         copy.wait()
 
 
-def exchange_heads(n_t, trees, x, back):
-    if back:
-        _, rows, wide = x.shape
-        shape = (n_t * rows, wide * trees // n_t)
-    else:
-        shape = (trees, x.shape[0] // n_t, x.shape[1] * (n_t // trees))
+def exchange_heads(n_t, trees, x):
+    _, rows, wide = x.shape
     dma = pltpu.SemaphoreType.DMA
     return pl.pallas_call(
-        functools.partial(heads_kernel, n_t, trees, back),
+        functools.partial(heads_kernel, n_t, trees),
         in_specs=[VMEM],
         out_specs=VMEM,
-        out_shape=jax.ShapeDtypeStruct(shape, bf16),
+        out_shape=jax.ShapeDtypeStruct((n_t * rows, wide * trees // n_t), bf16),
         scratch_shapes=[dma((n_t - 1,)), dma((n_t - 1,))],
-        compiler_params=pltpu.CompilerParams(collective_id=2 if back else 1, has_side_effects=True),
-        name="heads_back" if back else "heads_out",
+        compiler_params=pltpu.CompilerParams(collective_id=2, has_side_effects=True),
+        name="heads_back",
     )(x)
 
 
@@ -304,10 +449,42 @@
     )(x, w, cosine, sine, mq, mk)
 
 
-def fwd_kernel(q_ref, k_ref, vt_ref, o_ref, qb_ref):
-    qi = pl.program_id(1)
+def fwd_kernel(
+    n_d, n_t, trees, q_ref, k_ref, vt_ref, ow_ref, up_ref, o_ref, qb_ref, att_ref, ow_all, up_all,
+    kept, ss, rs, here, *sems,
+):
+    qi = pl.program_id(0)
+    steps = pl.num_programs(0)
     heads = q_ref.shape[0]
     row, col = row_of((BLOCK, BLOCK)), lane_of((BLOCK, BLOCK))
+    d, t = lax.axis_index("dp"), lax.axis_index("tensor")
+    group = n_t // trees
+    rows, width = att_ref.shape[1], o_ref.shape[1]
+    per = BLOCK // rows
+    weights = Spread(n_d, n_t, [up_ref, ow_ref], [up_all, ow_all], sems)
+    first_group = max(0, k_ref.shape[1] // BLOCK - 4)
+    place = att_ref.at[t // group, :, span(lax.rem(t, group), width)]
+
+    def outgoing(i, r, k):
+        return pltpu.make_async_remote_copy(
+            src_ref=kept.at[i, pl.ds(r * rows, rows)], dst_ref=place, send_sem=ss.at[k], recv_sem=rs.at[k],
+            device_id=(d, lax.rem(t + k, n_t)), device_id_type=MESH,
+        )
+
+    @pl.when(qi == 0)
+    def _():
+        barrier(
+            [(d, lax.rem(t + k, n_t)) for k in range(1, n_t)] + [(lax.rem(d + k, n_d), t) for k in range(1, n_d)]
+        )
+        weights.begin()
+
+    for g in range(weights.groups()):
+        if first_group + g < k_ref.shape[1] // BLOCK:
+
+            @pl.when(qi == first_group + g)
+            def _():
+                weights.group(g)
+
     qs = [q_ref[h] for h in range(heads)]
 
     def scores(h, j):
@@ -342,25 +519,59 @@
             a, b, c = split3(-(m + jnp.log(total)))
             extra = jnp.where(r == 80, a, jnp.where(r == 81, b, jnp.where(r == 82, c, 0.0))).T
             qb_ref[g] = qs[g] + extra.astype(bf16)
-        o_ref[:, h * HEAD_DIM : (h + 2) * HEAD_DIM] = jnp.concatenate(outs, axis=0).T.astype(bf16)
-
-
-def attend(q, k, vt):
+        slab = jnp.concatenate(outs, axis=0).T.astype(bf16)
+        o_ref[:, h * HEAD_DIM : (h + 2) * HEAD_DIM] = slab
+        kept[qi, :, h * HEAD_DIM : (h + 2) * HEAD_DIM] = slab
+
+    def local(r):
+        return pltpu.make_async_copy(kept.at[t // per, pl.ds(r * rows, rows)], place, here.at[0])
+
+    for r in range(per):
+        k = lax.rem(qi * per + r + n_t - t, n_t)
+
+        @pl.when(k != 0)
+        def _():
+            outgoing(qi, r, k).start()
+
+        @pl.when(k == 0)
+        def _():
+            local(r).start()
+
+    @pl.when(qi == steps - 1)
+    def _():
+        for g in range(k_ref.shape[1] // BLOCK - first_group, weights.groups()):
+            weights.group(g)
+        for k in range(1, n_t):
+            outgoing(0, 0, k).wait()
+        local(0).wait()
+        weights.end()
+
+
+def attend(n_d, n_t, trees, q, k, vt, ow, up):
     heads, rows, _ = q.shape
-    together = min(4, heads)
-    slab = pl.BlockSpec((together, rows, LANES), lambda h, i: (h, 0, 0))
-    block = pl.BlockSpec((together, BLOCK, LANES), lambda h, i: (h, i, 0))
+    slab = pl.BlockSpec((heads, rows, LANES), lambda i: (0, 0, 0))
+    block = pl.BlockSpec((heads, BLOCK, LANES), lambda i: (0, i, 0))
+    wide = heads * HEAD_DIM
+    dma = pltpu.SemaphoreType.DMA
+    sds = jax.ShapeDtypeStruct
     return pl.pallas_call(
-        fwd_kernel,
-        grid=(heads // together, rows // BLOCK),
-        in_specs=[block, slab, pl.BlockSpec((together, VROWS, rows), lambda h, i: (h, 0, 0))],
-        out_specs=[pl.BlockSpec((BLOCK, together * HEAD_DIM), lambda h, i: (i, h)), block],
+        functools.partial(fwd_kernel, n_d, n_t, trees),
+        grid=(rows // BLOCK,),
+        in_specs=[block, slab, pl.BlockSpec((heads, VROWS, rows), lambda i: (0, 0, 0)), VMEM, VMEM],
+        out_specs=[pl.BlockSpec((BLOCK, wide), lambda i: (i, 0)), block, HBM, HBM, HBM],
         out_shape=[
-            jax.ShapeDtypeStruct((rows, heads * HEAD_DIM), bf16),
-            jax.ShapeDtypeStruct(q.shape, bf16),
+            sds((rows, wide), bf16),
+            sds(q.shape, bf16),
+            sds((trees, rows // n_t, wide * n_t // trees), bf16),
+            sds((n_t,) + ow.shape, bf16),
+            sds((n_t,) + up.shape, bf16),
         ],
+        scratch_shapes=[
+            pltpu.VMEM((rows // BLOCK, BLOCK, wide), bf16), dma((n_t,)), dma((n_t,)), dma((1,)),
+        ] + Spread.sems(2, n_d, n_t),
+        compiler_params=pltpu.CompilerParams(collective_id=1, has_side_effects=True),
         name="attend",
-    )(q, k, vt)
+    )(q, k, vt, ow, up)
 
 
 def bwd_kernel(q_ref, k_ref, v_ref, kt_ref, d_ref, o_ref, cos_ref, sin_ref, m_ref, sums, wide):
@@ -493,8 +704,7 @@
         feed_in[...] = (ln_parts(h)[0] * par(2) + par(3)).astype(bf16)
         acc[...] = jnp.zeros_like(acc)
 
-    up = up_ref[...].reshape(feed_in.shape[1], -1)
-    down = down_ref[...].reshape(-1, feed_in.shape[1])
+    up, down = up_ref[0], down_ref[0]
 
     @pl.when(phase == 0)
     def _():
@@ -544,7 +754,7 @@
 
 def feed(att, x, cot, ow, par, up, down):
     rows, wide = att.shape
-    n_d, n_t, _, width = up.shape
+    n_t, _, width = up.shape
     one = lambda a: pl.BlockSpec(a.shape, lambda p, n: (0,) * len(a.shape), pipeline_mode=pl.Buffered(1))
     sds = jax.ShapeDtypeStruct
     outs = [
@@ -553,7 +763,7 @@
         sds((8, wide), f32),
     ]
     chunk = lambda a: pl.BlockSpec((1,) + a.shape[1:], lambda p, n: (p * n, 0, 0))
-    weight = lambda a: pl.BlockSpec((a.shape[0], 1) + a.shape[2:], lambda p, n: (0, n, 0, 0))
+    weight = lambda a: pl.BlockSpec((1,) + a.shape[1:], lambda p, n: (n, 0, 0))
     return pl.pallas_call(
         feed_kernel,
         grid=(2, n_t),
@@ -580,18 +790,6 @@
         return 0
 
     lax.fori_loop(0, rows // step, body, 0)
-
-
-def orders(n_d):
-    bits = n_d.bit_length() - 1
-    return [list(range(bits)), list(range(bits - 1, -1, -1))]
-
-
-def combos(bits):
-    masks = [0]
-    for b in bits:
-        masks = masks + [m ^ (1 << b) for m in masks]
-    return masks
 
 
 def finish_kernel(
@@ -888,34 +1086,25 @@
     tree = t // group
     width = out_weight.shape[0]
 
-    def part(w):
-        return lax.dynamic_slice_in_dim(w, d * (w.shape[0] // n_d), w.shape[0] // n_d, 0)
-
-    def everyone(w):
-        full = lax.all_gather(part(w), ("dp", "tensor"), axis=0, tiled=False)
-        return full.reshape((n_d, n_t) + full.shape[1:])
-
-    out_all, up_all, down_all = everyone(out_weight), everyone(up_weight), everyone(down_weight)
-    out_all = out_all.transpose(1, 0, 2, 3).reshape(-1, wide)
-
     mine = lambda a: lax.dynamic_index_in_dim(a, tree, 0, keepdims=False)
     cosine, sine, mq, mk = tables(mine(lengths), mine(parents), n_t * rows)
 
     x = tokens.astype(f32)
     normed = layer_norm(x, first_gain, first_shift)
-    gathered, w = gather_tree(n_d, n_t, normed.astype(bf16), in_weight.transpose(1, 0, 2))
+    gathered, w, down_all = gather_tree(
+        n_d, n_t, normed.astype(bf16), in_weight.transpose(1, 0, 2), down_weight
+    )
     w = w.transpose(1, 2, 0, 3).reshape(3, wide, -1)
     q, k, v, kt, vt = project(gathered, w, cosine, sine, mq, mk)
-    attended, qb = attend(q, k, vt)
-    att = exchange_heads(n_t, trees, attended, False)
+    attended, qb, att, out_all, up_all = attend(n_d, n_t, trees, q, k, vt, out_weight, up_weight)
     par = jnp.stack(
         [second_gain, second_shift, third_gain, third_shift, fourth_gain, fourth_shift, first_gain, first_shift]
     )
     flat = lambda a: a.reshape(trees * rows, a.shape[-1])
     output, back_hidden, back_att, up_g, down_g, out_g, vec = feed(
-        flat(att), flat(tokens), flat(cotangent), out_all, par, up_all, down_all
+        flat(att), flat(tokens), flat(cotangent), out_all.reshape(-1, wide), par, up_all, down_all
     )
-    d_heads = exchange_heads(n_t, trees, back_att.reshape(trees, rows, wide), True)
+    d_heads = exchange_heads(n_t, trees, back_att.reshape(trees, rows, wide))
     back_mixed = attend_back(qb, k, v, kt, d_heads, attended, cosine, sine)
     w_flat = w.transpose(1, 0, 2).reshape(wide, -1)
     partial = lax.dot_general(back_mixed, w_flat, NT, preferred_element_type=f32).astype(bf16)

time: 574 us -> 526 us (0.916)
  waiting for transfers between devices: 64.7 us -> 0 us
  Pallas kernels: 445 us -> 481 us
  between operations: 14 us -> 0.91 us
  local copies, waits for them, and re-layouts: 25.5 us -> 18.4 us
    all_gather x3 -> x0, waiting for transfers between devices: 64.6 us -> none  [everyone(): full = lax.all_gather(part(w), ('dp', 'tensor'), axis=0, tiled=False)]
    pallas_call x1, Pallas kernels: 60.4 us -> 102 us  [gather_tree(): pl.pallas_call(functools.partial(gather_kernel, n_d, n_t), in_specs=[VMEM...]
    pallas_call x3 -> x2, Pallas kernels: 106 us -> 101 us  [the longest x1 76 us: attend(): pl.pallas_call(functools.partial(fwd_kernel, n_d, n_t, trees), grid=(rows...]
  transfers between devices with their start and end apart: 3 -> 0, of which waited for: 1 -> 0; matrix products, arithmetic and copies ran while one was open for 4% -> 0% of each run, Pallas kernels for 28% -> 0%
where the time goes in v3:
time: 526 us; the launch traced here: 525 us
  Pallas kernels  481 us (91%)
  local copies, waits for them, and re-layouts  18.4 us (3%)
  other arithmetic  13.4 us (3%)
  matrix products  11.7 us (2%)
    pallas_call x1, Pallas kernels, finish(): pl.pallas_call(functools.partial(finish_kernel, n_d, n_t), in_specs=[VMEM...  152 us
    pallas_call x1, Pallas kernels, gather_tree(): pl.pallas_call(functools.partial(gather_kernel, n_d, n_t), in_specs=[VMEM...  102 us
    pallas_call x1, Pallas kernels, attend(): pl.pallas_call(functools.partial(fwd_kernel, n_d, n_t, trees), grid=(rows...  76 us
    pallas_call x1, Pallas kernels, attend_back(): pl.pallas_call(bwd_kernel, grid=(rows // BLOCK,), in_specs=[whole(q), blo...  60.7 us
    pallas_call x1, Pallas kernels, feed(): pl.pallas_call(feed_kernel, grid=(2, n_t), in_specs=[one(a) for a in (att...  52.2 us
    pallas_call x1, Pallas kernels, exchange_heads(): pl.pallas_call(functools.partial(heads_kernel, n_t, trees), in_specs=[VME...  25.1 us
    pallas_call x1, Pallas kernels, project(): pl.pallas_call(qkv_kernel, grid=(rows // BLOCK,), in_specs=[pl.BlockSpec(...  12.6 us

profile of v3, /device:TPU:0, one launch (start us, length us, event | category | flops | bytes accessed | tf_op | source)
XLA Modules:
  0.0 524.9 jit_solution(5251497418486205915)
XLA Ops:
  0.8 0.8 dynamic-slice_bitcast_fusion.1
  1.5 0.7 dynamic-slice_bitcast_fusion
  2.3 0.2 reduce-window.7
  2.6 1.4 convert_reduce_fusion
  4.0 1.6 fusion.2
  5.8 0.1 select_reduce_fusion.3
  5.9 0.1 select_reduce_fusion
  6.1 0.7 stack.35.par_ref
  6.8 1.4 fusion.5.x_ref
  8.2 2.7 fusion.11
  10.9 5.5 %fusion.6 = (f32[2048,128]{1,0:T(8,128)}, f32[2048,128]{1,0:T(8,128)}) fusion(f32[128]{0:T(128)S(1)} %get-tuple-element.86, f32[128]{0:T(128)S(1)} %get-tuple-element.87, f32[2048]{0:T(1024)S(1)} %add_convert_fusion), kind=kLoop, calls=%fused_computation.15 | loop fusion | flops 524288 | bytes 2106368 | tf_op jit(solution)/shard_map/mul | solution.py:83
  16.4 101.8 %gather_tree.1 = (bf16[2048,1024]{1,0:T(8,128)(2,1)}, bf16[2,3,1024,128]{3,2,1,0:T(8,128)(2,1)}, bf16[8,512,1024]{2,1,0:T(8,128)(2,1)}) custom-call(bf16[2,256,1024]{2,1,0:T(8,128)(2,1)} %fusion.5.x_ref, bf16[3,1024,128]{2,1,0:T(8,128)(2,1)} %bitcast.66, bf16[512,1024]{1,0:T(8,128)(2,1)} %f_ref.1), custom_call_target="tpu_custom_call" | custom-call | tf_op jit(solution)/shard_map/gather_tree/pallas_call | solution.py:337
  118.3 2.8 fusion.17
  121.0 1.8 copy.36
  122.8 12.6 %project.1 = (bf16[4,2048,128]{2,1,0:T(8,128)(2,1)}, bf16[4,2048,128]{2,1,0:T(8,128)(2,1)}, bf16[4,2048,128]{2,1,0:T(8,128)(2,1)}, bf16[4,64,2048]{2,1,0:T(8,128)(2,1)}, bf16[4,80,2048]{2,1,0:T(8,128)(2,1)}) custom-call(bf16[2048,1024]{1,0:T(8,128)(2,1)} %get-tuple-element.40.x_ref, bf16[3,1024,256]{2,1,0:T(8,128)(2,1)} %get-tuple-element.71.w_ref, ...), custom_call_target="tpu_custom_call" | custom-call | tf_op jit(solution)/shard_map/project/pallas_call | solution.py:430
  135.5 76.0 %attend.1 = (bf16[2048,256]{1,0:T(8,128)(2,1)}, bf16[4,2048,128]{2,1,0:T(8,128)(2,1)}, bf16[2,256,1024]{2,1,0:T(8,128)(2,1)}, bf16[8,128,1024]{2,1,0:T(8,128)(2,1)}, bf16[8,1024,512]{2,1,0:T(8,128)(2,1)}) custom-call(bf16[4,2048,128]{2,1,0:T(8,128)(2,1)} %get-tuple-element.42.q_ref, bf16[4,2048,128]{2,1,0:T(8,128)(2,1)} %get-tuple-element.43.k_ref, ...), custom_call_target="tpu_custom_call" | custom-call | tf_op jit(solution)/shard_map/attend/pallas_call | solution.py:557
  211.5 52.2 %feed.1 = (bf16[512,1024]{1,0:T(8,128)(2,1)}, f32[512,1024]{1,0:T(8,128)}, bf16[512,1024]{1,0:T(8,128)(2,1)}, bf16[8,1024,512]{2,1,0:T(8,128)(2,1)}, bf16[8,512,...) custom-call(bf16[512,1024]{1,0:T(8,128)(2,1)} %bitcast.65, bf16[512,1024]{1,0:T(8,128)(2,1)} %bitcast.55, ...), custom_call_target="tpu_custom_call" | custom-call | tf_op jit(solution)/shard_map/feed/pallas_call | solution.py:767
  263.7 25.1 %heads_back.1.d_ref = bf16[2048,256]{1,0:T(8,128)(2,1)} custom-call(bf16[2,256,1024]{2,1,0:T(8,128)(2,1)} %bitcast.63), custom_call_target="tpu_custom_call" | custom-call | tf_op jit(solution)/shard_map/heads_back/pallas_call | solution.py:374
  288.8 60.7 %attend_back.1 = bf16[2048,768]{1,0:T(8,128)(2,1)} custom-call(bf16[4,2048,128]{2,1,0:T(8,128)(2,1)} %get-tuple-element.50.q_ref, bf16[4,2048,128]{2,1,0:T(8,128)(2,1)} %get-tuple-element.43.k_ref, bf16[4,2048,128]{2,1,0:T(8,128)(2,1)} %get-tuple-element.51.v_ref, bf16[4,64,2048]{2,1,0:T(8,128)(2,1)} %get-tuple-element.52.kt_ref, ...), custom_call_target="tpu_custom_call" | custom-call | tf_op jit(solution)/shard_map/attend_back/pallas_call | solution.py:659
  349.5 6.8 %convolution_convert_fusion.1 = bf16[1024,768]{0,1:T(8,128)(2,1)S(1)} fusion(bf16[2048,1024]{1,0:T(8,128)(2,1)} %get-tuple-element.40.x_ref, bf16[2048,768]{1,0:T(8,128)(2,1)} %attend_back.1), kind=kOutput, calls=%fused_computation.9 | convolution fusion | flops 3222011904 | bytes 8912896 | tf_op jit(solution)/shard_map/dot_general | solution.py:1111
  356.3 4.9 convolution_convert_fusion.sum_ref
  361.2 1.6 copy.37
  362.8 152.0 %finish.1 = (bf16[2,256,1024]{2,1,0:T(8,128)(2,1)}, f32[8,1024]{1,0:T(8,128)}, f32[1024,512]{1,0:T(8,128)}, f32[512,1024]{1,0:T(8,128)}, f32[128,1024]{1,0:T(8,128)}, /*index=5*/f32[3072,128]{1,0:T(8,128)}) custom-call(bf16[2048,1024]{1,0:T(8,128)(2,1)} %convolution_convert_fusion.sum_ref, bf16[2,256,1024]{2,1,0:T(8,128)(2,1)} %x_ref.1, ...), custom_call_target="tpu_custom_call" | custom-call | tf_op jit(solution)/shard_map/finish/pallas_call | solution.py:1057
  514.8 1.8 fusion.18
  516.7 2.3 copy.47
  518.9 1.1 copy.48
  520.1 0.2 copy-done.6
  520.3 0.8 copy.49
  521.1 0.2 copy-done.3
  521.3 1.3 copy.50
  522.6 1.0 copy-done.2
  523.6 1.3 copy.51
  (36 shorter events, 0.4 us)
Async XLA Ops:
  0.7 6.2 %copy-start = (bf16[2,256,1024]{2,1,0:T(8,128)(2,1)S(1)}, bf16[2,256,1024]{2,1,0:T(8,128)(2,1)}, u32[]{:S(2)}) copy-start(bf16[2,256,1024]{2,1,0:T(8,128)(2,1)} %x_ref.1) | copy-start | bytes 3145732
  0.7 5.4 %copy-start.7 = (f32[1024]{0:T(1024)S(1)}, f32[1024]{0:T(1024)}, u32[]{:S(2)}) copy-start(f32[1024]{0:T(1024)} %param.21) | copy-start | bytes 12292
  0.7 5.4 %copy-start.8 = (f32[1024]{0:T(1024)S(1)}, f32[1024]{0:T(1024)}, u32[]{:S(2)}) copy-start(f32[1024]{0:T(1024)} %param.20) | copy-start | bytes 12292
  0.7 5.4 %copy-start.14 = (f32[1024]{0:T(1024)S(1)}, f32[1024]{0:T(1024)}, u32[]{:S(2)}) copy-start(f32[1024]{0:T(1024)} %param.31) | copy-start | bytes 12292
  0.7 5.4 %copy-start.13 = (f32[1024]{0:T(1024)S(1)}, f32[1024]{0:T(1024)}, u32[]{:S(2)}) copy-start(f32[1024]{0:T(1024)} %param.30) | copy-start | bytes 12292
  0.7 5.4 %copy-start.12 = (f32[1024]{0:T(1024)S(1)}, f32[1024]{0:T(1024)}, u32[]{:S(2)}) copy-start(f32[1024]{0:T(1024)} %param.27) | copy-start | bytes 12292
  0.7 5.4 %copy-start.11 = (f32[1024]{0:T(1024)S(1)}, f32[1024]{0:T(1024)}, u32[]{:S(2)}) copy-start(f32[1024]{0:T(1024)} %param.26) | copy-start | bytes 12292
  0.7 5.4 %copy-start.10 = (f32[1024]{0:T(1024)S(1)}, f32[1024]{0:T(1024)}, u32[]{:S(2)}) copy-start(f32[1024]{0:T(1024)} %param.25) | copy-start | bytes 12292
  0.7 5.4 %copy-start.9 = (f32[1024]{0:T(1024)S(1)}, f32[1024]{0:T(1024)}, u32[]{:S(2)}) copy-start(f32[1024]{0:T(1024)} %param.24) | copy-start | bytes 12292
  349.5 6.8 %copy-start.1 = (bf16[2048,768]{1,0:T(8,128)(2,1)S(1)}, bf16[2048,768]{1,0:T(8,128)(2,1)}, u32[]{:S(2)}) copy-start(bf16[2048,768]{1,0:T(8,128)(2,1)} %attend_back.1) | copy-start | bytes 9437188
  349.5 6.8 %copy-start.4 = (bf16[1024,3,256]{0,2,1:T(8,128)(2,1)S(1)}, bf16[1024,3,256]{0,2,1:T(8,128)(2,1)}, u32[]{:S(2)}) copy-start(bf16[1024,3,256]{0,2,1:T(8,128)(2,1)} %copy.36) | copy-start | bytes 4718596
  514.8 4.1 copy-start.5
  518.9 1.4 copy-start.6
  518.9 2.3 copy-start.3
  521.3 2.3 copy-start.2

commit v4 on v3

--- a/solution.py
+++ b/solution.py
@@ -109,6 +109,20 @@
     return copy
 
 
+def add_rows(target, source, step=64):
+    rows = target.shape[0]
+    step = min(step, rows)
+    while rows % step:
+        step //= 2
+
+    def body(i, _):
+        at = span(i, step)
+        target[at, :] = target[at, :] + source[at, :]
+        return 0
+
+    lax.fori_loop(0, rows // step, body, 0)
+
+
 def orders(n_d):
     bits = n_d.bit_length() - 1
     return [list(range(bits)), list(range(bits - 1, -1, -1))]
@@ -350,36 +364,6 @@
         compiler_params=pltpu.CompilerParams(collective_id=0, has_side_effects=True),
         name="gather_tree",
     )(normed, weight, down)
-
-
-def heads_kernel(n_t, trees, x_ref, o_ref, ss, rs):
-    d, t = lax.axis_index("dp"), lax.axis_index("tensor")
-    group = n_t // trees
-    others = [lax.rem(t + k, n_t) for k in range(1, n_t)]
-    barrier([(d, o) for o in others])
-    rows, width = x_ref.shape[1], x_ref.shape[2] // group
-    cut = lambda o: x_ref.at[o // group, :, span(lax.rem(o, group), width)]
-    place = o_ref.at[span(t, rows), :]
-    copies = [
-        send(cut(o), place, ss.at[k], rs.at[k], (d, o)) for k, o in enumerate(others)
-    ]
-    place[...] = cut(t)[...]
-    for copy in copies:
-        copy.wait()
-
-
-def exchange_heads(n_t, trees, x):
-    _, rows, wide = x.shape
-    dma = pltpu.SemaphoreType.DMA
-    return pl.pallas_call(
-        functools.partial(heads_kernel, n_t, trees),
-        in_specs=[VMEM],
-        out_specs=VMEM,
-        out_shape=jax.ShapeDtypeStruct((n_t * rows, wide * trees // n_t), bf16),
-        scratch_shapes=[dma((n_t - 1,)), dma((n_t - 1,))],
-        compiler_params=pltpu.CompilerParams(collective_id=2, has_side_effects=True),
-        name="heads_back",
-    )(x)
 
 
 def qkv_kernel(x_ref, w_ref, cos_ref, sin_ref, mq_ref, mk_ref, q_ref, k_ref, v_ref, kt_ref, vt_ref):
@@ -574,17 +558,173 @@
     )(q, k, vt, ow, up)
 
 
-def bwd_kernel(q_ref, k_ref, v_ref, kt_ref, d_ref, o_ref, cos_ref, sin_ref, m_ref, sums, wide):
+class Reduce:
+    def __init__(self, n_d, n_t, sources, totals, scratch):
+        self.n_d, self.n_t, self.sources, self.totals = n_d, n_t, sources, totals
+        count = len(sources)
+        self.mine, self.side, self.land_at, self.far = (
+            scratch[i * count : (i + 1) * count] for i in range(4)
+        )
+        self.s_load, self.s_side, self.r_side, self.s_hop, self.r_hop, self.s_far, self.r_far = scratch[4 * count :]
+        self.d, self.t = lax.axis_index("dp"), lax.axis_index("tensor")
+        self.chips = n_t // 2
+        self.chip, self.core = self.t // 2, lax.rem(self.t, 2)
+        self.other = 2 * self.chip + 1 - self.core
+        self.dest = [lax.rem(self.chip + k, self.chips) for k in range(1, self.chips)] + [self.chip]
+        self.bits = n_d.bit_length() - 1
+        self.units = [(n, k) for k in range(self.chips) for n in range(count)]
+
+    @staticmethod
+    def scratch(n_d, n_t, shapes):
+        dma = pltpu.SemaphoreType.DMA
+        chips, slots, count = n_t // 2, 2 * (n_d - 1), len(shapes)
+        vm = lambda lead, r, c: pltpu.VMEM(lead + (r, c), bf16)
+        units = count * chips
+        return (
+            [vm((chips,), r, c) for r, c in shapes] * 2
+            + [vm((chips, slots), r // n_d, c // 2) for r, c in shapes]
+            + [vm((chips - 1,), r // n_d, c) for r, c in shapes]
+            + [dma((units,)), dma((units,)), dma((units,)), dma((units, slots)), dma((units, slots))]
+            + [dma((units,)), dma((units,))]
+        )
+
+    def remote(self, src, dst, ssem, rsem, device):
+        return pltpu.make_async_remote_copy(
+            src_ref=src, dst_ref=dst, send_sem=ssem, recv_sem=rsem, device_id=device, device_id_type=MESH
+        )
+
+    def load(self, u):
+        n, k = self.units[u]
+        source = self.sources[n].at[2 * self.dest[k] + self.core]
+        return pltpu.make_async_copy(source, self.mine[n].at[k], self.s_load.at[u])
+
+    def beside(self, u):
+        n, k = self.units[u]
+        source = self.sources[n].at[2 * self.dest[k] + 1 - self.core]
+        return self.remote(source, self.side[n].at[k], self.s_side.at[u], self.r_side.at[u], (self.d, self.other))
+
+    def cut(self, u, part, stream):
+        n, k = self.units[u]
+        _, height, width = self.mine[n].shape
+        height, width = height // self.n_d, width // 2
+        return self.mine[n].at[k, span(part, height), pl.ds(stream * width, width)]
+
+    def hops(self, u, step):
+        n, k = self.units[u]
+        slot = 0 if step == 0 else self.n_d - (self.n_d >> step)
+        out = []
+        for stream, order in enumerate(orders(self.n_d)):
+            partner = lax.bitwise_xor(self.d, 1 << order[step])
+            for j, m in enumerate(combos(order[step + 1 :])):
+                i = (slot + j) * 2 + stream
+                landing = self.land_at[n].at[k, i]
+                copy = self.remote(
+                    self.cut(u, lax.bitwise_xor(partner, m), stream), landing,
+                    self.s_hop.at[u, i], self.r_hop.at[u, i], (partner, self.t),
+                )
+                out.append((copy, self.cut(u, lax.bitwise_xor(self.d, m), stream), landing))
+        return out
+
+    def piece(self, u):
+        n, k = self.units[u]
+        return self.mine[n].at[k, span(self.d, self.mine[n].shape[1] // self.n_d), :]
+
+    def away(self, u):
+        n, k = self.units[u]
+        return self.remote(
+            self.piece(u), self.far[n].at[k], self.s_far.at[u], self.r_far.at[u],
+            (self.d, 2 * self.dest[k] + self.core),
+        )
+
+    def begin(self):
+        for u in range(len(self.units)):
+            self.load(u).start()
+            self.beside(u).start()
+
+    def events(self):
+        return len(self.units) + self.bits
+
+    def event(self, e):
+        if e < len(self.units):
+            n, k = self.units[e]
+            self.load(e).wait()
+            self.beside(e).wait_recv()
+            add_rows(self.mine[n].at[k], self.side[n].at[k])
+            for copy, _, _ in self.hops(e, 0):
+                copy.start()
+        for step in range(self.bits):
+            u = e - 1 - step
+            if 0 <= u < len(self.units):
+                for copy, target, landing in self.hops(u, step):
+                    copy.wait_recv()
+                    add_rows(target, landing)
+                if step + 1 < self.bits:
+                    for copy, _, _ in self.hops(u, step + 1):
+                        copy.start()
+                elif self.units[u][1] < self.chips - 1:
+                    self.away(u).start()
+
+    def end(self):
+        for u, (n, k) in enumerate(self.units):
+            if k < self.chips - 1:
+                self.away(u).wait_recv()
+            else:
+                total = self.piece(u)[...].astype(f32)
+                for i in range(self.chips - 1):
+                    total = total + self.far[n][i].astype(f32)
+                self.totals[n][...] = total.astype(bf16)
+        for u, (n, k) in enumerate(self.units):
+            self.beside(u).wait_send()
+            for step in range(self.bits):
+                for copy, _, _ in self.hops(u, step):
+                    copy.wait_send()
+            if k < self.chips - 1:
+                self.away(u).wait_send()
+
+
+def bwd_kernel(
+    n_d, n_t, q_ref, k_ref, v_ref, kt_ref, x_ref, o_ref, cos_ref, sin_ref, up_ref, down_ref, og_ref,
+    m_ref, up_tot, down_tot, og_tot, sums, wide, d_ref, hs, hr, *scratch,
+):
     j = pl.program_id(0)
     heads, rows, _ = q_ref.shape
     nq = rows // BLOCK
     row, col = row_of((BLOCK, BLOCK)), lane_of((BLOCK, BLOCK))
     lane = lane_of((BLOCK, LANES))
     first = lane < HEAD_DIM
+    d, t = lax.axis_index("dp"), lax.axis_index("tensor")
+    trees, part, _ = x_ref.shape
+    group, width = n_t // trees, heads * HEAD_DIM
+    gradients = Reduce(n_d, n_t, [up_ref, down_ref, og_ref], [up_tot, down_tot, og_tot], scratch)
+    ahead = 3
+    points = 10
+
+    def point(p):
+        left = gradients.events() - ahead
+        for e in range(ahead + p * left // points, ahead + (p + 1) * left // points):
+            gradients.event(e)
+
+    def cut(o):
+        return x_ref.at[o // group, :, span(lax.rem(o, group), width)]
+
+    def outgoing(k):
+        o = lax.rem(t + k, n_t)
+        return gradients.remote(cut(o), d_ref.at[span(t, part), :], hs.at[k], hr.at[k], (d, o))
 
     @pl.when(j == 0)
     def _():
+        barrier(
+            [(d, lax.rem(t + k, n_t)) for k in range(1, n_t)] + [(lax.rem(d + k, n_d), t) for k in range(1, n_d)]
+        )
+        for k in range(1, n_t):
+            outgoing(k).start()
+        gradients.begin()
+        d_ref[span(t, part), :] = cut(t)[...]
         sums[...] = jnp.zeros_like(sums)
+        for e in range(ahead):
+            gradients.event(e)
+        for k in range(1, n_t):
+            outgoing(k).wait()
 
         def widen(i, _):
             at = span(i, BLOCK)
@@ -602,6 +742,13 @@
 
         lax.fori_loop(0, nq, widen, 0)
 
+    for p in range(0, points, 2):
+        if p // 2 < nq:
+
+            @pl.when(j == p // 2)
+            def _():
+                point(p)
+
     ks = [k_ref[h] for h in range(heads)]
     vs = [v_ref[h] for h in range(heads)]
     kts = [kt_ref[h] for h in range(heads)]
@@ -626,7 +773,16 @@
         return tuple(out)
 
     state = tuple(pair(h, j, True) for h in range(heads))
-    state = lax.fori_loop(j + 1, nq, step, state)
+    middle = (j + 1 + nq) // 2
+    state = lax.fori_loop(j + 1, middle, step, state)
+    for p in range(1, points, 2):
+        if p // 2 < nq:
+
+            @pl.when(j == p // 2)
+            def _():
+                point(p)
+
+    state = lax.fori_loop(middle, nq, step, state)
 
     def join(a, b):
         return jnp.where(first, a, pltpu.roll(b, HEAD_DIM, 1))
@@ -650,28 +806,43 @@
             begin = n * total + h * HEAD_DIM
             m_ref[:, begin : begin + 2 * HEAD_DIM] = part.astype(bf16)
 
-
-def attend_back(q, k, v, kt, d, o, cosine, sine):
+    @pl.when(j == nq - 1)
+    def _():
+        for p in range(2 * nq, points):
+            point(p)
+        gradients.end()
+
+
+def attend_back(n_d, n_t, q, k, v, kt, x, o, cosine, sine, up_g, down_g, out_g):
     heads, rows, _ = q.shape
-    whole = lambda a: pl.BlockSpec(a.shape, lambda j: (0,) * a.ndim)
+    whole = lambda a: pl.BlockSpec(a.shape, lambda j: (0,) * a.ndim, pipeline_mode=pl.Buffered(1))
     block = pl.BlockSpec((heads, BLOCK, LANES), lambda j: (0, j, 0))
     table = pl.BlockSpec((BLOCK, LANES), lambda j: (j, 0))
+    wide = heads * HEAD_DIM
+    dma = pltpu.SemaphoreType.DMA
+    sds = jax.ShapeDtypeStruct
+    shapes = [a.shape[1:] for a in (up_g, down_g, out_g)]
     return pl.pallas_call(
-        bwd_kernel,
+        functools.partial(bwd_kernel, n_d, n_t),
         grid=(rows // BLOCK,),
         in_specs=[
             whole(q), block, block,
             pl.BlockSpec((heads, HEAD_DIM, BLOCK), lambda j: (0, 0, j)),
-            whole(d), whole(o), table, table,
+            VMEM, whole(o), table, table, HBM, HBM, HBM,
         ],
-        out_specs=pl.BlockSpec((BLOCK, 3 * heads * HEAD_DIM), lambda j: (j, 0)),
-        out_shape=jax.ShapeDtypeStruct((rows, 3 * heads * HEAD_DIM), bf16),
+        out_specs=[pl.BlockSpec((BLOCK, 3 * wide), lambda j: (j, 0)), VMEM, VMEM, VMEM],
+        out_shape=[sds((rows, 3 * wide), bf16)] + [sds((r // n_d, c), bf16) for r, c in shapes],
         scratch_shapes=[
             pltpu.VMEM((heads, HEAD_DIM, rows), f32),
             pltpu.VMEM((heads, rows, LANES), bf16),
-        ],
+            pltpu.VMEM((rows, wide), bf16),
+            dma((n_t,)), dma((n_t,)),
+        ] + Reduce.scratch(n_d, n_t, shapes),
+        compiler_params=pltpu.CompilerParams(
+            collective_id=2, has_side_effects=True, vmem_limit_bytes=67043328
+        ),
         name="attend_back",
-    )(q, k, v, kt, d, o, cosine, sine)
+    )(q, k, v, kt, x, o, cosine, sine, up_g, down_g, out_g)
 
 
 def ln_parts(v):
@@ -778,28 +949,12 @@
         compiler_params=pltpu.CompilerParams(vmem_limit_bytes=64 << 20),
         name="feed",
     )(att, x, cot, ow, par, up, down)
-def add_rows(target, source, step=64):
-    rows = target.shape[0]
-    step = min(step, rows)
-    while rows % step:
-        step //= 2
-
-    def body(i, _):
-        at = span(i, step)
-        target[at, :] = target[at, :] + source[at, :]
-        return 0
-
-    lax.fori_loop(0, rows // step, body, 0)
-
-
 def finish_kernel(
-    n_d, n_t, sum_ref, x_ref, hid_ref, par_ref, vec_in, up_ref, down_ref, og_ref, ig_ref,
+    n_d, n_t, sum_ref, x_ref, hid_ref, par_ref, vec_in, up_tot, down_tot, og_tot, ig_ref,
     bt_ref, vec_ref, up_out, down_out, og_out, ig_out,
-    mine_up, mine_down, mine_og, mine_ig, side_up, side_down, side_og,
-    hop_up, hop_down, hop_og, hop_ig, far_up, far_down, far_og, far_ig,
-    full_up, full_down, full_og, full_ig,
+    mine, landed, far, full_up, full_down, full_og, full_ig,
     r_side, r_out, r_land, vec_now, vec_got, vec_far,
-    s_load, s_side, r_sides, s_hop, r_hop, s_far, r_far, s_all, r_all, s_own, r_own,
+    s_load, s_hop, r_hop, s_all, r_all, s_own, r_own,
     s_red, r_red, s_redside, r_redside, s_vec, r_vec,
 ):
     d, t = lax.axis_index("dp"), lax.axis_index("tensor")
@@ -814,110 +969,79 @@
     peers = [lax.rem(d + k, n_d) for k in range(1, n_d)]
     bits = n_d.bit_length() - 1
     barrier([(d, lax.rem(t + k, n_t)) for k in range(1, n_t)] + [(p, t) for p in peers])
+    totals = [up_tot, down_tot, og_tot]
+    fulls = [full_up, full_down, full_og, full_ig]
+    outs = [up_out, down_out, og_out, ig_out]
 
     red_pairs = []
     for k, c in enumerate(dest):
         theirs = sum_ref.at[span(2 * c + 1 - core, rows), :]
         red_pairs.append(send(theirs, r_side.at[k], s_redside.at[k], r_redside.at[k], (d, other)))
-
-    items = [
-        (up_ref, mine_up, side_up, hop_up, far_up, full_up, up_out),
-        (down_ref, mine_down, side_down, hop_down, far_down, full_down, down_out),
-        (og_ref, mine_og, side_og, hop_og, far_og, full_og, og_out),
-        (ig_ref, mine_ig, None, hop_ig, far_ig, full_ig, ig_out),
-    ]
-    units = [(n, k) for k in range(chips) for n in range(3)]
-    units = units[:3] + [(3, i) for i in range(trees)] + units[3:]
-    number = {u: i for i, u in enumerate(units)}
-    loads, sides = {}, {}
-    for u in units:
-        n, k = u
-        source, mine, side = items[n][:3]
-        i = number[u]
-        if n < 3:
-            sides[u] = send(source.at[2 * dest[k] + 1 - core], side.at[k], s_side.at[i], r_sides.at[i], (d, other))
-            loads[u] = pltpu.make_async_copy(source.at[2 * dest[k] + core], mine.at[k], s_load.at[i])
+    loads = []
+    for k in range(trees):
+        loads.append(pltpu.make_async_copy(ig_ref.at[k], mine.at[k], s_load.at[k]))
+        loads[k].start()
+    hops, spreads = {}, []
+
+    def cut(k, part):
+        return mine.at[k, span(part, mine.shape[1] // n_d), :]
+
+    def hop(k, step):
+        slot = 0 if step == 0 else n_d - (n_d >> step)
+        order = orders(n_d)[k % 2]
+        partner = lax.bitwise_xor(d, 1 << order[step])
+        for j, m in enumerate(combos(order[step + 1 :])):
+            hops[k, step, j] = send(
+                cut(k, lax.bitwise_xor(partner, m)), landed.at[k, slot + j],
+                s_hop.at[k, slot + j], r_hop.at[k, slot + j], (partner, t),
+            )
+
+    def land(k, step):
+        slot = 0 if step == 0 else n_d - (n_d >> step)
+        for j, m in enumerate(combos(orders(n_d)[k % 2][step + 1 :])):
+            hops[k, step, j].wait_recv()
+            add_rows(cut(k, lax.bitwise_xor(d, m)), landed.at[k, slot + j])
+        if step + 1 < bits:
+            hop(k, step + 1)
         else:
-            loads[u] = pltpu.make_async_copy(source.at[k], mine.at[k], s_load.at[i])
-        loads[u].start()
-
+            away(k)
+
+    def spread(n, source):
+        at = span(d, fulls[n].shape[0] // n_d)
+        for j, p in enumerate(peers):
+            spreads.append(send(source, fulls[n].at[at, :], s_all.at[n, j], r_all.at[n, j], (p, t)))
+
+    def owner(i):
+        return lax.rem(t, group) * trees + i
+
+    def away(k):
+        here = t // group
+
+        @pl.when(owner(k) != t)
+        def _():
+            send(cut(k, d), far.at[here], s_own.at[k], r_own.at[here], (d, owner(k)))
+
+        @pl.when(owner(k) == t)
+        def _():
+            far[here] = cut(k, d)[...]
+
+    for k in range(trees):
+        loads[k].wait()
+        hop(k, 0)
+    spread(0, totals[0])
     red_copies = []
     for k, c in enumerate(line):
         red_pairs[k].wait_recv()
         r_out[k] = sum_ref[span(2 * c + core, rows), :] + r_side[k]
         red_copies.append(send(r_out.at[k], r_land.at[k], s_red.at[k], r_red.at[k], (d, 2 * c + core)))
-
-    hops = {}
-
-    def cut(n, k, part, stream):
-        mine = items[n][1]
-        height, width = mine.shape[1] // n_d, mine.shape[2] // (2 if n < 3 else 1)
-        return mine.at[k, span(part, height), pl.ds(stream * width, width)]
-
-    def streams(n, k):
-        return orders(n_d) if n < 3 else [orders(n_d)[k % 2]]
-
-    def begin(u):
-        n, k = u
-        loads[u].wait()
-        if n < 3:
-            sides[u].wait_recv()
-            add_rows(items[n][1].at[k], items[n][2].at[k])
-        hop(u, 0)
-
-    def hop(u, step):
-        n, k = u
-        slot = 0 if step == 0 else n_d - (n_d >> step)
-        for stream, order in enumerate(streams(n, k)):
-            partner = lax.bitwise_xor(d, 1 << order[step])
-            for j, m in enumerate(combos(order[step + 1 :])):
-                i = (slot + j) * 2 + stream
-                hops[u, step, stream, j] = send(
-                    cut(n, k, lax.bitwise_xor(partner, m), stream),
-                    items[n][3].at[k, i],
-                    s_hop.at[number[u], i],
-                    r_hop.at[number[u], i],
-                    (partner, t),
-                )
-
-    def land(u, step):
-        n, k = u
-        slot = 0 if step == 0 else n_d - (n_d >> step)
-        for stream, order in enumerate(streams(n, k)):
-            for j, m in enumerate(combos(order[step + 1 :])):
-                i = (slot + j) * 2 + stream
-                hops[u, step, stream, j].wait_recv()
-                add_rows(cut(n, k, lax.bitwise_xor(d, m), stream), items[n][3].at[k, i])
-        if step + 1 < bits:
-            hop(u, step + 1)
-        else:
-            away(u)
-
-    fars = {}
-
-    def piece(n, k):
-        mine = items[n][1]
-        return mine.at[k, span(d, mine.shape[1] // n_d), :]
-
-    def owner(i):
-        return lax.rem(t, group) * trees + i
-
-    def away(u):
-        n, k = u
-        far = items[n][4]
-        if n < 3:
-            if k < chips - 1:
-                fars[u] = send(piece(n, k), far.at[k], s_far.at[n, k], r_far.at[n, k], (d, 2 * dest[k] + core))
-        else:
-            here = t // group
-
-            @pl.when(owner(k) != t)
-            def _():
-                send(piece(n, k), far.at[here], s_own.at[k], r_own.at[here], (d, owner(k)))
-
-            @pl.when(owner(k) == t)
-            def _():
-                far[here] = piece(n, k)[...]
+    for n in range(3):
+        fulls[n][span(d, fulls[n].shape[0] // n_d), :] = totals[n][...]
+    for step in range(bits):
+        for k in range(trees):
+            land(k, step)
+        if step == 0:
+            spread(1, totals[1])
+            spread(2, totals[2])
 
     def reduced():
         red_pairs[chips - 1].wait_recv()
@@ -960,111 +1084,86 @@
                     send(vec_far.at[chip], vec_far.at[chip], s_vec.at[n], r_vec.at[n], (d, 2 * c + core))
                 )
 
-    count = len(units)
-    vec_at = count - 1 - len(vec_partners)
-    for i in range(count + bits):
-        if i < count:
-            begin(units[i])
-        for step in range(bits):
-            if 0 <= i - 1 - step < count:
-                land(units[i - 1 - step], step)
-        if i == vec_at - 1:
-            reduced()
-        if vec_at <= i <= vec_at + len(vec_partners):
-            vec_step(i - vec_at)
-
-    spreads = []
-    for n in range(4):
-        source, mine, side, hops_ref, far, full, out = items[n]
-        height = full.shape[0] // n_d
-        if n < 3:
-            for k in range(chips - 1):
-                fars[n, k].wait_recv()
-            total = mine[chips - 1, span(d, height), :].astype(f32)
-            for k in range(chips - 1):
-                total = total + far[k].astype(f32)
-        else:
-            for j in range(trees):
-                giver = j * group + t // trees
-
-                @pl.when(giver != t)
-                def _():
-                    pltpu.make_async_remote_copy(
-                        src_ref=far.at[j], dst_ref=far.at[j], send_sem=s_own.at[0], recv_sem=r_own.at[j],
-                        device_id=(d, giver), device_id_type=MESH,
-                    ).wait_recv()
-
-            total = far[0].astype(f32)
-            for j in range(1, trees):
-                total = total + far[j].astype(f32)
-        at = span(d, height)
-        full[at, :] = total.astype(bf16)
-        for j, p in enumerate(peers):
-            spreads.append(send(full.at[at, :], full.at[at, :], s_all.at[n, j], r_all.at[n, j], (p, t)))
+    def widen_all(n):
+        full, out = fulls[n], outs[n]
+        for j in range(n_d - 1):
+            spread_of[n][j].wait_recv()
+        height = 64
+        while full.shape[0] % height:
+            height //= 2
+
+        def widen(i, _):
+            out[span(i, height), :] = full[span(i, height), :].astype(f32)
+            return 0
+
+        lax.fori_loop(0, full.shape[0] // height, widen, 0)
+
+    for j in range(trees):
+        giver = j * group + t // trees
+
+        @pl.when(giver != t)
+        def _():
+            pltpu.make_async_remote_copy(
+                src_ref=far.at[j], dst_ref=far.at[j], send_sem=s_own.at[0], recv_sem=r_own.at[j],
+                device_id=(d, giver), device_id_type=MESH,
+            ).wait_recv()
+
+    total = far[0].astype(f32)
+    for j in range(1, trees):
+        total = total + far[j].astype(f32)
+    at = span(d, full_ig.shape[0] // n_d)
+    full_ig[at, :] = total.astype(bf16)
+    spread(3, full_ig.at[at, :])
+    spread_of = [spreads[n * (n_d - 1) : (n + 1) * (n_d - 1)] for n in range(4)]
+
+    reduced()
+    for i in range(len(vec_partners) + 1):
+        vec_step(i)
+        if i < 3:
+            widen_all(i)
+    for n in range(len(vec_partners) + 1, 3):
+        widen_all(n)
+    widen_all(3)
     for k in range(chips - 1):
         vec_copies[len(vec_partners) + k].wait()
     total = vec_far[0]
     for c in range(1, chips):
         total = total + vec_far[c]
     vec_ref[...] = total
-    for n in range(4):
-        full, out = items[n][5:7]
-        for j in range(n_d - 1):
-            spreads[n * (n_d - 1) + j].wait_recv()
-
-        height = 64
-        while full.shape[0] % height:
-            height //= 2
-
-        def widen(i, _):
-            out[span(i, height), :] = full[span(i, height), :].astype(f32)
-            return 0
-
-        lax.fori_loop(0, full.shape[0] // height, widen, 0)
 
     for k in range(trees):
 
         @pl.when(owner(k) != t)
         def _():
             pltpu.make_async_remote_copy(
-                src_ref=piece(3, k), dst_ref=piece(3, k), send_sem=s_own.at[k], recv_sem=r_own.at[0],
+                src_ref=cut(k, d), dst_ref=cut(k, d), send_sem=s_own.at[k], recv_sem=r_own.at[0],
                 device_id=(d, owner(k)), device_id_type=MESH,
             ).wait_send()
 
-    for copy in red_pairs + red_copies + list(sides.values()) + list(hops.values()) + list(fars.values()) + spreads:
+    for copy in red_pairs + red_copies + list(hops.values()) + spreads:
         copy.wait_send()
 
 
-def finish(n_d, n_t, partial, x, hidden, par, vec, up_g, down_g, out_g, in_g):
+def finish(n_d, n_t, partial, x, hidden, par, vec, up_t, down_t, out_t, in_g):
     trees, rows, wide = x.shape
     chips = n_t // 2
     bits = n_d.bit_length() - 1
     dma = pltpu.SemaphoreType.DMA
     sds = jax.ShapeDtypeStruct
-    any_ = pl.BlockSpec(memory_space=pl.ANY)
-    shapes = [a.shape[1:] for a in (up_g, down_g, out_g, in_g)]
-    counts = [chips] * 3 + [trees]
+    shapes = [(a.shape[0] * n_d, a.shape[1]) for a in (up_t, down_t, out_t)] + [in_g.shape[1:]]
     vm = lambda lead, shape, kind=bf16: pltpu.VMEM(tuple(lead) + tuple(shape), kind)
-    mine = [vm((c,), s) for c, s in zip(counts, shapes)]
-    side = [vm((c,), s) for c, s in zip(counts[:3], shapes[:3])]
-    slots = 2 * (n_d - 1)
-    hop = [vm((c, slots), (s[0] // n_d, s[1] // 2)) for c, s in zip(counts[:3], shapes[:3])]
-    hop.append(vm((trees, slots), (shapes[3][0] // n_d, shapes[3][1])))
-    far = [vm((c,), (s[0] // n_d, s[1])) for c, s in zip([chips - 1] * 3 + [trees], shapes)]
-    full = [vm((), s) for s in shapes]
-    n_units = 3 * chips + trees
+    part = (shapes[3][0] // n_d, shapes[3][1])
     partners = 1 + bits
     return pl.pallas_call(
         functools.partial(finish_kernel, n_d, n_t),
-        in_specs=[VMEM] * 5 + [any_] * 4,
+        in_specs=[VMEM] * 8 + [HBM],
         out_specs=[VMEM] * 6,
         out_shape=[sds(x.shape, bf16), sds((8, wide), f32)] + [sds(s, f32) for s in shapes],
-        scratch_shapes=mine + side + hop + far + full + [
+        scratch_shapes=[vm((trees,), shapes[3]), vm((trees, n_d - 1), part), vm((trees,), part)]
+        + [vm((), s) for s in shapes] + [
             vm((chips, rows), (wide,)), vm((chips - 1, rows), (wide,)), vm((chips - 1, rows), (wide,)),
             vm((8,), (wide,), f32), vm((2 * partners, 8), (wide,), f32), vm((chips, 8), (wide,), f32),
-            dma((n_units,)), dma((n_units,)), dma((n_units,)),
-            dma((n_units, slots)), dma((n_units, slots)),
-            dma((3, chips - 1)), dma((3, chips - 1)),
+            dma((trees,)), dma((trees, n_d - 1)), dma((trees, n_d - 1)),
             dma((4, n_d - 1)), dma((4, n_d - 1)),
             dma((trees,)), dma((trees,)),
             dma((chips - 1,)), dma((chips - 1,)), dma((chips,)), dma((chips,)),
@@ -1074,7 +1173,9 @@
             collective_id=3, has_side_effects=True, vmem_limit_bytes=67043328
         ),
         name="finish",
-    )(partial, x, hidden, par, vec, up_g, down_g, out_g, in_g)
+    )(partial, x, hidden, par, vec, up_t, down_t, out_t, in_g)
+
+
 def shards(
     n_d, n_t,
     tokens, cotangent, lengths, parents, first_gain, first_shift, in_weight, out_weight,
@@ -1104,15 +1205,17 @@
     output, back_hidden, back_att, up_g, down_g, out_g, vec = feed(
         flat(att), flat(tokens), flat(cotangent), out_all.reshape(-1, wide), par, up_all, down_all
     )
-    d_heads = exchange_heads(n_t, trees, back_att.reshape(trees, rows, wide))
-    back_mixed = attend_back(qb, k, v, kt, d_heads, attended, cosine, sine)
+    back_mixed, up_t, down_t, out_t = attend_back(
+        n_d, n_t, qb, k, v, kt, back_att.reshape(trees, rows, wide), attended, cosine, sine,
+        up_g, down_g, out_g.reshape(n_t, width, wide),
+    )
     w_flat = w.transpose(1, 0, 2).reshape(wide, -1)
     partial = lax.dot_general(back_mixed, w_flat, NT, preferred_element_type=f32).astype(bf16)
     in_part = lax.dot_general(gathered, back_mixed, TN, preferred_element_type=f32)
     in_part = in_part.astype(bf16).reshape(wide, 3, trees, width).transpose(2, 1, 0, 3)
     back_tokens, vec, up_sum, down_sum, out_sum, in_sum = finish(
         n_d, n_t, partial, tokens, back_hidden.reshape(x.shape), par, vec,
-        up_g, down_g, out_g.reshape(n_t, width, wide), in_part.reshape(trees, 3 * wide, width),
+        up_t, down_t, out_t, in_part.reshape(trees, 3 * wide, width),
     )
     return (
         output.reshape(tokens.shape),

time: 526 us -> 499 us (0.949); the launches traced: 525 us -> 492 us
  Pallas kernels: 481 us -> 445 us
    pallas_call x1, Pallas kernels: 152 us -> 87.7 us  [finish(): pl.pallas_call(functools.partial(finish_kernel, n_d, n_t), in_specs=[VMEM...]
    pallas_call x2 -> x1, Pallas kernels: 85.8 us -> 115 us  [attend_back(): pl.pallas_call(functools.partial(bwd_kernel, n_d, n_t), grid=(rows // BLO...]
where the time goes in v4:
time: 499 us; the launch traced here: 492 us
  Pallas kernels  445 us (89%)
  local copies, waits for them, and re-layouts  18.2 us (4%)
  matrix products  13.8 us (3%)
  other arithmetic  13.4 us (3%)
    pallas_call x1, Pallas kernels, attend_back(): pl.pallas_call(functools.partial(bwd_kernel, n_d, n_t), grid=(rows // BLO...  115 us
    pallas_call x1, Pallas kernels, gather_tree(): pl.pallas_call(functools.partial(gather_kernel, n_d, n_t), in_specs=[VMEM...  102 us
    pallas_call x1, Pallas kernels, finish(): pl.pallas_call(functools.partial(finish_kernel, n_d, n_t), in_specs=[VMEM...  87.7 us
    pallas_call x1, Pallas kernels, attend(): pl.pallas_call(functools.partial(fwd_kernel, n_d, n_t, trees), grid=(rows...  76 us
    pallas_call x1, Pallas kernels, feed(): pl.pallas_call(feed_kernel, grid=(2, n_t), in_specs=[one(a) for a in (att...  52.4 us
    pallas_call x1, Pallas kernels, project(): pl.pallas_call(qkv_kernel, grid=(rows // BLOCK,), in_specs=[pl.BlockSpec(...  12.6 us

profile of v4, /device:TPU:0, one launch (start us, length us, event | category | flops | bytes accessed | tf_op | source)
XLA Modules:
  0.0 492.3 jit_solution(15876049216264131197)
XLA Ops:
  0.8 0.8 dynamic-slice_bitcast_fusion.1
  1.5 0.7 dynamic-slice_bitcast_fusion
  2.3 0.2 reduce-window.7
  2.6 1.4 convert_reduce_fusion
  4.0 1.6 fusion.2
  5.7 0.1 convert_reduce_fusion.1
  5.8 0.1 select_reduce_fusion.3
  5.9 0.1 select_reduce_fusion
  6.1 0.7 stack.35.par_ref
  6.8 1.4 fusion.5.x_ref
  8.2 2.6 fusion.11
  10.9 5.5 %fusion.6 = (f32[2048,128]{1,0:T(8,128)}, f32[2048,128]{1,0:T(8,128)}) fusion(f32[128]{0:T(128)S(1)} %get-tuple-element.94, f32[128]{0:T(128)S(1)} %get-tuple-element.95, f32[2048]{0:T(1024)S(1)} %add_convert_fusion), kind=kLoop, calls=%fused_computation.15 | loop fusion | flops 524288 | bytes 2106368 | tf_op jit(solution)/shard_map/mul | solution.py:83
  16.4 101.8 %gather_tree.1 = (bf16[2048,1024]{1,0:T(8,128)(2,1)}, bf16[2,3,1024,128]{3,2,1,0:T(8,128)(2,1)}, bf16[8,512,1024]{2,1,0:T(8,128)(2,1)}) custom-call(bf16[2,256,1024]{2,1,0:T(8,128)(2,1)} %fusion.5.x_ref, bf16[3,1024,128]{2,1,0:T(8,128)(2,1)} %bitcast.66, bf16[512,1024]{1,0:T(8,128)(2,1)} %f_ref.1), custom_call_target="tpu_custom_call" | custom-call | tf_op jit(solution)/shard_map/gather_tree/pallas_call | solution.py:351
  118.3 2.8 fusion.17
  121.0 1.8 copy.36
  122.8 12.6 %project.1 = (bf16[4,2048,128]{2,1,0:T(8,128)(2,1)}, bf16[4,2048,128]{2,1,0:T(8,128)(2,1)}, bf16[4,2048,128]{2,1,0:T(8,128)(2,1)}, bf16[4,64,2048]{2,1,0:T(8,128)(2,1)}, bf16[4,80,2048]{2,1,0:T(8,128)(2,1)}) custom-call(bf16[2048,1024]{1,0:T(8,128)(2,1)} %get-tuple-element.44.x_ref, bf16[3,1024,256]{2,1,0:T(8,128)(2,1)} %get-tuple-element.79.w_ref, ...), custom_call_target="tpu_custom_call" | custom-call | tf_op jit(solution)/shard_map/project/pallas_call | solution.py:414
  135.5 76.0 %attend.1 = (bf16[2048,256]{1,0:T(8,128)(2,1)}, bf16[4,2048,128]{2,1,0:T(8,128)(2,1)}, bf16[2,256,1024]{2,1,0:T(8,128)(2,1)}, bf16[8,128,1024]{2,1,0:T(8,128)(2,1)}, bf16[8,1024,512]{2,1,0:T(8,128)(2,1)}) custom-call(bf16[4,2048,128]{2,1,0:T(8,128)(2,1)} %get-tuple-element.46.q_ref, bf16[4,2048,128]{2,1,0:T(8,128)(2,1)} %get-tuple-element.47.k_ref, ...), custom_call_target="tpu_custom_call" | custom-call | tf_op jit(solution)/shard_map/attend/pallas_call | solution.py:541
  211.4 52.4 %feed.1 = (bf16[512,1024]{1,0:T(8,128)(2,1)}, f32[512,1024]{1,0:T(8,128)}, bf16[512,1024]{1,0:T(8,128)(2,1)}, bf16[8,1024,512]{2,1,0:T(8,128)(2,1)}, bf16[8,512,...) custom-call(bf16[512,1024]{1,0:T(8,128)(2,1)} %bitcast.64, bf16[512,1024]{1,0:T(8,128)(2,1)} %bitcast.55, ...), custom_call_target="tpu_custom_call" | custom-call | tf_op jit(solution)/shard_map/feed/pallas_call | solution.py:938
  263.9 114.9 %attend_back.1 = (bf16[2048,768]{1,0:T(8,128)(2,1)}, bf16[256,512]{1,0:T(8,128)(2,1)}, bf16[128,1024]{1,0:T(8,128)(2,1)}, bf16[32,1024]{1,0:T(8,128)(2,1)}) custom-call(bf16[4,2048,128]{2,1,0:T(8,128)(2,1)} %get-tuple-element.54.q_ref, bf16[4,2048,128]{2,1,0:T(8,128)(2,1)} %get-tuple-element.47.k_ref, bf16[4,2048,128]{2,1,0:T(8,128)(2,1)} %get-tuple-element.55.v_ref, ...), custom_call_target="tpu_custom_call" | custom-call | tf_op jit(solution)/shard_map/attend_back/pallas_call | solution.py:825
  378.8 6.6 %convolution_convert_fusion.1 = bf16[1024,768]{0,1:T(8,128)(2,1)S(1)} fusion(bf16[2048,1024]{1,0:T(8,128)(2,1)} %get-tuple-element.44.x_ref, bf16[2048,768]{1,0:T(8,128)(2,1)} %get-tuple-element.62), kind=kOutput, calls=%fused_computation.9 | convolution fusion | flops 3222011904 | bytes 8912896 | tf_op jit(solution)/shard_map/dot_general | solution.py:1214
  385.4 1.6 copy.37
  387.0 7.2 %convolution_convert_fusion.sum_ref = bf16[2048,1024]{1,0:T(8,128)(2,1)} fusion(bf16[2048,768]{1,0:T(8,128)(2,1)} %get-tuple-element.62, bf16[1024,768]{0,1:T(8,128)(2,1)S(1)} %bitcast.60), kind=kOutput, calls=%fused_computation | convolution fusion | flops 3223322624 | bytes 8912896 | tf_op jit(solution)/shard_map/dot_general | solution.py:1213
  394.2 87.7 %finish.1 = (bf16[2,256,1024]{2,1,0:T(8,128)(2,1)}, f32[8,1024]{1,0:T(8,128)}, f32[1024,512]{1,0:T(8,128)}, f32[512,1024]{1,0:T(8,128)}, f32[128,1024]{1,0:T(8,128)}, /*index=5*/f32[3072,128]{1,0:T(8,128)}) custom-call(bf16[2048,1024]{1,0:T(8,128)(2,1)} %convolution_convert_fusion.sum_ref, bf16[2,256,1024]{2,1,0:T(8,128)(2,1)} %x_ref.1, ...), custom_call_target="tpu_custom_call" | custom-call | tf_op jit(solution)/shard_map/finish/pallas_call | solution.py:1157
  481.9 1.7 fusion.18
  483.6 2.3 copy.47
  485.9 1.1 copy.48
  487.0 0.2 copy-done.5
  487.2 0.8 copy.49
  488.0 0.2 copy-done.2
  488.2 1.3 copy.50
  489.5 1.0 copy-done.1
  490.5 1.3 copy.51
  (33 shorter events, 0.2 us)
Async XLA Ops:
  0.7 6.2 %copy-start = (bf16[2,256,1024]{2,1,0:T(8,128)(2,1)S(1)}, bf16[2,256,1024]{2,1,0:T(8,128)(2,1)}, u32[]{:S(2)}) copy-start(bf16[2,256,1024]{2,1,0:T(8,128)(2,1)} %x_ref.1) | copy-start | bytes 3145732
  0.7 5.4 %copy-start.6 = (f32[1024]{0:T(1024)S(1)}, f32[1024]{0:T(1024)}, u32[]{:S(2)}) copy-start(f32[1024]{0:T(1024)} %param.21) | copy-start | bytes 12292
  0.7 5.4 %copy-start.7 = (f32[1024]{0:T(1024)S(1)}, f32[1024]{0:T(1024)}, u32[]{:S(2)}) copy-start(f32[1024]{0:T(1024)} %param.20) | copy-start | bytes 12292
  0.7 5.4 %copy-start.13 = (f32[1024]{0:T(1024)S(1)}, f32[1024]{0:T(1024)}, u32[]{:S(2)}) copy-start(f32[1024]{0:T(1024)} %param.31) | copy-start | bytes 12292
  0.7 5.4 %copy-start.12 = (f32[1024]{0:T(1024)S(1)}, f32[1024]{0:T(1024)}, u32[]{:S(2)}) copy-start(f32[1024]{0:T(1024)} %param.30) | copy-start | bytes 12292
  0.7 5.4 %copy-start.11 = (f32[1024]{0:T(1024)S(1)}, f32[1024]{0:T(1024)}, u32[]{:S(2)}) copy-start(f32[1024]{0:T(1024)} %param.27) | copy-start | bytes 12292
  0.7 5.4 %copy-start.10 = (f32[1024]{0:T(1024)S(1)}, f32[1024]{0:T(1024)}, u32[]{:S(2)}) copy-start(f32[1024]{0:T(1024)} %param.26) | copy-start | bytes 12292
  0.7 5.4 %copy-start.9 = (f32[1024]{0:T(1024)S(1)}, f32[1024]{0:T(1024)}, u32[]{:S(2)}) copy-start(f32[1024]{0:T(1024)} %param.25) | copy-start | bytes 12292
  0.7 5.4 %copy-start.8 = (f32[1024]{0:T(1024)S(1)}, f32[1024]{0:T(1024)}, u32[]{:S(2)}) copy-start(f32[1024]{0:T(1024)} %param.24) | copy-start | bytes 12292
  385.4 1.6 copy-start.3
  481.9 4.0 copy-start.4
  485.9 1.4 copy-start.5
  485.9 2.3 copy-start.2
  488.2 2.3 copy-start.1

commit v5 on v4

--- a/solution.py
+++ b/solution.py
@@ -270,7 +270,10 @@
             self.mine(a, True).wait_recv()
 
 
-def gather_kernel(n_d, n_t, x_ref, w_ref, f_ref, o_ref, u_ref, all_ref, rs, ss, rb, sb, rw, sw, rp, sp, *sems):
+def gather_kernel(
+    n_d, n_t, x_ref, w_ref, f_ref, o_ref, u_ref, all_ref,
+    passing, rs, ss, rb, sb, rw, sw, rp, sp, *sems,
+):
     d, t = lax.axis_index("dp"), lax.axis_index("tensor")
     trees, rows, _ = x_ref.shape
     chips = n_t // 2
@@ -279,12 +282,13 @@
     other = 2 * chip + 1 - core
     near = group // 2
     tree = t // group
-    line = [lax.rem(chip + k, chips) for k in range(1, chips)]
     planes = [lax.rem(d + k, n_d) for k in range(1, n_d)]
     owners = [(j * group + t // trees) for j in range(trees)]
     givers = [lax.rem(t, group) * trees + i for i in range(trees)]
     barrier([(d, lax.rem(t + k, n_t)) for k in range(1, n_t)] + [(p, t) for p in planes])
     part = w_ref.shape[1] // n_d
+    weights = Spread(n_d, n_t, [f_ref], [all_ref], sems)
+    exists = weights.exists
 
     copies = []
     mine = w_ref.at[:, span(d, part), :]
@@ -299,15 +303,68 @@
         def _():
             u_ref[lax.rem(t, trees), :, span(d, part), :] = w_ref[:, span(d, part), :]
 
-    def block(c, k):
-        return o_ref.at[span(2 * c + k, rows)]
-
-    for k, c in enumerate(line):
-        copies.append(send(x_ref.at[c // near], block(chip, core), ss.at[k], rs.at[k], (d, 2 * c + core)))
-    weights = Spread(n_d, n_t, [f_ref], [all_ref], sems)
     weights.begin()
+
+    def block(c):
+        return o_ref.at[span(2 * c + core, rows)]
+
+    def beyond(c, way, j):
+        return (j * near + near - 1 >= c) if way > 0 else (j * near <= c)
+
+    def hop(way, h, j, here):
+        source = chip - way * (h - 1)
+        if h == 1:
+            src = x_ref.at[j]
+        else:
+            src = block(source) if here else passing.at[j, source]
+        return src, source
+
+    def pass_on(way, h):
+        for j in range(trees):
+
+            @pl.when(exists(chip - way * (h - 1)) & exists(chip + way) & beyond(chip + way, way, j))
+            def _():
+                i = weights.slot(way, h)
+                to = chip + way
+                for here in (True, False) if h > 1 else (True,):
+                    src, source = hop(way, h, j, here)
+                    for there in (True, False):
+                        at_home = (tree == j) if here else (tree != j)
+                        lands = (to // near == j) if there else (to // near != j)
+
+                        @pl.when((at_home & lands) if h > 1 else lands)
+                        def _():
+                            dst = block(source) if there else passing.at[j, source]
+                            send(src, dst, ss.at[j, i], rs.at[j, i], (d, 2 * to + core))
+
+    def row_copy(j, i):
+        return weights.remote(x_ref.at[j], passing.at[j, 0], ss.at[j, i], rs.at[j, i], (d, other))
+
+    def share(way, h):
+        source = chip - way * h
+        i = weights.slot(way, h)
+        return weights.remote(block(source), block(source), sb.at[i], rb.at[i], (d, other))
+
+    def arrive(way, h):
+        for j in range(trees):
+
+            @pl.when(exists(chip - way * h) & beyond(chip, way, j))
+            def _():
+                row_copy(j, weights.slot(way, h)).wait_recv()
+
+        if h < chips - 1:
+            pass_on(way, h + 1)
+
+        @pl.when(exists(chip - way * h))
+        def _():
+            share(way, h).start()
+
+    for way in (1, -1):
+        pass_on(way, 1)
     o_ref[span(t, rows), :] = x_ref[tree]
-    copies.append(send(x_ref.at[tree], block(chip, core), sb.at[chips - 1], rb.at[chips - 1], (d, other)))
+    last = 2 * (chips - 1)
+    copies.append(send(x_ref.at[tree], block(chip), sb.at[last], rb.at[last], (d, other)))
+    weights.group(0)
     for i in range(trees):
         slot = u_ref.at[i, :, span(d, part), :]
 
@@ -321,11 +378,11 @@
     mine_all = u_ref.at[:, :, span(d, part), :]
     for k, p in enumerate(planes):
         copies.append(send(mine_all, mine_all, sp.at[k], rp.at[k], (p, t)))
-    for k in range(chips - 1):
-        source = lax.rem(chip + chips - 1 - k, chips)
-        copies[k].wait_recv()
-        copies.append(send(block(source, core), block(source, core), sb.at[k], rb.at[k], (d, other)))
-    for g in range(weights.groups()):
+    for h in range(1, chips):
+        for way in (1, -1):
+            arrive(way, h)
+        weights.group(h)
+    for g in range(chips, weights.groups()):
         weights.group(g)
     weights.end()
     for j in range(trees):
@@ -337,16 +394,26 @@
                 device_id=(d, owners[j]), device_id_type=MESH,
             ).wait_send()
 
-    for i, copy in enumerate(copies):
-        if i < chips - 1:
-            copy.wait_send()
-        else:
-            copy.wait()
+    for way in (1, -1):
+        for h in range(1, chips):
+            for j in range(trees):
+
+                @pl.when(exists(chip - way * (h - 1)) & exists(chip + way) & beyond(chip + way, way, j))
+                def _():
+                    row_copy(j, weights.slot(way, h)).wait_send()
+
+            @pl.when(exists(chip - way * h))
+            def _():
+                share(way, h).wait()
+
+    for copy in copies:
+        copy.wait()
 
 
 def gather_tree(n_d, n_t, normed, weight, down):
     trees, rows, wide = normed.shape
     chips = n_t // 2
+    hops = 2 * (chips - 1)
     dma = pltpu.SemaphoreType.DMA
     return pl.pallas_call(
         functools.partial(gather_kernel, n_d, n_t),
@@ -358,7 +425,8 @@
             jax.ShapeDtypeStruct((n_t,) + down.shape, bf16),
         ],
         scratch_shapes=[
-            dma((chips - 1,)), dma((chips - 1,)), dma((chips,)), dma((chips,)),
+            pltpu.VMEM((trees, chips, rows, wide), bf16),
+            dma((trees, hops)), dma((trees, hops)), dma((hops + 1,)), dma((hops + 1,)),
             dma((trees,)), dma((trees,)), dma((n_d - 1,)), dma((n_d - 1,)),
         ] + Spread.sems(1, n_d, n_t),
         compiler_params=pltpu.CompilerParams(collective_id=0, has_side_effects=True),
@@ -435,9 +503,9 @@
 
 def fwd_kernel(
     n_d, n_t, trees, q_ref, k_ref, vt_ref, ow_ref, up_ref, o_ref, qb_ref, att_ref, ow_all, up_all,
-    kept, ss, rs, here, *sems,
+    ss, rs, here, *sems,
 ):
-    qi = pl.program_id(0)
+    turn = pl.program_id(0)
     steps = pl.num_programs(0)
     heads = q_ref.shape[0]
     row, col = row_of((BLOCK, BLOCK)), lane_of((BLOCK, BLOCK))
@@ -445,17 +513,19 @@
     group = n_t // trees
     rows, width = att_ref.shape[1], o_ref.shape[1]
     per = BLOCK // rows
+    qi = jnp.where(turn == steps - 1, t // per, jnp.where(turn >= t // per, turn + 1, turn))
+    at = span(qi, BLOCK)
     weights = Spread(n_d, n_t, [up_ref, ow_ref], [up_all, ow_all], sems)
     first_group = max(0, k_ref.shape[1] // BLOCK - 4)
     place = att_ref.at[t // group, :, span(lax.rem(t, group), width)]
 
     def outgoing(i, r, k):
         return pltpu.make_async_remote_copy(
-            src_ref=kept.at[i, pl.ds(r * rows, rows)], dst_ref=place, send_sem=ss.at[k], recv_sem=rs.at[k],
+            src_ref=o_ref.at[span(i * per + r, rows)], dst_ref=place, send_sem=ss.at[k], recv_sem=rs.at[k],
             device_id=(d, lax.rem(t + k, n_t)), device_id_type=MESH,
         )
 
-    @pl.when(qi == 0)
+    @pl.when(turn == 0)
     def _():
         barrier(
             [(d, lax.rem(t + k, n_t)) for k in range(1, n_t)] + [(lax.rem(d + k, n_d), t) for k in range(1, n_d)]
@@ -465,11 +535,11 @@
     for g in range(weights.groups()):
         if first_group + g < k_ref.shape[1] // BLOCK:
 
-            @pl.when(qi == first_group + g)
+            @pl.when(turn == first_group + g)
             def _():
                 weights.group(g)
 
-    qs = [q_ref[h] for h in range(heads)]
+    qs = [q_ref[h, at, :] for h in range(heads)]
 
     def scores(h, j):
         return dot(k_ref[h, span(j, BLOCK), :], qs[h], NT)
@@ -502,13 +572,11 @@
             outs.append(acc[:HEAD_DIM] / total)
             a, b, c = split3(-(m + jnp.log(total)))
             extra = jnp.where(r == 80, a, jnp.where(r == 81, b, jnp.where(r == 82, c, 0.0))).T
-            qb_ref[g] = qs[g] + extra.astype(bf16)
-        slab = jnp.concatenate(outs, axis=0).T.astype(bf16)
-        o_ref[:, h * HEAD_DIM : (h + 2) * HEAD_DIM] = slab
-        kept[qi, :, h * HEAD_DIM : (h + 2) * HEAD_DIM] = slab
+            qb_ref[g, at, :] = qs[g] + extra.astype(bf16)
+        o_ref[at, h * HEAD_DIM : (h + 2) * HEAD_DIM] = jnp.concatenate(outs, axis=0).T.astype(bf16)
 
     def local(r):
-        return pltpu.make_async_copy(kept.at[t // per, pl.ds(r * rows, rows)], place, here.at[0])
+        return pltpu.make_async_copy(o_ref.at[span(t // per * per + r, rows)], place, here.at[0])
 
     for r in range(per):
         k = lax.rem(qi * per + r + n_t - t, n_t)
@@ -521,7 +589,7 @@
         def _():
             local(r).start()
 
-    @pl.when(qi == steps - 1)
+    @pl.when(turn == steps - 1)
     def _():
         for g in range(k_ref.shape[1] // BLOCK - first_group, weights.groups()):
             weights.group(g)
@@ -533,16 +601,14 @@
 
 def attend(n_d, n_t, trees, q, k, vt, ow, up):
     heads, rows, _ = q.shape
-    slab = pl.BlockSpec((heads, rows, LANES), lambda i: (0, 0, 0))
-    block = pl.BlockSpec((heads, BLOCK, LANES), lambda i: (0, i, 0))
     wide = heads * HEAD_DIM
     dma = pltpu.SemaphoreType.DMA
     sds = jax.ShapeDtypeStruct
     return pl.pallas_call(
         functools.partial(fwd_kernel, n_d, n_t, trees),
         grid=(rows // BLOCK,),
-        in_specs=[block, slab, pl.BlockSpec((heads, VROWS, rows), lambda i: (0, 0, 0)), VMEM, VMEM],
-        out_specs=[pl.BlockSpec((BLOCK, wide), lambda i: (i, 0)), block, HBM, HBM, HBM],
+        in_specs=[VMEM] * 5,
+        out_specs=[VMEM, VMEM, HBM, HBM, HBM],
         out_shape=[
             sds((rows, wide), bf16),
             sds(q.shape, bf16),
@@ -551,7 +617,7 @@
             sds((n_t,) + up.shape, bf16),
         ],
         scratch_shapes=[
-            pltpu.VMEM((rows // BLOCK, BLOCK, wide), bf16), dma((n_t,)), dma((n_t,)), dma((1,)),
+            dma((n_t,)), dma((n_t,)), dma((1,)),
         ] + Spread.sems(2, n_d, n_t),
         compiler_params=pltpu.CompilerParams(collective_id=1, has_side_effects=True),
         name="attend",

time: 499 us -> 484 us (0.970)
  Pallas kernels: 445 us -> 430 us
    pallas_call x1, Pallas kernels: 102 us -> 84.6 us  [gather_tree(): pl.pallas_call(functools.partial(gather_kernel, n_d, n_t), in_specs=[VMEM...]
    pallas_call x1, Pallas kernels: 87.7 us -> 93.7 us  [finish(): pl.pallas_call(functools.partial(finish_kernel, n_d, n_t), in_specs=[VMEM...]
where the time goes in v5:
time: 484 us; the launch traced here: 477 us
  Pallas kernels  430 us (89%)
  local copies, waits for them, and re-layouts  18.2 us (4%)
  matrix products  13.8 us (3%)
  other arithmetic  13.4 us (3%)
    pallas_call x1, Pallas kernels, attend_back(): pl.pallas_call(functools.partial(bwd_kernel, n_d, n_t), grid=(rows // BLO...  112 us
    pallas_call x1, Pallas kernels, finish(): pl.pallas_call(functools.partial(finish_kernel, n_d, n_t), in_specs=[VMEM...  93.7 us
    pallas_call x1, Pallas kernels, gather_tree(): pl.pallas_call(functools.partial(gather_kernel, n_d, n_t), in_specs=[VMEM...  84.6 us
    pallas_call x1, Pallas kernels, attend(): pl.pallas_call(functools.partial(fwd_kernel, n_d, n_t, trees), grid=(rows...  74.9 us
    pallas_call x1, Pallas kernels, feed(): pl.pallas_call(feed_kernel, grid=(2, n_t), in_specs=[one(a) for a in (att...  52.4 us
    pallas_call x1, Pallas kernels, project(): pl.pallas_call(qkv_kernel, grid=(rows // BLOCK,), in_specs=[pl.BlockSpec(...  12.6 us

profile of v5, /device:TPU:0, one launch (start us, length us, event | category | flops | bytes accessed | tf_op | source)
XLA Modules:
  0.0 476.6 jit_solution(6948275228294974623)
XLA Ops:
  0.8 0.8 dynamic-slice_bitcast_fusion.1
  1.5 0.7 dynamic-slice_bitcast_fusion
  2.3 0.2 reduce-window.7
  2.6 1.4 convert_reduce_fusion
  4.0 1.6 fusion.2
  5.7 0.1 convert_reduce_fusion.1
  5.8 0.1 select_reduce_fusion.3
  5.9 0.1 select_reduce_fusion
  6.1 0.7 stack.35.par_ref
  6.8 1.4 fusion.5.x_ref
  8.2 2.6 fusion.11
  10.9 5.5 %fusion.6 = (f32[2048,128]{1,0:T(8,128)}, f32[2048,128]{1,0:T(8,128)}) fusion(f32[128]{0:T(128)S(1)} %get-tuple-element.94, f32[128]{0:T(128)S(1)} %get-tuple-element.95, f32[2048]{0:T(1024)S(1)} %add_convert_fusion), kind=kLoop, calls=%fused_computation.15 | loop fusion | flops 524288 | bytes 2106368 | tf_op jit(solution)/shard_map/mul | solution.py:83
  16.4 84.6 %gather_tree.1 = (bf16[2048,1024]{1,0:T(8,128)(2,1)}, bf16[2,3,1024,128]{3,2,1,0:T(8,128)(2,1)}, bf16[8,512,1024]{2,1,0:T(8,128)(2,1)}) custom-call(bf16[2,256,1024]{2,1,0:T(8,128)(2,1)} %fusion.5.x_ref, bf16[3,1024,128]{2,1,0:T(8,128)(2,1)} %bitcast.66, bf16[512,1024]{1,0:T(8,128)(2,1)} %f_ref.1), custom_call_target="tpu_custom_call" | custom-call | tf_op jit(solution)/shard_map/gather_tree/pallas_call | solution.py:418
  101.0 2.8 fusion.17
  103.8 1.8 copy.36
  105.5 12.6 %project.1 = (bf16[4,2048,128]{2,1,0:T(8,128)(2,1)}, bf16[4,2048,128]{2,1,0:T(8,128)(2,1)}, bf16[4,2048,128]{2,1,0:T(8,128)(2,1)}, bf16[4,64,2048]{2,1,0:T(8,128)(2,1)}, bf16[4,80,2048]{2,1,0:T(8,128)(2,1)}) custom-call(bf16[2048,1024]{1,0:T(8,128)(2,1)} %get-tuple-element.44.x_ref, bf16[3,1024,256]{2,1,0:T(8,128)(2,1)} %get-tuple-element.79.w_ref, ...), custom_call_target="tpu_custom_call" | custom-call | tf_op jit(solution)/shard_map/project/pallas_call | solution.py:482
  118.2 74.9 %attend.1 = (bf16[2048,256]{1,0:T(8,128)(2,1)}, bf16[4,2048,128]{2,1,0:T(8,128)(2,1)}, bf16[2,256,1024]{2,1,0:T(8,128)(2,1)}, bf16[8,128,1024]{2,1,0:T(8,128)(2,1)}, bf16[8,1024,512]{2,1,0:T(8,128)(2,1)}) custom-call(bf16[4,2048,128]{2,1,0:T(8,128)(2,1)} %get-tuple-element.46.q_ref, bf16[4,2048,128]{2,1,0:T(8,128)(2,1)} %get-tuple-element.47.k_ref, ...), custom_call_target="tpu_custom_call" | custom-call | tf_op jit(solution)/shard_map/attend/pallas_call | solution.py:607
  193.1 52.4 %feed.1 = (bf16[512,1024]{1,0:T(8,128)(2,1)}, f32[512,1024]{1,0:T(8,128)}, bf16[512,1024]{1,0:T(8,128)(2,1)}, bf16[8,1024,512]{2,1,0:T(8,128)(2,1)}, bf16[8,512,...) custom-call(bf16[512,1024]{1,0:T(8,128)(2,1)} %bitcast.64, bf16[512,1024]{1,0:T(8,128)(2,1)} %bitcast.55, ...), custom_call_target="tpu_custom_call" | custom-call | tf_op jit(solution)/shard_map/feed/pallas_call | solution.py:1004
  245.5 111.5 %attend_back.1 = (bf16[2048,768]{1,0:T(8,128)(2,1)}, bf16[256,512]{1,0:T(8,128)(2,1)}, bf16[128,1024]{1,0:T(8,128)(2,1)}, bf16[32,1024]{1,0:T(8,128)(2,1)}) custom-call(bf16[4,2048,128]{2,1,0:T(8,128)(2,1)} %get-tuple-element.54.q_ref, bf16[4,2048,128]{2,1,0:T(8,128)(2,1)} %get-tuple-element.47.k_ref, bf16[4,2048,128]{2,1,0:T(8,128)(2,1)} %get-tuple-element.55.v_ref, ...), custom_call_target="tpu_custom_call" | custom-call | tf_op jit(solution)/shard_map/attend_back/pallas_call | solution.py:891
  357.0 6.6 %convolution_convert_fusion.1 = bf16[1024,768]{0,1:T(8,128)(2,1)S(1)} fusion(bf16[2048,1024]{1,0:T(8,128)(2,1)} %get-tuple-element.44.x_ref, bf16[2048,768]{1,0:T(8,128)(2,1)} %get-tuple-element.62), kind=kOutput, calls=%fused_computation.9 | convolution fusion | flops 3222011904 | bytes 8912896 | tf_op jit(solution)/shard_map/dot_general | solution.py:1280
  363.7 1.6 copy.37
  365.2 7.2 %convolution_convert_fusion.sum_ref = bf16[2048,1024]{1,0:T(8,128)(2,1)} fusion(bf16[2048,768]{1,0:T(8,128)(2,1)} %get-tuple-element.62, bf16[1024,768]{0,1:T(8,128)(2,1)S(1)} %bitcast.60), kind=kOutput, calls=%fused_computation | convolution fusion | flops 3223322624 | bytes 8912896 | tf_op jit(solution)/shard_map/dot_general | solution.py:1279
  372.4 93.7 %finish.1 = (bf16[2,256,1024]{2,1,0:T(8,128)(2,1)}, f32[8,1024]{1,0:T(8,128)}, f32[1024,512]{1,0:T(8,128)}, f32[512,1024]{1,0:T(8,128)}, f32[128,1024]{1,0:T(8,128)}, /*index=5*/f32[3072,128]{1,0:T(8,128)}) custom-call(bf16[2048,1024]{1,0:T(8,128)(2,1)} %convolution_convert_fusion.sum_ref, bf16[2,256,1024]{2,1,0:T(8,128)(2,1)} %x_ref.1, ...), custom_call_target="tpu_custom_call" | custom-call | tf_op jit(solution)/shard_map/finish/pallas_call | solution.py:1223
  466.2 1.7 fusion.18
  467.9 2.3 copy.47
  470.1 1.1 copy.48
  471.3 0.2 copy-done.5
  471.5 0.8 copy.49
  472.3 0.2 copy-done.2
  472.5 1.3 copy.50
  473.8 1.0 copy-done.1
  474.8 1.3 copy.51
  (33 shorter events, 0.2 us)
Async XLA Ops:
  0.7 6.2 %copy-start = (bf16[2,256,1024]{2,1,0:T(8,128)(2,1)S(1)}, bf16[2,256,1024]{2,1,0:T(8,128)(2,1)}, u32[]{:S(2)}) copy-start(bf16[2,256,1024]{2,1,0:T(8,128)(2,1)} %x_ref.1) | copy-start | bytes 3145732
  0.7 5.4 %copy-start.6 = (f32[1024]{0:T(1024)S(1)}, f32[1024]{0:T(1024)}, u32[]{:S(2)}) copy-start(f32[1024]{0:T(1024)} %param.21) | copy-start | bytes 12292
  0.7 5.4 %copy-start.7 = (f32[1024]{0:T(1024)S(1)}, f32[1024]{0:T(1024)}, u32[]{:S(2)}) copy-start(f32[1024]{0:T(1024)} %param.20) | copy-start | bytes 12292
  0.7 5.4 %copy-start.13 = (f32[1024]{0:T(1024)S(1)}, f32[1024]{0:T(1024)}, u32[]{:S(2)}) copy-start(f32[1024]{0:T(1024)} %param.31) | copy-start | bytes 12292
  0.7 5.4 %copy-start.12 = (f32[1024]{0:T(1024)S(1)}, f32[1024]{0:T(1024)}, u32[]{:S(2)}) copy-start(f32[1024]{0:T(1024)} %param.30) | copy-start | bytes 12292
  0.7 5.4 %copy-start.11 = (f32[1024]{0:T(1024)S(1)}, f32[1024]{0:T(1024)}, u32[]{:S(2)}) copy-start(f32[1024]{0:T(1024)} %param.27) | copy-start | bytes 12292
  0.7 5.4 %copy-start.10 = (f32[1024]{0:T(1024)S(1)}, f32[1024]{0:T(1024)}, u32[]{:S(2)}) copy-start(f32[1024]{0:T(1024)} %param.26) | copy-start | bytes 12292
  0.7 5.4 %copy-start.9 = (f32[1024]{0:T(1024)S(1)}, f32[1024]{0:T(1024)}, u32[]{:S(2)}) copy-start(f32[1024]{0:T(1024)} %param.25) | copy-start | bytes 12292
  0.7 5.4 %copy-start.8 = (f32[1024]{0:T(1024)S(1)}, f32[1024]{0:T(1024)}, u32[]{:S(2)}) copy-start(f32[1024]{0:T(1024)} %param.24) | copy-start | bytes 12292
  363.7 1.6 copy-start.3
  466.2 4.0 copy-start.4
  470.1 1.4 copy-start.5
  470.1 2.3 copy-start.2
  472.5 2.3 copy-start.1

commit v6 on v5

--- a/solution.py
+++ b/solution.py
@@ -135,6 +135,17 @@
     return masks
 
 
+def halves(rows, width, tile=16):
+    return (rows // 2, width) if rows % (2 * tile) == 0 else (rows, width // 2)
+
+
+def half(part, stream, rows, width):
+    height, wide = halves(rows, width)
+    if height < rows:
+        return span(2 * part + stream, height), slice(None)
+    return span(part, rows), pl.ds(stream * wide, wide)
+
+
 class Spread:
     def __init__(self, n_d, n_t, shards, alls, sems):
         self.n_d, self.n_t, self.shards, self.alls = n_d, n_t, shards, alls
@@ -178,13 +189,13 @@
 
     def across(self, a, way, h, step, arriving):
         source = self.chip - way * h
-        q, half = self.rows(a), self.shards[a].shape[1] // 2
         out = []
         for stream, order in enumerate(orders(self.n_d)):
             partner = lax.bitwise_xor(self.d, 1 << order[step])
             for j, m in enumerate(combos(order[:step])):
                 block = lax.bitwise_xor(partner if arriving else self.d, m)
-                ref = self.alls[a].at[2 * source + self.core, span(block, q), pl.ds(stream * half, half)]
+                rows, cols = half(block, stream, self.rows(a), self.shards[a].shape[1])
+                ref = self.alls[a].at[2 * source + self.core, rows, cols]
                 i = stream * (self.n_d - 1) + (1 << step) - 1 + j
                 k = self.slot(way, h)
                 out.append(self.remote(ref, ref, self.ps.at[a, k, i], self.pr.at[a, k, i], (partner, self.t)))
@@ -648,7 +659,7 @@
         units = count * chips
         return (
             [vm((chips,), r, c) for r, c in shapes] * 2
-            + [vm((chips, slots), r // n_d, c // 2) for r, c in shapes]
+            + [vm((chips, slots), *halves(r // n_d, c)) for r, c in shapes]
             + [vm((chips - 1,), r // n_d, c) for r, c in shapes]
             + [dma((units,)), dma((units,)), dma((units,)), dma((units, slots)), dma((units, slots))]
             + [dma((units,)), dma((units,))]
@@ -672,8 +683,8 @@
     def cut(self, u, part, stream):
         n, k = self.units[u]
         _, height, width = self.mine[n].shape
-        height, width = height // self.n_d, width // 2
-        return self.mine[n].at[k, span(part, height), pl.ds(stream * width, width)]
+        rows, cols = half(part, stream, height // self.n_d, width)
+        return self.mine[n].at[k, rows, cols]
 
     def hops(self, u, step):
         n, k = self.units[u]
@@ -1016,10 +1027,10 @@
         name="feed",
     )(att, x, cot, ow, par, up, down)
 def finish_kernel(
-    n_d, n_t, sum_ref, x_ref, hid_ref, par_ref, vec_in, up_tot, down_tot, og_tot, ig_ref,
+    n_d, n_t, bm_ref, w_ref, x_ref, hid_ref, par_ref, vec_in, up_tot, down_tot, og_tot, g_hbm,
     bt_ref, vec_ref, up_out, down_out, og_out, ig_out,
-    mine, landed, far, full_up, full_down, full_og, full_ig,
-    r_side, r_out, r_land, vec_now, vec_got, vec_far,
+    g_ref, mine, landed, far, full_up, full_down, full_og, full_ig,
+    r_give, r_keep, r_side, r_out, r_land, vec_now, vec_got, vec_far,
     s_load, s_hop, r_hop, s_all, r_all, s_own, r_own,
     s_red, r_red, s_redside, r_redside, s_vec, r_vec,
 ):
@@ -1031,7 +1042,6 @@
     chip, core = t // 2, lax.rem(t, 2)
     other = 2 * chip + 1 - core
     line = [lax.rem(chip + k, chips) for k in range(1, chips)]
-    dest = line + [chip]
     peers = [lax.rem(d + k, n_d) for k in range(1, n_d)]
     bits = n_d.bit_length() - 1
     barrier([(d, lax.rem(t + k, n_t)) for k in range(1, n_t)] + [(p, t) for p in peers])
@@ -1039,14 +1049,8 @@
     fulls = [full_up, full_down, full_og, full_ig]
     outs = [up_out, down_out, og_out, ig_out]
 
-    red_pairs = []
-    for k, c in enumerate(dest):
-        theirs = sum_ref.at[span(2 * c + 1 - core, rows), :]
-        red_pairs.append(send(theirs, r_side.at[k], s_redside.at[k], r_redside.at[k], (d, other)))
-    loads = []
-    for k in range(trees):
-        loads.append(pltpu.make_async_copy(ig_ref.at[k], mine.at[k], s_load.at[k]))
-        loads[k].start()
+    load = pltpu.make_async_copy(g_hbm, g_ref, s_load.at[0])
+    load.start()
     hops, spreads = {}, []
 
     def cut(k, part):
@@ -1091,15 +1095,55 @@
         def _():
             far[here] = cut(k, d)[...]
 
+    spread(0, totals[0])
+    spread(2, totals[2])
+
+    def chip_at(k):
+        return lax.rem(chip + 1 + k, chips)
+
+    def pair(k):
+        return pltpu.make_async_remote_copy(
+            src_ref=r_give.at[k], dst_ref=r_side.at[k], send_sem=s_redside.at[k], recv_sem=r_redside.at[k],
+            device_id=(d, other), device_id_type=MESH,
+        )
+
+    def red(k):
+        return pltpu.make_async_remote_copy(
+            src_ref=r_out.at[k], dst_ref=r_land.at[k], send_sem=s_red.at[k], recv_sem=r_red.at[k],
+            device_id=(d, 2 * chip_at(k) + core), device_id_type=MESH,
+        )
+
+    def rows_of(device):
+        return dot(bm_ref[span(device, rows), :], w_ref[...], NT).astype(bf16)
+
+    def step_rows(k, _):
+        r_give[k] = rows_of(2 * chip_at(k) + 1 - core)
+        r_keep[k] = rows_of(2 * chip_at(k) + core)
+        pair(k).start()
+
+        @pl.when(k > 0)
+        def _():
+            pair(k - 1).wait_recv()
+            r_out[k - 1] = r_keep[k - 1] + r_side[k - 1]
+            red(k - 1).start()
+
+        return 0
+
+    lax.fori_loop(0, chips, step_rows, 0)
+
+    columns, width = bm_ref.shape[1] // 3, mine.shape[2]
+    load.wait()
+
+    def step_weight(i, _):
+        p, c = i // (wide // BLOCK), lax.rem(i, wide // BLOCK)
+        product = dot(g_ref[:, span(c, BLOCK)], bm_ref[:, span(p, columns)], TN).astype(bf16)
+        for j in range(trees):
+            mine[j, span(i, BLOCK), :] = product[:, j * width : (j + 1) * width]
+        return 0
+
+    lax.fori_loop(0, 3 * (wide // BLOCK), step_weight, 0)
     for k in range(trees):
-        loads[k].wait()
         hop(k, 0)
-    spread(0, totals[0])
-    red_copies = []
-    for k, c in enumerate(line):
-        red_pairs[k].wait_recv()
-        r_out[k] = sum_ref[span(2 * c + core, rows), :] + r_side[k]
-        red_copies.append(send(r_out.at[k], r_land.at[k], s_red.at[k], r_red.at[k], (d, 2 * c + core)))
     for n in range(3):
         fulls[n][span(d, fulls[n].shape[0] // n_d), :] = totals[n][...]
     for step in range(bits):
@@ -1107,28 +1151,31 @@
             land(k, step)
         if step == 0:
             spread(1, totals[1])
-            spread(2, totals[2])
 
     def reduced():
-        red_pairs[chips - 1].wait_recv()
-        back = [None] * trees
-        own = sum_ref[span(t, rows), :].astype(f32) + r_side[chips - 1].astype(f32)
+        pair(chips - 1).wait_recv()
+        for k in range(chips - 1):
+            red(k).wait_recv()
         hit = chip // near
-        x = x_ref[...].astype(f32)
-        for k in range(chips - 1):
-            red_copies[k].wait_recv()
+        vec_now[0:6] = vec_in[0:6]
+        vec_now[6:8] = jnp.zeros((2, wide), f32)
+        height = min(64, rows)
         for tree in range(trees):
-            e = jnp.where(hit == tree, own, 0.0)
-            for k in range(chips - 1):
-                source = lax.rem(chip + chips - 1 - k, chips)
-                e = e + jnp.where(source // near == tree, r_land[k].astype(f32), 0.0)
-            norm, r = ln_parts(x[tree])
-            g, b = jnp.sum(e * norm, axis=0, keepdims=True), jnp.sum(e, axis=0, keepdims=True)
-            bt_ref[tree] = (hid_ref[tree] + ln_back(e, norm, r, par_ref[6:7])).astype(bf16)
-            back[tree] = (g, b)
-        vec_now[0:6] = vec_in[0:6]
-        vec_now[6:7] = sum(g for g, _ in back)
-        vec_now[7:8] = sum(b for _, b in back)
+
+            def body(i, _):
+                at = span(i, height)
+                own = r_keep[chips - 1, at, :].astype(f32) + r_side[chips - 1, at, :].astype(f32)
+                e = jnp.where(hit == tree, own, 0.0)
+                for k in range(chips - 1):
+                    source = lax.rem(chip + chips - 1 - k, chips)
+                    e = e + jnp.where(source // near == tree, r_land[k, at, :].astype(f32), 0.0)
+                norm, r = ln_parts(x_ref[tree, at, :].astype(f32))
+                vec_now[6:7] = vec_now[6:7] + jnp.sum(e * norm, axis=0, keepdims=True)
+                vec_now[7:8] = vec_now[7:8] + jnp.sum(e, axis=0, keepdims=True)
+                bt_ref[tree, at, :] = (hid_ref[tree, at, :] + ln_back(e, norm, r, par_ref[6:7])).astype(bf16)
+                return 0
+
+            lax.fori_loop(0, rows // height, body, 0)
 
     vec_partners = [(d, other)] + [(lax.bitwise_xor(d, 1 << b), t) for b in range(bits)]
     vec_copies = []
@@ -1180,7 +1227,7 @@
     at = span(d, full_ig.shape[0] // n_d)
     full_ig[at, :] = total.astype(bf16)
     spread(3, full_ig.at[at, :])
-    spread_of = [spreads[n * (n_d - 1) : (n + 1) * (n_d - 1)] for n in range(4)]
+    spread_of = [spreads[i * (n_d - 1) : (i + 1) * (n_d - 1)] for i in (0, 2, 1, 3)]
 
     reduced()
     for i in range(len(vec_partners) + 1):
@@ -1206,30 +1253,35 @@
                 device_id=(d, owner(k)), device_id_type=MESH,
             ).wait_send()
 
-    for copy in red_pairs + red_copies + list(hops.values()) + spreads:
+    for k in range(chips):
+        pair(k).wait_send()
+    for k in range(chips - 1):
+        red(k).wait_send()
+    for copy in list(hops.values()) + spreads:
         copy.wait_send()
 
 
-def finish(n_d, n_t, partial, x, hidden, par, vec, up_t, down_t, out_t, in_g):
+def finish(n_d, n_t, mixed, w, x, hidden, par, vec, up_t, down_t, out_t, gathered, width):
     trees, rows, wide = x.shape
     chips = n_t // 2
     bits = n_d.bit_length() - 1
     dma = pltpu.SemaphoreType.DMA
     sds = jax.ShapeDtypeStruct
-    shapes = [(a.shape[0] * n_d, a.shape[1]) for a in (up_t, down_t, out_t)] + [in_g.shape[1:]]
+    shapes = [(a.shape[0] * n_d, a.shape[1]) for a in (up_t, down_t, out_t)] + [(3 * wide, width)]
     vm = lambda lead, shape, kind=bf16: pltpu.VMEM(tuple(lead) + tuple(shape), kind)
     part = (shapes[3][0] // n_d, shapes[3][1])
     partners = 1 + bits
     return pl.pallas_call(
         functools.partial(finish_kernel, n_d, n_t),
-        in_specs=[VMEM] * 8 + [HBM],
+        in_specs=[VMEM] * 9 + [HBM],
         out_specs=[VMEM] * 6,
         out_shape=[sds(x.shape, bf16), sds((8, wide), f32)] + [sds(s, f32) for s in shapes],
-        scratch_shapes=[vm((trees,), shapes[3]), vm((trees, n_d - 1), part), vm((trees,), part)]
+        scratch_shapes=[vm((), gathered.shape), vm((trees,), shapes[3]), vm((trees, n_d - 1), part), vm((trees,), part)]
         + [vm((), s) for s in shapes] + [
-            vm((chips, rows), (wide,)), vm((chips - 1, rows), (wide,)), vm((chips - 1, rows), (wide,)),
+            vm((chips, rows), (wide,)), vm((chips, rows), (wide,)), vm((chips, rows), (wide,)),
+            vm((chips - 1, rows), (wide,)), vm((chips - 1, rows), (wide,)),
             vm((8,), (wide,), f32), vm((2 * partners, 8), (wide,), f32), vm((chips, 8), (wide,), f32),
-            dma((trees,)), dma((trees, n_d - 1)), dma((trees, n_d - 1)),
+            dma((1,)), dma((trees, n_d - 1)), dma((trees, n_d - 1)),
             dma((4, n_d - 1)), dma((4, n_d - 1)),
             dma((trees,)), dma((trees,)),
             dma((chips - 1,)), dma((chips - 1,)), dma((chips,)), dma((chips,)),
@@ -1239,7 +1291,7 @@
             collective_id=3, has_side_effects=True, vmem_limit_bytes=67043328
         ),
         name="finish",
-    )(partial, x, hidden, par, vec, up_t, down_t, out_t, in_g)
+    )(mixed, w, x, hidden, par, vec, up_t, down_t, out_t, gathered)
 
 
 def shards(
@@ -1276,12 +1328,9 @@
         up_g, down_g, out_g.reshape(n_t, width, wide),
     )
     w_flat = w.transpose(1, 0, 2).reshape(wide, -1)
-    partial = lax.dot_general(back_mixed, w_flat, NT, preferred_element_type=f32).astype(bf16)
-    in_part = lax.dot_general(gathered, back_mixed, TN, preferred_element_type=f32)
-    in_part = in_part.astype(bf16).reshape(wide, 3, trees, width).transpose(2, 1, 0, 3)
     back_tokens, vec, up_sum, down_sum, out_sum, in_sum = finish(
-        n_d, n_t, partial, tokens, back_hidden.reshape(x.shape), par, vec,
-        up_t, down_t, out_t, in_part.reshape(trees, 3 * wide, width),
+        n_d, n_t, back_mixed, w_flat, tokens, back_hidden.reshape(x.shape), par, vec,
+        up_t, down_t, out_t, gathered, width,
     )
     return (
         output.reshape(tokens.shape),

time: 484 us -> 463 us (0.957); the launches traced: 477 us -> 463 us
  matrix products: 13.8 us -> 0 us
    dot_general x2 -> x0, matrix products: 13.8 us -> none  [the longest x1 7.19 us: shards(): lax.dot_general(back_mixed, w_flat, NT, preferred_element_type=f32)]
where the time goes in v6:
time: 463 us
  Pallas kernels  431 us (93%)
  local copies, waits for them, and re-layouts  17.6 us (4%)
  other arithmetic  13.5 us (3%)
    pallas_call x1, Pallas kernels, attend_back(): pl.pallas_call(functools.partial(bwd_kernel, n_d, n_t), grid=(rows // BLO...  111 us
    pallas_call x1, Pallas kernels, finish(): pl.pallas_call(functools.partial(finish_kernel, n_d, n_t), in_specs=[VMEM...  95.1 us
    pallas_call x1, Pallas kernels, gather_tree(): pl.pallas_call(functools.partial(gather_kernel, n_d, n_t), in_specs=[VMEM...  84.6 us
    pallas_call x1, Pallas kernels, attend(): pl.pallas_call(functools.partial(fwd_kernel, n_d, n_t, trees), grid=(rows...  74.9 us
    pallas_call x1, Pallas kernels, feed(): pl.pallas_call(feed_kernel, grid=(2, n_t), in_specs=[one(a) for a in (att...  52.2 us
    pallas_call x1, Pallas kernels, project(): pl.pallas_call(qkv_kernel, grid=(rows // BLOCK,), in_specs=[pl.BlockSpec(...  12.7 us

profile of v6, /device:TPU:0, one launch (start us, length us, event | category | flops | bytes accessed | tf_op | source)
XLA Modules:
  0.0 462.9 jit_solution(11666519547212867060)
XLA Ops:
  0.8 0.8 dynamic-slice_bitcast_fusion.1
  1.5 0.7 dynamic-slice_bitcast_fusion
  2.2 0.1 pad_add_fusion
  2.3 0.2 reduce-window.7
  2.5 0.1 bitcast_subtract_fusion
  2.6 1.4 convert_reduce_fusion
  4.0 1.6 fusion.2
  5.7 0.1 convert_reduce_fusion.1
  5.8 0.1 select_reduce_fusion.3
  5.9 0.1 select_reduce_fusion
  6.1 0.7 stack.35.par_ref
  6.8 1.4 fusion.5.x_ref
  8.2 2.7 fusion.11
  10.9 5.6 %fusion.6 = (f32[2048,128]{1,0:T(8,128)}, f32[2048,128]{1,0:T(8,128)}) fusion(f32[128]{0:T(128)S(1)} %get-tuple-element.94, f32[128]{0:T(128)S(1)} %get-tuple-element.95, f32[2048]{0:T(1024)S(1)} %add_convert_fusion), kind=kLoop, calls=%fused_computation.13 | loop fusion | flops 524288 | bytes 2106368 | tf_op jit(solution)/shard_map/mul | solution.py:83
  16.5 84.6 %gather_tree.1 = (bf16[2048,1024]{1,0:T(8,128)(2,1)}, bf16[2,3,1024,128]{3,2,1,0:T(8,128)(2,1)}, bf16[8,512,1024]{2,1,0:T(8,128)(2,1)}) custom-call(bf16[2,256,1024]{2,1,0:T(8,128)(2,1)} %fusion.5.x_ref, bf16[3,1024,128]{2,1,0:T(8,128)(2,1)} %bitcast.56, bf16[512,1024]{1,0:T(8,128)(2,1)} %f_ref.1), custom_call_target="tpu_custom_call" | custom-call | tf_op jit(solution)/shard_map/gather_tree/pallas_call | solution.py:429
  101.1 2.8 fusion.17
  103.9 0.9 copy.36
  104.7 1.6 copy.37.w_ref
  106.4 12.7 %project.1 = (bf16[4,2048,128]{2,1,0:T(8,128)(2,1)}, bf16[4,2048,128]{2,1,0:T(8,128)(2,1)}, bf16[4,2048,128]{2,1,0:T(8,128)(2,1)}, bf16[4,64,2048]{2,1,0:T(8,128)(2,1)}, bf16[4,80,2048]{2,1,0:T(8,128)(2,1)}) custom-call(bf16[2048,1024]{1,0:T(8,128)(2,1)} %get-tuple-element.44.x_ref.g_hbm, bf16[3,1024,256]{2,1,0:T(8,128)(2,1)} %get-tuple-element.79.w_ref, ...), custom_call_target="tpu_custom_call" | custom-call | tf_op jit(solution)/shard_map/project/pallas_call | solution.py:493
  119.0 74.9 %attend.1 = (bf16[2048,256]{1,0:T(8,128)(2,1)}, bf16[4,2048,128]{2,1,0:T(8,128)(2,1)}, bf16[2,256,1024]{2,1,0:T(8,128)(2,1)}, bf16[8,128,1024]{2,1,0:T(8,128)(2,1)}, bf16[8,1024,512]{2,1,0:T(8,128)(2,1)}) custom-call(bf16[4,2048,128]{2,1,0:T(8,128)(2,1)} %get-tuple-element.46.q_ref, bf16[4,2048,128]{2,1,0:T(8,128)(2,1)} %get-tuple-element.47.k_ref, ...), custom_call_target="tpu_custom_call" | custom-call | tf_op jit(solution)/shard_map/attend/pallas_call | solution.py:618
  193.9 52.2 %feed.1 = (bf16[512,1024]{1,0:T(8,128)(2,1)}, f32[512,1024]{1,0:T(8,128)}, bf16[512,1024]{1,0:T(8,128)(2,1)}, bf16[8,1024,512]{2,1,0:T(8,128)(2,1)}, bf16[8,512,...) custom-call(bf16[512,1024]{1,0:T(8,128)(2,1)} %bitcast.54, bf16[512,1024]{1,0:T(8,128)(2,1)} %bitcast.47, ...), custom_call_target="tpu_custom_call" | custom-call | tf_op jit(solution)/shard_map/feed/pallas_call | solution.py:1015
  246.2 111.5 %attend_back.1 = (bf16[2048,768]{1,0:T(8,128)(2,1)}, bf16[256,512]{1,0:T(8,128)(2,1)}, bf16[128,1024]{1,0:T(8,128)(2,1)}, bf16[32,1024]{1,0:T(8,128)(2,1)}) custom-call(bf16[4,2048,128]{2,1,0:T(8,128)(2,1)} %get-tuple-element.54.q_ref, bf16[4,2048,128]{2,1,0:T(8,128)(2,1)} %get-tuple-element.47.k_ref, bf16[4,2048,128]{2,1,0:T(8,128)(2,1)} %get-tuple-element.55.v_ref, ...), custom_call_target="tpu_custom_call" | custom-call | tf_op jit(solution)/shard_map/attend_back/pallas_call | solution.py:902
  357.6 95.1 %finish.1 = (bf16[2,256,1024]{2,1,0:T(8,128)(2,1)}, f32[8,1024]{1,0:T(8,128)}, f32[1024,512]{1,0:T(8,128)}, f32[512,1024]{1,0:T(8,128)}, f32[128,1024]{1,0:T(8,128)}, /*index=5*/f32[3072,128]{1,0:T(8,128)}) custom-call(bf16[2048,768]{1,0:T(8,128)(2,1)} %get-tuple-element.62.bm_ref, bf16[1024,768]{1,0:T(8,128)(2,1)} %copy.37.w_ref, ...), custom_call_target="tpu_custom_call" | custom-call | tf_op jit(solution)/shard_map/finish/pallas_call | solution.py:1274
  452.7 1.9 fusion.18
  454.6 2.3 copy.47
  456.9 1.1 copy.48
  458.0 0.2 copy-done.4
  458.2 0.8 copy.49
  459.0 0.2 copy-done.2
  459.2 1.3 copy.50
  460.5 1.0 copy-done.1
  461.5 1.3 copy.51
  (29 shorter events, 0.1 us)
Async XLA Ops:
  0.7 6.2 %copy-start = (bf16[2,256,1024]{2,1,0:T(8,128)(2,1)S(1)}, bf16[2,256,1024]{2,1,0:T(8,128)(2,1)}, u32[]{:S(2)}) copy-start(bf16[2,256,1024]{2,1,0:T(8,128)(2,1)} %x_ref.1) | copy-start | bytes 3145732
  0.7 5.4 %copy-start.5 = (f32[1024]{0:T(1024)S(1)}, f32[1024]{0:T(1024)}, u32[]{:S(2)}) copy-start(f32[1024]{0:T(1024)} %param.21) | copy-start | bytes 12292
  0.7 5.4 %copy-start.6 = (f32[1024]{0:T(1024)S(1)}, f32[1024]{0:T(1024)}, u32[]{:S(2)}) copy-start(f32[1024]{0:T(1024)} %param.20) | copy-start | bytes 12292
  0.7 5.4 %copy-start.12 = (f32[1024]{0:T(1024)S(1)}, f32[1024]{0:T(1024)}, u32[]{:S(2)}) copy-start(f32[1024]{0:T(1024)} %param.31) | copy-start | bytes 12292
  0.7 5.4 %copy-start.11 = (f32[1024]{0:T(1024)S(1)}, f32[1024]{0:T(1024)}, u32[]{:S(2)}) copy-start(f32[1024]{0:T(1024)} %param.30) | copy-start | bytes 12292
  0.7 5.4 %copy-start.10 = (f32[1024]{0:T(1024)S(1)}, f32[1024]{0:T(1024)}, u32[]{:S(2)}) copy-start(f32[1024]{0:T(1024)} %param.27) | copy-start | bytes 12292
  0.7 5.4 %copy-start.9 = (f32[1024]{0:T(1024)S(1)}, f32[1024]{0:T(1024)}, u32[]{:S(2)}) copy-start(f32[1024]{0:T(1024)} %param.26) | copy-start | bytes 12292
  0.7 5.4 %copy-start.8 = (f32[1024]{0:T(1024)S(1)}, f32[1024]{0:T(1024)}, u32[]{:S(2)}) copy-start(f32[1024]{0:T(1024)} %param.25) | copy-start | bytes 12292
  0.7 5.4 %copy-start.7 = (f32[1024]{0:T(1024)S(1)}, f32[1024]{0:T(1024)}, u32[]{:S(2)}) copy-start(f32[1024]{0:T(1024)} %param.24) | copy-start | bytes 12292
  452.7 4.1 copy-start.3
  456.8 1.4 copy-start.4
  456.9 2.3 copy-start.2
  459.2 2.3 copy-start.1

commit v7 on v6

--- a/solution.py
+++ b/solution.py
@@ -282,8 +282,8 @@
 
 
 def gather_kernel(
-    n_d, n_t, x_ref, w_ref, f_ref, o_ref, u_ref, all_ref,
-    passing, rs, ss, rb, sb, rw, sw, rp, sp, *sems,
+    n_d, n_t, v_ref, gain_ref, w_ref, f_ref, o_ref, u_ref, all_ref,
+    x_ref, passing, rs, ss, rb, sb, rw, sw, rp, sp, *sems,
 ):
     d, t = lax.axis_index("dp"), lax.axis_index("tensor")
     trees, rows, _ = x_ref.shape
@@ -370,9 +370,19 @@
         def _():
             share(way, h).start()
 
+    height = min(64, rows)
+
+    def norm_rows(i, _):
+        at = span(i, height)
+        for j in range(trees):
+            v = v_ref[j, at, :].astype(f32)
+            x_ref[j, at, :] = layer_norm(v, gain_ref[6:7], gain_ref[7:8]).astype(bf16)
+        return 0
+
+    lax.fori_loop(0, rows // height, norm_rows, 0)
+    o_ref[span(t, rows), :] = x_ref[tree]
     for way in (1, -1):
         pass_on(way, 1)
-    o_ref[span(t, rows), :] = x_ref[tree]
     last = 2 * (chips - 1)
     copies.append(send(x_ref.at[tree], block(chip), sb.at[last], rb.at[last], (d, other)))
     weights.group(0)
@@ -421,14 +431,14 @@
         copy.wait()
 
 
-def gather_tree(n_d, n_t, normed, weight, down):
-    trees, rows, wide = normed.shape
+def gather_tree(n_d, n_t, tokens, par, weight, down):
+    trees, rows, wide = tokens.shape
     chips = n_t // 2
     hops = 2 * (chips - 1)
     dma = pltpu.SemaphoreType.DMA
     return pl.pallas_call(
         functools.partial(gather_kernel, n_d, n_t),
-        in_specs=[VMEM] * 3,
+        in_specs=[VMEM] * 4,
         out_specs=[VMEM] * 2 + [HBM],
         out_shape=[
             jax.ShapeDtypeStruct((n_t * rows, wide), bf16),
@@ -436,13 +446,13 @@
             jax.ShapeDtypeStruct((n_t,) + down.shape, bf16),
         ],
         scratch_shapes=[
-            pltpu.VMEM((trees, chips, rows, wide), bf16),
+            pltpu.VMEM((trees, rows, wide), bf16), pltpu.VMEM((trees, chips, rows, wide), bf16),
             dma((trees, hops)), dma((trees, hops)), dma((hops + 1,)), dma((hops + 1,)),
             dma((trees,)), dma((trees,)), dma((n_d - 1,)), dma((n_d - 1,)),
         ] + Spread.sems(1, n_d, n_t),
         compiler_params=pltpu.CompilerParams(collective_id=0, has_side_effects=True),
         name="gather_tree",
-    )(normed, weight, down)
+    )(tokens, par, weight, down)
 
 
 def qkv_kernel(x_ref, w_ref, cos_ref, sin_ref, mq_ref, mk_ref, q_ref, k_ref, v_ref, kt_ref, vt_ref):
@@ -1098,38 +1108,87 @@
     spread(0, totals[0])
     spread(2, totals[2])
 
-    def chip_at(k):
-        return lax.rem(chip + 1 + k, chips)
-
-    def pair(k):
+    tree = chip // near
+
+    def exists(c):
+        return (c >= 0) & (c < chips)
+
+    def at_step(i):
+        return jnp.where(chip < chips // 2, chips - 1 - i, i)
+
+    def past(way, x):
+        return (x > chip) if way > 0 else (x < chip)
+
+    def comes(way, j):
+        return (j * near <= chip - 1) if way > 0 else (j * near + near - 1 >= chip + 1)
+
+    def pair(x):
         return pltpu.make_async_remote_copy(
-            src_ref=r_give.at[k], dst_ref=r_side.at[k], send_sem=s_redside.at[k], recv_sem=r_redside.at[k],
+            src_ref=r_give.at[x], dst_ref=r_side.at[x], send_sem=s_redside.at[x], recv_sem=r_redside.at[x],
             device_id=(d, other), device_id_type=MESH,
         )
 
-    def red(k):
+    def red(way, x, j, source, arriving=False):
+        w = 0 if way > 0 else 1
+        to = chip - way if arriving else chip + way
         return pltpu.make_async_remote_copy(
-            src_ref=r_out.at[k], dst_ref=r_land.at[k], send_sem=s_red.at[k], recv_sem=r_red.at[k],
-            device_id=(d, 2 * chip_at(k) + core), device_id_type=MESH,
+            src_ref=source, dst_ref=r_land.at[w, x, j], send_sem=s_red.at[w, x, j], recv_sem=r_red.at[w, x, j],
+            device_id=(d, 2 * to + core), device_id_type=MESH,
         )
+
+    def arrived(way, x, j):
+        w = 0 if way > 0 else 1
+        red(way, x, j, r_land.at[w, x, j], True).wait_recv()
 
     def rows_of(device):
         return dot(bm_ref[span(device, rows), :], w_ref[...], NT).astype(bf16)
 
-    def step_rows(k, _):
-        r_give[k] = rows_of(2 * chip_at(k) + 1 - core)
-        r_keep[k] = rows_of(2 * chip_at(k) + core)
-        pair(k).start()
-
-        @pl.when(k > 0)
+    def first_rows(x):
+        pair(x).wait_recv()
+
+        @pl.when(x != chip)
         def _():
-            pair(k - 1).wait_recv()
-            r_out[k - 1] = r_keep[k - 1] + r_side[k - 1]
-            red(k - 1).start()
+            r_out[x] = r_keep[x] + r_side[x]
+
+        for way in (1, -1):
+
+            @pl.when(past(way, x) & jnp.logical_not(comes(way, tree)))
+            def _():
+                red(way, x, tree, r_out.at[x]).start()
+
+    def step_rows(i, _):
+        x = at_step(i)
+        r_give[x] = rows_of(2 * x + 1 - core)
+        r_keep[x] = rows_of(2 * x + core)
+        pair(x).start()
+
+        @pl.when(i > 0)
+        def _():
+            first_rows(at_step(i - 1))
 
         return 0
 
     lax.fori_loop(0, chips, step_rows, 0)
+    first_rows(at_step(chips - 1))
+
+    def later_rows(i):
+        x = at_step(i)
+        for way in (1, -1):
+            for j in range(trees):
+
+                @pl.when(past(way, x) & comes(way, j))
+                def _():
+                    arrived(way, x, j)
+                    passing = r_land.at[0 if way > 0 else 1, x, j]
+
+                    @pl.when(tree == j)
+                    def _():
+                        add_rows(r_out.at[x], passing)
+                        red(way, x, j, r_out.at[x]).start()
+
+                    @pl.when(tree != j)
+                    def _():
+                        red(way, x, j, passing).start()
 
     columns, width = bm_ref.shape[1] // 3, mine.shape[2]
     load.wait()
@@ -1146,33 +1205,42 @@
         hop(k, 0)
     for n in range(3):
         fulls[n][span(d, fulls[n].shape[0] // n_d), :] = totals[n][...]
-    for step in range(bits):
-        for k in range(trees):
-            land(k, step)
-        if step == 0:
+    for i in range(max(chips, bits)):
+        if i < chips:
+            later_rows(i)
+        if i < bits:
+            for k in range(trees):
+                land(k, i)
+        if i == 0:
             spread(1, totals[1])
 
     def reduced():
-        pair(chips - 1).wait_recv()
-        for k in range(chips - 1):
-            red(k).wait_recv()
-        hit = chip // near
+        for w, way in enumerate((1, -1)):
+            for j in range(trees):
+
+                @pl.when(comes(way, j))
+                def _():
+                    arrived(way, chip, j)
+
+                @pl.when(jnp.logical_not(comes(way, j)))
+                def _():
+                    r_land[w, chip, j] = jnp.zeros((rows, wide), bf16)
+
         vec_now[0:6] = vec_in[0:6]
         vec_now[6:8] = jnp.zeros((2, wide), f32)
         height = min(64, rows)
-        for tree in range(trees):
+        for j in range(trees):
 
             def body(i, _):
                 at = span(i, height)
-                own = r_keep[chips - 1, at, :].astype(f32) + r_side[chips - 1, at, :].astype(f32)
-                e = jnp.where(hit == tree, own, 0.0)
-                for k in range(chips - 1):
-                    source = lax.rem(chip + chips - 1 - k, chips)
-                    e = e + jnp.where(source // near == tree, r_land[k, at, :].astype(f32), 0.0)
-                norm, r = ln_parts(x_ref[tree, at, :].astype(f32))
+                own = r_keep[chip, at, :].astype(f32) + r_side[chip, at, :].astype(f32)
+                e = jnp.where(tree == j, own, 0.0)
+                for w in range(2):
+                    e = e + r_land[w, chip, j, at, :].astype(f32)
+                norm, r = ln_parts(x_ref[j, at, :].astype(f32))
                 vec_now[6:7] = vec_now[6:7] + jnp.sum(e * norm, axis=0, keepdims=True)
                 vec_now[7:8] = vec_now[7:8] + jnp.sum(e, axis=0, keepdims=True)
-                bt_ref[tree, at, :] = (hid_ref[tree, at, :] + ln_back(e, norm, r, par_ref[6:7])).astype(bf16)
+                bt_ref[j, at, :] = (hid_ref[j, at, :] + ln_back(e, norm, r, par_ref[6:7])).astype(bf16)
                 return 0
 
             lax.fori_loop(0, rows // height, body, 0)
@@ -1255,8 +1323,18 @@
 
     for k in range(chips):
         pair(k).wait_send()
-    for k in range(chips - 1):
-        red(k).wait_send()
+    for x in range(chips):
+        for way in (1, -1):
+
+            @pl.when(past(way, x))
+            def _():
+                red(way, x, tree, r_out.at[x]).wait_send()
+                for j in range(trees):
+
+                    @pl.when(comes(way, j) & (tree != j))
+                    def _():
+                        red(way, x, j, r_land.at[0 if way > 0 else 1, x, j]).wait_send()
+
     for copy in list(hops.values()) + spreads:
         copy.wait_send()
 
@@ -1279,12 +1357,12 @@
         scratch_shapes=[vm((), gathered.shape), vm((trees,), shapes[3]), vm((trees, n_d - 1), part), vm((trees,), part)]
         + [vm((), s) for s in shapes] + [
             vm((chips, rows), (wide,)), vm((chips, rows), (wide,)), vm((chips, rows), (wide,)),
-            vm((chips - 1, rows), (wide,)), vm((chips - 1, rows), (wide,)),
+            vm((chips, rows), (wide,)), vm((2, chips, trees, rows), (wide,)),
             vm((8,), (wide,), f32), vm((2 * partners, 8), (wide,), f32), vm((chips, 8), (wide,), f32),
             dma((1,)), dma((trees, n_d - 1)), dma((trees, n_d - 1)),
             dma((4, n_d - 1)), dma((4, n_d - 1)),
             dma((trees,)), dma((trees,)),
-            dma((chips - 1,)), dma((chips - 1,)), dma((chips,)), dma((chips,)),
+            dma((2, chips, trees)), dma((2, chips, trees)), dma((chips,)), dma((chips,)),
             dma((partners + chips - 1,)), dma((partners + chips - 1,)),
         ],
         compiler_params=pltpu.CompilerParams(
@@ -1308,17 +1386,15 @@
     mine = lambda a: lax.dynamic_index_in_dim(a, tree, 0, keepdims=False)
     cosine, sine, mq, mk = tables(mine(lengths), mine(parents), n_t * rows)
 
-    x = tokens.astype(f32)
-    normed = layer_norm(x, first_gain, first_shift)
+    par = jnp.stack(
+        [second_gain, second_shift, third_gain, third_shift, fourth_gain, fourth_shift, first_gain, first_shift]
+    )
     gathered, w, down_all = gather_tree(
-        n_d, n_t, normed.astype(bf16), in_weight.transpose(1, 0, 2), down_weight
+        n_d, n_t, tokens, par, in_weight.transpose(1, 0, 2), down_weight
     )
     w = w.transpose(1, 2, 0, 3).reshape(3, wide, -1)
     q, k, v, kt, vt = project(gathered, w, cosine, sine, mq, mk)
     attended, qb, att, out_all, up_all = attend(n_d, n_t, trees, q, k, vt, out_weight, up_weight)
-    par = jnp.stack(
-        [second_gain, second_shift, third_gain, third_shift, fourth_gain, fourth_shift, first_gain, first_shift]
-    )
     flat = lambda a: a.reshape(trees * rows, a.shape[-1])
     output, back_hidden, back_att, up_g, down_g, out_g, vec = feed(
         flat(att), flat(tokens), flat(cotangent), out_all.reshape(-1, wide), par, up_all, down_all
@@ -1329,7 +1405,7 @@
     )
     w_flat = w.transpose(1, 0, 2).reshape(wide, -1)
     back_tokens, vec, up_sum, down_sum, out_sum, in_sum = finish(
-        n_d, n_t, back_mixed, w_flat, tokens, back_hidden.reshape(x.shape), par, vec,
+        n_d, n_t, back_mixed, w_flat, tokens, back_hidden.reshape(tokens.shape), par, vec,
         up_t, down_t, out_t, gathered, width,
     )
     return (

time: 463 us -> 450 us (0.972)
  Pallas kernels: 431 us -> 422 us
    pallas_call x1, Pallas kernels: 95.1 us -> 85.8 us  [finish(): pl.pallas_call(functools.partial(finish_kernel, n_d, n_t), in_specs=[VMEM...]
where the time goes in v7:
time: 450 us; the launch traced here: 449 us
  Pallas kernels  422 us (94%)
  local copies, waits for them, and re-layouts  18 us (4%)
  other arithmetic  8.91 us (2%)
    pallas_call x1, Pallas kernels, attend_back(): pl.pallas_call(functools.partial(bwd_kernel, n_d, n_t), grid=(rows // BLO...  111 us
    pallas_call x1, Pallas kernels, finish(): pl.pallas_call(functools.partial(finish_kernel, n_d, n_t), in_specs=[VMEM...  85.8 us
    pallas_call x1, Pallas kernels, gather_tree(): pl.pallas_call(functools.partial(gather_kernel, n_d, n_t), in_specs=[VMEM...  84.6 us
    pallas_call x1, Pallas kernels, attend(): pl.pallas_call(functools.partial(fwd_kernel, n_d, n_t, trees), grid=(rows...  74.9 us
    pallas_call x1, Pallas kernels, feed(): pl.pallas_call(feed_kernel, grid=(2, n_t), in_specs=[one(a) for a in (att...  52.2 us
    pallas_call x1, Pallas kernels, project(): pl.pallas_call(qkv_kernel, grid=(rows // BLOCK,), in_specs=[pl.BlockSpec(...  12.6 us

profile of v7, /device:TPU:0, one launch (start us, length us, event | category | flops | bytes accessed | tf_op | source)
XLA Modules:
  0.0 449.3 jit_solution(8887978965129709050)
XLA Ops:
  0.7 0.7 dynamic-slice_bitcast_fusion.1
  1.4 0.7 dynamic-slice_bitcast_fusion
  2.0 0.1 pad_add_fusion
  2.1 0.2 reduce-window.7
  2.3 0.1 bitcast_subtract_fusion
  2.4 0.1 convert_reduce_fusion
  2.5 0.1 select_reduce_fusion.3
  2.6 0.1 select_reduce_fusion
  2.8 1.5 stack.35.gain_ref.par_ref
  4.2 2.7 fusion.5
  6.9 5.5 %fusion = (f32[2048,128]{1,0:T(8,128)}, f32[2048,128]{1,0:T(8,128)}) fusion(f32[128]{0:T(128)S(1)} %get-tuple-element.94, f32[128]{0:T(128)S(1)} %get-tuple-element.95, f32[2048]{0:T(1024)S(1)} %add_convert_fusion), kind=kLoop, calls=%fused_computation.5 | loop fusion | flops 524288 | bytes 2106368 | tf_op jit(solution)/shard_map/mul | solution.py:83
  12.4 84.6 %gather_tree.1 = (bf16[2048,1024]{1,0:T(8,128)(2,1)}, bf16[2,3,1024,128]{3,2,1,0:T(8,128)(2,1)}, bf16[8,512,1024]{2,1,0:T(8,128)(2,1)}) custom-call(bf16[2,256,1024]{2,1,0:T(8,128)(2,1)} %x_ref.1, f32[8,1024]{1,0:T(8,128)} %stack.35.gain_ref.par_ref, bf16[3,1024,128]{2,1,0:T(8,128)(2,1)} %bitcast.56, bf16[512,1024]{1,0:T(8,128)(2,1)} %f_ref.1), custom_call_target="tpu_custom_call" | custom-call | tf_op jit(solution)/shard_map/gather_tree/pallas_call | solution.py:439
  97.0 2.8 fusion.11
  99.8 0.9 copy.36
  100.7 1.6 copy.37.w_ref
  102.3 12.6 %project.1 = (bf16[4,2048,128]{2,1,0:T(8,128)(2,1)}, bf16[4,2048,128]{2,1,0:T(8,128)(2,1)}, bf16[4,2048,128]{2,1,0:T(8,128)(2,1)}, bf16[4,64,2048]{2,1,0:T(8,128)(2,1)}, bf16[4,80,2048]{2,1,0:T(8,128)(2,1)}) custom-call(bf16[2048,1024]{1,0:T(8,128)(2,1)} %get-tuple-element.44.x_ref.g_hbm, bf16[3,1024,256]{2,1,0:T(8,128)(2,1)} %get-tuple-element.79.w_ref, ...), custom_call_target="tpu_custom_call" | custom-call | tf_op jit(solution)/shard_map/project/pallas_call | solution.py:503
  114.9 74.9 %attend.1 = (bf16[2048,256]{1,0:T(8,128)(2,1)}, bf16[4,2048,128]{2,1,0:T(8,128)(2,1)}, bf16[2,256,1024]{2,1,0:T(8,128)(2,1)}, bf16[8,128,1024]{2,1,0:T(8,128)(2,1)}, bf16[8,1024,512]{2,1,0:T(8,128)(2,1)}) custom-call(bf16[4,2048,128]{2,1,0:T(8,128)(2,1)} %get-tuple-element.46.q_ref, bf16[4,2048,128]{2,1,0:T(8,128)(2,1)} %get-tuple-element.47.k_ref, ...), custom_call_target="tpu_custom_call" | custom-call | tf_op jit(solution)/shard_map/attend/pallas_call | solution.py:628
  189.8 52.2 %feed.1 = (bf16[512,1024]{1,0:T(8,128)(2,1)}, f32[512,1024]{1,0:T(8,128)}, bf16[512,1024]{1,0:T(8,128)(2,1)}, bf16[8,1024,512]{2,1,0:T(8,128)(2,1)}, bf16[8,512,...) custom-call(bf16[512,1024]{1,0:T(8,128)(2,1)} %bitcast.54, bf16[512,1024]{1,0:T(8,128)(2,1)} %bitcast.47, ...), custom_call_target="tpu_custom_call" | custom-call | tf_op jit(solution)/shard_map/feed/pallas_call | solution.py:1025
  242.0 111.5 %attend_back.1 = (bf16[2048,768]{1,0:T(8,128)(2,1)}, bf16[256,512]{1,0:T(8,128)(2,1)}, bf16[128,1024]{1,0:T(8,128)(2,1)}, bf16[32,1024]{1,0:T(8,128)(2,1)}) custom-call(bf16[4,2048,128]{2,1,0:T(8,128)(2,1)} %get-tuple-element.54.q_ref, bf16[4,2048,128]{2,1,0:T(8,128)(2,1)} %get-tuple-element.47.k_ref, bf16[4,2048,128]{2,1,0:T(8,128)(2,1)} %get-tuple-element.55.v_ref, ...), custom_call_target="tpu_custom_call" | custom-call | tf_op jit(solution)/shard_map/attend_back/pallas_call | solution.py:912
  353.5 85.8 %finish.1 = (bf16[2,256,1024]{2,1,0:T(8,128)(2,1)}, f32[8,1024]{1,0:T(8,128)}, f32[1024,512]{1,0:T(8,128)}, f32[512,1024]{1,0:T(8,128)}, f32[128,1024]{1,0:T(8,128)}, /*index=5*/f32[3072,128]{1,0:T(8,128)}) custom-call(bf16[2048,768]{1,0:T(8,128)(2,1)} %get-tuple-element.62.bm_ref, bf16[1024,768]{1,0:T(8,128)(2,1)} %copy.37.w_ref, ...), custom_call_target="tpu_custom_call" | custom-call | tf_op jit(solution)/shard_map/finish/pallas_call | solution.py:1352
  439.3 0.0 copy-start.2
  439.3 1.7 fusion.12
  441.0 2.3 copy.47
  443.2 0.0 copy-done.2
  443.2 0.0 copy-start.3
  443.3 1.1 copy.48
  444.4 0.2 copy-done.3
  444.6 0.8 copy.49
  445.4 0.2 copy-done.1
  445.6 1.3 copy.50
  446.9 1.0 copy-done
  447.9 1.3 copy.51
  (6 shorter events, 0.0 us)
Async XLA Ops:
  439.3 4.0 copy-start.2
  443.2 1.4 copy-start.3
  443.3 2.3 copy-start.1
  445.6 2.3 copy-start

commit v8 on v7

--- a/solution.py
+++ b/solution.py
@@ -783,7 +783,7 @@
     trees, part, _ = x_ref.shape
     group, width = n_t // trees, heads * HEAD_DIM
     gradients = Reduce(n_d, n_t, [up_ref, down_ref, og_ref], [up_tot, down_tot, og_tot], scratch)
-    ahead = 3
+    ahead = 5
     points = 10
 
     def point(p):
@@ -1038,8 +1038,8 @@
     )(att, x, cot, ow, par, up, down)
 def finish_kernel(
     n_d, n_t, bm_ref, w_ref, x_ref, hid_ref, par_ref, vec_in, up_tot, down_tot, og_tot, g_hbm,
-    bt_ref, vec_ref, up_out, down_out, og_out, ig_out,
-    g_ref, mine, landed, far, full_up, full_down, full_og, full_ig,
+    bt_ref, vec_ref, full_up, full_down, full_og, full_ig,
+    g_ref, mine, landed, far,
     r_give, r_keep, r_side, r_out, r_land, vec_now, vec_got, vec_far,
     s_load, s_hop, r_hop, s_all, r_all, s_own, r_own,
     s_red, r_red, s_redside, r_redside, s_vec, r_vec,
@@ -1057,7 +1057,6 @@
     barrier([(d, lax.rem(t + k, n_t)) for k in range(1, n_t)] + [(p, t) for p in peers])
     totals = [up_tot, down_tot, og_tot]
     fulls = [full_up, full_down, full_og, full_ig]
-    outs = [up_out, down_out, og_out, ig_out]
 
     load = pltpu.make_async_copy(g_hbm, g_ref, s_load.at[0])
     load.start()
@@ -1245,40 +1244,6 @@
 
             lax.fori_loop(0, rows // height, body, 0)
 
-    vec_partners = [(d, other)] + [(lax.bitwise_xor(d, 1 << b), t) for b in range(bits)]
-    vec_copies = []
-
-    def vec_step(i):
-        if i > 0:
-            vec_copies[i - 1].wait()
-            vec_now[...] = vec_now[...] + vec_got[i - 1]
-        if i < len(vec_partners):
-            vec_got[len(vec_partners) + i] = vec_now[...]
-            vec_copies.append(
-                send(vec_got.at[len(vec_partners) + i], vec_got.at[i], s_vec.at[i], r_vec.at[i], vec_partners[i])
-            )
-        else:
-            vec_far[chip] = vec_now[...]
-            for k, c in enumerate(line):
-                n = len(vec_partners) + k
-                vec_copies.append(
-                    send(vec_far.at[chip], vec_far.at[chip], s_vec.at[n], r_vec.at[n], (d, 2 * c + core))
-                )
-
-    def widen_all(n):
-        full, out = fulls[n], outs[n]
-        for j in range(n_d - 1):
-            spread_of[n][j].wait_recv()
-        height = 64
-        while full.shape[0] % height:
-            height //= 2
-
-        def widen(i, _):
-            out[span(i, height), :] = full[span(i, height), :].astype(f32)
-            return 0
-
-        lax.fori_loop(0, full.shape[0] // height, widen, 0)
-
     for j in range(trees):
         giver = j * group + t // trees
 
@@ -1295,18 +1260,29 @@
     at = span(d, full_ig.shape[0] // n_d)
     full_ig[at, :] = total.astype(bf16)
     spread(3, full_ig.at[at, :])
-    spread_of = [spreads[i * (n_d - 1) : (i + 1) * (n_d - 1)] for i in (0, 2, 1, 3)]
 
     reduced()
-    for i in range(len(vec_partners) + 1):
-        vec_step(i)
-        if i < 3:
-            widen_all(i)
-    for n in range(len(vec_partners) + 1, 3):
-        widen_all(n)
-    widen_all(3)
-    for k in range(chips - 1):
-        vec_copies[len(vec_partners) + k].wait()
+
+    copy = send(vec_now, vec_got.at[0], s_vec.at[0], r_vec.at[0], (d, other))
+    copy.wait()
+    vec_got[1 + d] = vec_now[...] + vec_got[0]
+    row = vec_got.at[1 + d]
+    vec_copies = [send(row, row, s_vec.at[1 + k], r_vec.at[1 + k], (p, t)) for k, p in enumerate(peers)]
+    for copy in vec_copies:
+        copy.wait()
+    total = vec_got[1]
+    for i in range(1, n_d):
+        total = total + vec_got[1 + i]
+    vec_far[chip] = total
+    vec_copies = []
+    for k in range(1, chips):
+        c = lax.rem(chip + k, chips)
+        n = n_d - 1 + k
+        vec_copies.append(send(vec_far.at[chip], vec_far.at[chip], s_vec.at[n], r_vec.at[n], (d, 2 * c + core)))
+    for copy in spreads:
+        copy.wait_recv()
+    for copy in vec_copies:
+        copy.wait()
     total = vec_far[0]
     for c in range(1, chips):
         total = total + vec_far[c]
@@ -1348,22 +1324,21 @@
     shapes = [(a.shape[0] * n_d, a.shape[1]) for a in (up_t, down_t, out_t)] + [(3 * wide, width)]
     vm = lambda lead, shape, kind=bf16: pltpu.VMEM(tuple(lead) + tuple(shape), kind)
     part = (shapes[3][0] // n_d, shapes[3][1])
-    partners = 1 + bits
     return pl.pallas_call(
         functools.partial(finish_kernel, n_d, n_t),
         in_specs=[VMEM] * 9 + [HBM],
         out_specs=[VMEM] * 6,
-        out_shape=[sds(x.shape, bf16), sds((8, wide), f32)] + [sds(s, f32) for s in shapes],
+        out_shape=[sds(x.shape, bf16), sds((8, wide), f32)] + [sds(s, bf16) for s in shapes],
         scratch_shapes=[vm((), gathered.shape), vm((trees,), shapes[3]), vm((trees, n_d - 1), part), vm((trees,), part)]
-        + [vm((), s) for s in shapes] + [
+        + [
             vm((chips, rows), (wide,)), vm((chips, rows), (wide,)), vm((chips, rows), (wide,)),
             vm((chips, rows), (wide,)), vm((2, chips, trees, rows), (wide,)),
-            vm((8,), (wide,), f32), vm((2 * partners, 8), (wide,), f32), vm((chips, 8), (wide,), f32),
+            vm((8,), (wide,), f32), vm((1 + n_d, 8), (wide,), f32), vm((chips, 8), (wide,), f32),
             dma((1,)), dma((trees, n_d - 1)), dma((trees, n_d - 1)),
             dma((4, n_d - 1)), dma((4, n_d - 1)),
             dma((trees,)), dma((trees,)),
             dma((2, chips, trees)), dma((2, chips, trees)), dma((chips,)), dma((chips,)),
-            dma((partners + chips - 1,)), dma((partners + chips - 1,)),
+            dma((n_d + chips - 1,)), dma((n_d + chips - 1,)),
         ],
         compiler_params=pltpu.CompilerParams(
             collective_id=3, has_side_effects=True, vmem_limit_bytes=67043328
@@ -1412,11 +1387,11 @@
         output.reshape(tokens.shape),
         back_tokens,
         vec[6], vec[7],
-        in_sum.reshape(3, wide, width).transpose(1, 0, 2),
-        out_sum,
+        in_sum.astype(f32).reshape(3, wide, width).transpose(1, 0, 2),
+        out_sum.astype(f32),
         vec[0], vec[1], vec[2], vec[3],
-        up_sum,
-        down_sum,
+        up_sum.astype(f32),
+        down_sum.astype(f32),
         vec[4], vec[5],
     )
 

time: 450 us -> 438 us (0.973)
  Pallas kernels: 422 us -> 410 us
  other arithmetic: 8.91 us -> 16.3 us
  local copies, waits for them, and re-layouts: 18 us -> 10.9 us
    pallas_call x1, Pallas kernels: 85.8 us -> 74.4 us  [finish(): pl.pallas_call(functools.partial(finish_kernel, n_d, n_t), in_specs=[VMEM...]
    unnamed x13 -> x7, local copies, waits for them, and re-layouts: 8.26 us -> 0.98 us
    convert_element_type x0 -> x3, other arithmetic: none -> 4.97 us  [the longest x1 1.79 us: shards(): out_sum.astype(f32)]
where the time goes in v8:
time: 438 us
  Pallas kernels  410 us (94%)
  other arithmetic  16.3 us (4%)
  local copies, waits for them, and re-layouts  10.9 us (2%)
    pallas_call x1, Pallas kernels, attend_back(): pl.pallas_call(functools.partial(bwd_kernel, n_d, n_t), grid=(rows // BLO...  111 us
    pallas_call x1, Pallas kernels, gather_tree(): pl.pallas_call(functools.partial(gather_kernel, n_d, n_t), in_specs=[VMEM...  84.6 us
    pallas_call x1, Pallas kernels, attend(): pl.pallas_call(functools.partial(fwd_kernel, n_d, n_t, trees), grid=(rows...  74.9 us
    pallas_call x1, Pallas kernels, finish(): pl.pallas_call(functools.partial(finish_kernel, n_d, n_t), in_specs=[VMEM...  74.4 us
    pallas_call x1, Pallas kernels, feed(): pl.pallas_call(feed_kernel, grid=(2, n_t), in_specs=[one(a) for a in (att...  52.2 us
    pallas_call x1, Pallas kernels, project(): pl.pallas_call(qkv_kernel, grid=(rows // BLOCK,), in_specs=[pl.BlockSpec(...  12.7 us

profile of v8, /device:TPU:0, one launch (start us, length us, event | category | flops | bytes accessed | tf_op | source)
XLA Modules:
  0.0 437.6 jit_solution(18175181740196157552)
XLA Ops:
  0.7 0.7 dynamic-slice_bitcast_fusion.1
  1.4 0.7 dynamic-slice_bitcast_fusion
  2.0 0.1 pad_add_fusion
  2.1 0.2 reduce-window.7
  2.3 0.1 bitcast_subtract_fusion
  2.4 0.1 convert_reduce_fusion
  2.5 0.1 select_reduce_fusion.3
  2.6 0.1 select_reduce_fusion
  2.8 1.5 stack.35.gain_ref.par_ref
  4.2 2.7 fusion.5
  6.9 5.5 %fusion = (f32[2048,128]{1,0:T(8,128)}, f32[2048,128]{1,0:T(8,128)}) fusion(f32[128]{0:T(128)S(1)} %get-tuple-element.94, f32[128]{0:T(128)S(1)} %get-tuple-element.95, f32[2048]{0:T(1024)S(1)} %add_convert_fusion), kind=kLoop, calls=%fused_computation.6 | loop fusion | flops 524288 | bytes 2106368 | tf_op jit(solution)/shard_map/mul | solution.py:83
  12.4 84.6 %gather_tree.1 = (bf16[2048,1024]{1,0:T(8,128)(2,1)}, bf16[2,3,1024,128]{3,2,1,0:T(8,128)(2,1)}, bf16[8,512,1024]{2,1,0:T(8,128)(2,1)}) custom-call(bf16[2,256,1024]{2,1,0:T(8,128)(2,1)} %x_ref.1, f32[8,1024]{1,0:T(8,128)} %stack.35.gain_ref.par_ref, bf16[3,1024,128]{2,1,0:T(8,128)(2,1)} %bitcast.56, bf16[512,1024]{1,0:T(8,128)(2,1)} %f_ref.1), custom_call_target="tpu_custom_call" | custom-call | tf_op jit(solution)/shard_map/gather_tree/pallas_call | solution.py:439
  97.0 2.8 fusion.11
  99.8 0.9 copy.36
  100.7 1.6 copy.37.w_ref
  102.3 12.7 %project.1 = (bf16[4,2048,128]{2,1,0:T(8,128)(2,1)}, bf16[4,2048,128]{2,1,0:T(8,128)(2,1)}, bf16[4,2048,128]{2,1,0:T(8,128)(2,1)}, bf16[4,64,2048]{2,1,0:T(8,128)(2,1)}, bf16[4,80,2048]{2,1,0:T(8,128)(2,1)}) custom-call(bf16[2048,1024]{1,0:T(8,128)(2,1)} %get-tuple-element.44.x_ref.g_hbm, bf16[3,1024,256]{2,1,0:T(8,128)(2,1)} %get-tuple-element.79.w_ref, ...), custom_call_target="tpu_custom_call" | custom-call | tf_op jit(solution)/shard_map/project/pallas_call | solution.py:503
  115.0 74.9 %attend.1 = (bf16[2048,256]{1,0:T(8,128)(2,1)}, bf16[4,2048,128]{2,1,0:T(8,128)(2,1)}, bf16[2,256,1024]{2,1,0:T(8,128)(2,1)}, bf16[8,128,1024]{2,1,0:T(8,128)(2,1)}, bf16[8,1024,512]{2,1,0:T(8,128)(2,1)}) custom-call(bf16[4,2048,128]{2,1,0:T(8,128)(2,1)} %get-tuple-element.46.q_ref, bf16[4,2048,128]{2,1,0:T(8,128)(2,1)} %get-tuple-element.47.k_ref, ...), custom_call_target="tpu_custom_call" | custom-call | tf_op jit(solution)/shard_map/attend/pallas_call | solution.py:628
  189.9 52.2 %feed.1 = (bf16[512,1024]{1,0:T(8,128)(2,1)}, f32[512,1024]{1,0:T(8,128)}, bf16[512,1024]{1,0:T(8,128)(2,1)}, bf16[8,1024,512]{2,1,0:T(8,128)(2,1)}, bf16[8,512,...) custom-call(bf16[512,1024]{1,0:T(8,128)(2,1)} %bitcast.54, bf16[512,1024]{1,0:T(8,128)(2,1)} %bitcast.48, ...), custom_call_target="tpu_custom_call" | custom-call | tf_op jit(solution)/shard_map/feed/pallas_call | solution.py:1025
  242.1 111.0 %attend_back.1 = (bf16[2048,768]{1,0:T(8,128)(2,1)}, bf16[256,512]{1,0:T(8,128)(2,1)}, bf16[128,1024]{1,0:T(8,128)(2,1)}, bf16[32,1024]{1,0:T(8,128)(2,1)}) custom-call(bf16[4,2048,128]{2,1,0:T(8,128)(2,1)} %get-tuple-element.54.q_ref, bf16[4,2048,128]{2,1,0:T(8,128)(2,1)} %get-tuple-element.47.k_ref, bf16[4,2048,128]{2,1,0:T(8,128)(2,1)} %get-tuple-element.55.v_ref, ...), custom_call_target="tpu_custom_call" | custom-call | tf_op jit(solution)/shard_map/attend_back/pallas_call | solution.py:912
  353.1 74.4 %finish.1 = (bf16[2,256,1024]{2,1,0:T(8,128)(2,1)}, f32[8,1024]{1,0:T(8,128)}, bf16[1024,512]{1,0:T(8,128)(2,1)}, bf16[512,1024]{1,0:T(8,128)(2,1)}, bf16[128,10...) custom-call(bf16[2048,768]{1,0:T(8,128)(2,1)} %get-tuple-element.62.bm_ref, bf16[1024,768]{1,0:T(8,128)(2,1)} %copy.37.w_ref, ...), custom_call_target="tpu_custom_call" | custom-call | tf_op jit(solution)/shard_map/finish/pallas_call | solution.py:1327
  427.4 0.0 copy-start.1
  427.4 1.9 fusion.12
  429.3 1.8 convert_element_type.32
  431.1 2.4 convert_bitcast_fusion
  433.5 0.0 copy-done.1
  433.5 0.0 copy-start
  433.5 1.6 convert_element_type.33
  435.1 0.0 copy-done
  435.1 0.0 copy-start.2
  435.1 1.6 convert_element_type.34
  436.7 0.0 copy-done.2
  436.7 1.0 copy.43
  (4 shorter events, 0.0 us)
Async XLA Ops:
  427.4 6.0 %copy-start.1 = (bf16[1024,512]{1,0:T(8,128)(2,1)S(1)}, bf16[1024,512]{1,0:T(8,128)(2,1)}, u32[]{:S(2)}) copy-start(bf16[1024,512]{1,0:T(8,128)(2,1)} %get-tuple-element.72) | copy-start | bytes 3145732
  433.5 1.6 copy-start
  435.1 1.6 copy-start.2

commit v9 on v8

--- a/solution.py
+++ b/solution.py
@@ -783,7 +783,7 @@
     trees, part, _ = x_ref.shape
     group, width = n_t // trees, heads * HEAD_DIM
     gradients = Reduce(n_d, n_t, [up_ref, down_ref, og_ref], [up_tot, down_tot, og_tot], scratch)
-    ahead = 5
+    ahead = 6
     points = 10
 
     def point(p):

time: 438 us -> 440 us (level)
    pallas_call x1, Pallas kernels: 111 us -> 117 us  [attend_back(): pl.pallas_call(functools.partial(bwd_kernel, n_d, n_t), grid=(rows // BLO...]
    pallas_call x1, Pallas kernels: 74.4 us -> 69.4 us  [finish(): pl.pallas_call(functools.partial(finish_kernel, n_d, n_t), in_specs=[VMEM...]
where the time goes in v9:
time: 440 us; the launch traced here: 439 us
  Pallas kernels  411 us (93%)
  other arithmetic  16.3 us (4%)
  local copies, waits for them, and re-layouts  10.9 us (2%)
    pallas_call x1, Pallas kernels, attend_back(): pl.pallas_call(functools.partial(bwd_kernel, n_d, n_t), grid=(rows // BLO...  117 us
    pallas_call x1, Pallas kernels, gather_tree(): pl.pallas_call(functools.partial(gather_kernel, n_d, n_t), in_specs=[VMEM...  84.6 us
    pallas_call x1, Pallas kernels, attend(): pl.pallas_call(functools.partial(fwd_kernel, n_d, n_t, trees), grid=(rows...  74.9 us
    pallas_call x1, Pallas kernels, finish(): pl.pallas_call(functools.partial(finish_kernel, n_d, n_t), in_specs=[VMEM...  69.4 us
    pallas_call x1, Pallas kernels, feed(): pl.pallas_call(feed_kernel, grid=(2, n_t), in_specs=[one(a) for a in (att...  52.2 us
    pallas_call x1, Pallas kernels, project(): pl.pallas_call(qkv_kernel, grid=(rows // BLOCK,), in_specs=[pl.BlockSpec(...  12.7 us

profile of v9, /device:TPU:0, one launch (start us, length us, event | category | flops | bytes accessed | tf_op | source)
XLA Modules:
  0.0 439.0 jit_solution(14939410137007415229)
XLA Ops:
  0.7 0.7 dynamic-slice_bitcast_fusion.1
  1.4 0.7 dynamic-slice_bitcast_fusion
  2.0 0.1 pad_add_fusion
  2.1 0.2 reduce-window.7
  2.3 0.1 bitcast_subtract_fusion
  2.4 0.1 convert_reduce_fusion
  2.5 0.1 select_reduce_fusion.3
  2.6 0.1 select_reduce_fusion
  2.8 1.5 stack.35.gain_ref.par_ref
  4.2 2.7 fusion.5
  6.9 5.5 %fusion = (f32[2048,128]{1,0:T(8,128)}, f32[2048,128]{1,0:T(8,128)}) fusion(f32[128]{0:T(128)S(1)} %get-tuple-element.94, f32[128]{0:T(128)S(1)} %get-tuple-element.95, f32[2048]{0:T(1024)S(1)} %add_convert_fusion), kind=kLoop, calls=%fused_computation.6 | loop fusion | flops 524288 | bytes 2106368 | tf_op jit(solution)/shard_map/mul | solution.py:83
  12.4 84.6 %gather_tree.1 = (bf16[2048,1024]{1,0:T(8,128)(2,1)}, bf16[2,3,1024,128]{3,2,1,0:T(8,128)(2,1)}, bf16[8,512,1024]{2,1,0:T(8,128)(2,1)}) custom-call(bf16[2,256,1024]{2,1,0:T(8,128)(2,1)} %x_ref.1, f32[8,1024]{1,0:T(8,128)} %stack.35.gain_ref.par_ref, bf16[3,1024,128]{2,1,0:T(8,128)(2,1)} %bitcast.56, bf16[512,1024]{1,0:T(8,128)(2,1)} %f_ref.1), custom_call_target="tpu_custom_call" | custom-call | tf_op jit(solution)/shard_map/gather_tree/pallas_call | solution.py:439
  97.0 2.8 fusion.11
  99.8 0.9 copy.36
  100.7 1.6 copy.37.w_ref
  102.3 12.7 %project.1 = (bf16[4,2048,128]{2,1,0:T(8,128)(2,1)}, bf16[4,2048,128]{2,1,0:T(8,128)(2,1)}, bf16[4,2048,128]{2,1,0:T(8,128)(2,1)}, bf16[4,64,2048]{2,1,0:T(8,128)(2,1)}, bf16[4,80,2048]{2,1,0:T(8,128)(2,1)}) custom-call(bf16[2048,1024]{1,0:T(8,128)(2,1)} %get-tuple-element.44.x_ref.g_hbm, bf16[3,1024,256]{2,1,0:T(8,128)(2,1)} %get-tuple-element.79.w_ref, ...), custom_call_target="tpu_custom_call" | custom-call | tf_op jit(solution)/shard_map/project/pallas_call | solution.py:503
  115.0 74.9 %attend.1 = (bf16[2048,256]{1,0:T(8,128)(2,1)}, bf16[4,2048,128]{2,1,0:T(8,128)(2,1)}, bf16[2,256,1024]{2,1,0:T(8,128)(2,1)}, bf16[8,128,1024]{2,1,0:T(8,128)(2,1)}, bf16[8,1024,512]{2,1,0:T(8,128)(2,1)}) custom-call(bf16[4,2048,128]{2,1,0:T(8,128)(2,1)} %get-tuple-element.46.q_ref, bf16[4,2048,128]{2,1,0:T(8,128)(2,1)} %get-tuple-element.47.k_ref, ...), custom_call_target="tpu_custom_call" | custom-call | tf_op jit(solution)/shard_map/attend/pallas_call | solution.py:628
  189.9 52.2 %feed.1 = (bf16[512,1024]{1,0:T(8,128)(2,1)}, f32[512,1024]{1,0:T(8,128)}, bf16[512,1024]{1,0:T(8,128)(2,1)}, bf16[8,1024,512]{2,1,0:T(8,128)(2,1)}, bf16[8,512,...) custom-call(bf16[512,1024]{1,0:T(8,128)(2,1)} %bitcast.54, bf16[512,1024]{1,0:T(8,128)(2,1)} %bitcast.48, ...), custom_call_target="tpu_custom_call" | custom-call | tf_op jit(solution)/shard_map/feed/pallas_call | solution.py:1025
  242.1 117.3 %attend_back.1 = (bf16[2048,768]{1,0:T(8,128)(2,1)}, bf16[256,512]{1,0:T(8,128)(2,1)}, bf16[128,1024]{1,0:T(8,128)(2,1)}, bf16[32,1024]{1,0:T(8,128)(2,1)}) custom-call(bf16[4,2048,128]{2,1,0:T(8,128)(2,1)} %get-tuple-element.54.q_ref, bf16[4,2048,128]{2,1,0:T(8,128)(2,1)} %get-tuple-element.47.k_ref, bf16[4,2048,128]{2,1,0:T(8,128)(2,1)} %get-tuple-element.55.v_ref, ...), custom_call_target="tpu_custom_call" | custom-call | tf_op jit(solution)/shard_map/attend_back/pallas_call | solution.py:912
  359.4 69.4 %finish.1 = (bf16[2,256,1024]{2,1,0:T(8,128)(2,1)}, f32[8,1024]{1,0:T(8,128)}, bf16[1024,512]{1,0:T(8,128)(2,1)}, bf16[512,1024]{1,0:T(8,128)(2,1)}, bf16[128,10...) custom-call(bf16[2048,768]{1,0:T(8,128)(2,1)} %get-tuple-element.62.bm_ref, bf16[1024,768]{1,0:T(8,128)(2,1)} %copy.37.w_ref, ...), custom_call_target="tpu_custom_call" | custom-call | tf_op jit(solution)/shard_map/finish/pallas_call | solution.py:1327
  428.8 0.0 copy-start.1
  428.8 1.9 fusion.12
  430.7 1.8 convert_element_type.32
  432.5 2.4 convert_bitcast_fusion
  434.8 0.0 copy-done.1
  434.8 0.0 copy-start
  434.8 1.6 convert_element_type.33
  436.5 0.0 copy-done
  436.5 0.0 copy-start.2
  436.5 1.6 convert_element_type.34
  438.0 0.0 copy-done.2
  438.0 1.0 copy.43
  (4 shorter events, 0.0 us)
Async XLA Ops:
  428.8 6.0 %copy-start.1 = (bf16[1024,512]{1,0:T(8,128)(2,1)S(1)}, bf16[1024,512]{1,0:T(8,128)(2,1)}, u32[]{:S(2)}) copy-start(bf16[1024,512]{1,0:T(8,128)(2,1)} %get-tuple-element.72) | copy-start | bytes 3145732
  434.8 1.6 copy-start
  436.5 1.6 copy-start.2
